TPU v7x, 256 devices: a whole 4x4x8 slice. The times are simulated.
256 devices in a mesh: seq: 64 (over z, y, core), head: 4 (over x).
Axes of the slice: x: 4, y: 4, z: 8, core: 2. Of those that a mesh axis runs over, the one named last changes fastest.
Arguments:
- query_vectors: bfloat16 [131072, 1024], P('seq', 'head'), may hold values from -6 to 6
- key_vectors: bfloat16 [131072, 128], P('seq'), may hold values from -6 to 6
- value_vectors: bfloat16 [131072, 128], P('seq'), may hold values from -6 to 6
- output_grad: bfloat16 [131072, 1024], P('seq', 'head'), may hold values from -48 to 48
- random_blocks: int32 [1024, 3], P('seq'), may hold values from 0 to 1023, as said below
- global_blocks: int32 [2], replicated, may hold values from 0 to 1023
Outputs:
- query_grad: bfloat16 [131072, 1024], P('seq', 'head')
- key_grad: bfloat16 [131072, 128], P('seq')
- value_grad: bfloat16 [131072, 128], P('seq')
Inputs may be any that keep to these rules, and one draw needn't show every extreme that they name: `random_blocks`: take the query blocks in aligned runs of 16 and the key blocks in aligned runs of 16: all entries of one run of query blocks that fall into one run of key blocks name the same key block.
All inputs are finite; a program needn't handle non-finite values.
Results may differ from a plain program's by a relative error of at most 0.012.
Values may be sent and summed in bfloat16 or wider, within the bound.
A program may use at most 128 MiB of HBM per device.

v0:
```python
import jax
import jax.numpy as jnp
from jax import lax
from jax.sharding import PartitionSpec as P

DH = 128
BLOCK = 128
R = 3
G = 2


def with_halo(value, sides, width):
    for axis, dim in sides:
        size, length = (lax.axis_size(axis), value.shape[dim])
        up = [(i, (i + 1) % size) for i in range(size - 1)]
        down = [(j, i) for i, j in up]
        last = lax.slice_in_dim(value, length - width, length, axis=dim)
        first = lax.slice_in_dim(value, 0, width, axis=dim)
        before = lax.ppermute(last, axis, up)
        after = lax.ppermute(first, axis, down)
        value = jnp.concatenate([before, value, after], axis=dim)
    return value


def from_root(value, axis, source):
    kept = jnp.where(lax.axis_index(axis) == source, value, 0).astype(value.dtype)
    return lax.psum(kept, axis)


def from_behind(block, axis, distance):
    devices = range(lax.axis_size(axis))
    route = [(i - distance, i) for i in devices if i - distance in devices]
    return lax.ppermute(block, axis, route)


def softmax_rows(scores):
    largest = jnp.max(scores, axis=-1, keepdims=True)
    powers = jnp.exp(scores - largest)
    return powers / jnp.sum(powers, axis=-1, keepdims=True)


def body(query_vectors, key_vectors, value_vectors, output_grad, random_blocks, global_blocks):
    seq_count = lax.axis_size("seq")
    seq_index = lax.axis_index("seq")
    rows_dev = query_vectors.shape[0]
    blocks_dev = rows_dev // BLOCK
    heads_dev = query_vectors.shape[1] // DH
    factor = float(DH) ** (-0.5)
    pair_width = 2 * DH
    listed = 3 + R + G
    group_size = 4
    rounds = blocks_dev // group_size
    key_value = jnp.concatenate([key_vectors, value_vectors], axis=1)
    pair_blocks = key_value.reshape(blocks_dev, BLOCK, pair_width)
    owners = random_blocks // blocks_dev
    within = random_blocks % blocks_dev
    peer_ids = jnp.arange(seq_count, dtype=jnp.int32)
    matched = owners[:, :, None] == peer_ids[None, None, :]
    wanted = jnp.max(jnp.where(matched, within[:, :, None], -1), axis=(0, 1))
    requested = lax.all_to_all(
        wanted.reshape(seq_count, 1), "seq", split_axis=0, concat_axis=0, tiled=True
    )[:, 0]
    served = pair_blocks[jnp.clip(requested, 0, blocks_dev - 1)]
    fetched = lax.all_to_all(served, "seq", split_axis=0, concat_axis=0, tiled=True)
    extended = with_halo(key_value, (("seq", 0),), BLOCK)
    extended = extended.reshape(blocks_dev + 2, BLOCK, pair_width)
    global_list = []
    for global_slot in range(G):
        target = global_blocks[global_slot]
        fragment = lax.dynamic_index_in_dim(pair_blocks, target % blocks_dev, 0, keepdims=False)
        global_list.append(from_root(fragment, "seq", target // blocks_dev))
    global_pairs = jnp.stack(global_list)
    first_block = seq_index * blocks_dev
    total_blocks = seq_count * blocks_dev
    query_blocks = query_vectors.reshape(blocks_dev, BLOCK, heads_dev, DH)
    grad_blocks = output_grad.reshape(blocks_dev, BLOCK, heads_dev, DH)

    def advance(totals, position):
        window_acc, random_acc, global_acc = totals
        offset = position * group_size
        beside_all = lax.dynamic_slice_in_dim(extended, offset, group_size + 2, 0)
        window_panels = jnp.stack(
            [
                beside_all[0:group_size],
                beside_all[1 : group_size + 1],
                beside_all[2 : group_size + 2],
            ],
            axis=1,
        )
        owner_rows = lax.dynamic_slice_in_dim(owners, offset, group_size, 0)
        remote_panels = fetched[owner_rows]
        global_part = jnp.broadcast_to(global_pairs[None], (group_size, G, BLOCK, pair_width))
        panels = jnp.concatenate([window_panels, remote_panels, global_part], axis=1)
        panels = panels.reshape(group_size, listed * BLOCK, pair_width)
        key_row_matrix = panels[:, :, :DH]
        value_row_matrix = panels[:, :, DH:]
        query_row_matrix = lax.dynamic_slice_in_dim(query_blocks, offset, group_size, 0)
        gradient_rows = lax.dynamic_slice_in_dim(grad_blocks, offset, group_size, 0)
        block_ids = first_block + offset + jnp.arange(group_size, dtype=jnp.int32)
        allowed = jnp.concatenate(
            [
                (block_ids > 0)[:, None],
                jnp.ones((group_size, 1), dtype=jnp.bool_),
                (block_ids < total_blocks - 1)[:, None],
                jnp.ones((group_size, R + G), dtype=jnp.bool_),
            ],
            axis=1,
        )
        visible = jnp.repeat(allowed, BLOCK, axis=1)
        scores = (
            jnp.einsum(
                "awst,axt->aswx",
                query_row_matrix,
                key_row_matrix,
                preferred_element_type=jnp.float32,
            )
            * factor
        )
        scores = jnp.where(visible[:, None, None, :], scores, -jnp.inf)
        attention = softmax_rows(scores)
        attention_reduced = attention.astype(jnp.bfloat16)
        outputs = jnp.einsum(
            "uwsn,unj->uswj",
            attention_reduced,
            value_row_matrix,
            preferred_element_type=jnp.float32,
        )
        row_delta = jnp.sum(gradient_rows.astype(jnp.float32) * outputs, axis=-1)
        prob_grad = jnp.einsum(
            "awst,axt->aswx", gradient_rows, value_row_matrix, preferred_element_type=jnp.float32
        )
        score_gradient = (
            attention * (prob_grad - jnp.transpose(row_delta, (0, 2, 1))[..., None])
        ).astype(jnp.bfloat16)
        query_part = (
            jnp.einsum(
                "uwsn,unj->uswj", score_gradient, key_row_matrix, preferred_element_type=jnp.float32
            )
            * factor
        ).astype(jnp.bfloat16)
        key_part = (
            jnp.einsum(
                "uwva,uvwp->uap",
                score_gradient,
                query_row_matrix,
                preferred_element_type=jnp.float32,
            )
            * factor
        )
        value_part = jnp.einsum(
            "uwva,uvwp->uap", attention_reduced, gradient_rows, preferred_element_type=jnp.float32
        )
        gradients = jnp.concatenate([key_part, value_part], axis=-1).reshape(
            group_size, listed, BLOCK, pair_width
        )
        spread = jnp.zeros((group_size + 2, BLOCK, pair_width), dtype=jnp.float32)
        spread = spread.at[0:group_size].add(gradients[:, 0])
        spread = spread.at[1 : group_size + 1].add(gradients[:, 1])
        spread = spread.at[2 : group_size + 2].add(gradients[:, 2])
        updated = lax.dynamic_slice_in_dim(window_acc, offset, group_size + 2, 0) + spread
        window_acc = lax.dynamic_update_slice_in_dim(window_acc, updated, offset, 0)
        onehot = (owner_rows[:, :, None] == peer_ids[None, None, :]).astype(jnp.float32)
        random_acc = random_acc + jnp.einsum(
            "brn,brxc->nxc", onehot, gradients[:, 3 : 3 + R], precision=lax.Precision.HIGHEST
        )
        global_acc = global_acc + jnp.sum(gradients[:, 3 + R :], axis=0)
        return (
            (window_acc, random_acc, global_acc),
            query_part.reshape(group_size, BLOCK, heads_dev * DH),
        )

    start_totals = (
        jnp.zeros((blocks_dev + 2, BLOCK, pair_width), dtype=jnp.float32),
        jnp.zeros((seq_count, BLOCK, pair_width), dtype=jnp.float32),
        jnp.zeros((G, BLOCK, pair_width), dtype=jnp.float32),
    )
    (window_acc, random_acc, global_acc), query_parts = lax.scan(
        advance, start_totals, jnp.arange(rounds, dtype=jnp.int32)
    )
    query_grad = query_parts.reshape(rows_dev, heads_dev * DH)
    into_last = from_behind(window_acc[0].astype(jnp.bfloat16), "seq", -1).astype(jnp.float32)
    into_first = from_behind(window_acc[blocks_dev + 1].astype(jnp.bfloat16), "seq", 1).astype(
        jnp.float32
    )
    local_sum = window_acc[1 : blocks_dev + 1]
    local_sum = local_sum.at[blocks_dev - 1].add(into_last)
    local_sum = local_sum.at[0].add(into_first)
    global_total_sum = lax.psum(global_acc, "seq")
    block_range = jnp.arange(blocks_dev, dtype=jnp.int32)
    owned_indicator = (
        (global_blocks[None, :] // blocks_dev == seq_index)
        & (global_blocks[None, :] % blocks_dev == block_range[:, None])
    ).astype(jnp.float32)
    local_sum = local_sum + jnp.einsum(
        "ar,rdi->adi", owned_indicator, global_total_sum, precision=lax.Precision.HIGHEST
    )
    served_hot = (requested[None, :] == block_range[:, None]).astype(jnp.float32)
    returned = lax.all_to_all(
        random_acc.astype(jnp.bfloat16), "seq", split_axis=0, concat_axis=0, tiled=True
    ).astype(random_acc.dtype)
    local_sum = local_sum + jnp.einsum(
        "je,exc->jxc", served_hot, returned, precision=lax.Precision.HIGHEST
    )
    finished = lax.psum(local_sum.astype(jnp.bfloat16), "head")
    finished = finished.reshape(rows_dev, pair_width)
    return (query_grad, finished[:, :DH], finished[:, DH:])


def solution(mesh):
    return jax.shard_map(
        body,
        mesh=mesh,
        in_specs=(
            P("seq", "head"),
            P("seq", None),
            P("seq", None),
            P("seq", "head"),
            P("seq", None),
            P(),
        ),
        out_specs=(P("seq", "head"), P("seq", None), P("seq", None)),
        check_vma=False,
    )
```

profile of v0, /device:TPU:1, one launch (start us, length us, event | category | flops | bytes accessed | tf_op | source)
XLA Modules:
  0.0 699.7 jit_solution(18152049485967785271)
XLA Ops:
  8.9 13.1 %all-to-all-start = ((s32[64,1,1]{2,1,0:T(1,128)}), s32[64,1,1]{2,1,0:T(1,128)S(1)}, u32[]{:S(2)}, u32[]{:S(2)}) async-start(s32[64,1,1]{2,1,0:T(1,128)} %copy.161), calls=%async_computation | async-start | bytes 65536 | tf_op jit(solution)/shard_map/all_to_all | solution.py:60
  24.4 7.0 %all-to-all-done = s32[64,1,1]{2,1,0:T(1,128)S(1)} async-done(((s32[64,1,1]{2,1,0:T(1,128)}), s32[64,1,1]{2,1,0:T(1,128)S(1)}, u32[]{:S(2)}, u32[]{:S(2)}) %all-to-all-start) | async-done | bytes 288 | tf_op jit(solution)/shard_map/all_to_all | solution.py:60
  36.9 5.8 all-to-all-start.1
  49.4 3.5 collective-permute-start
  57.2 180.1 %all-reduce.10.cloned.1.call-done = (bf16[1,128,256]{2,1,0:T(8,128)(2,1)}, bf16[1,128,256]{2,1,0:T(8,128)(2,1)}) async-done(((bf16[1,128,256]{2,1,0:T(8,128)(2,1)}, bf16[1,128,256]{2,1,0:T(8,128)(2,1)}), (bf16[1,128,256]{2,1,0:T(8,128)(2,1)}, bf16[1,128,256]{2,1,0:T(8,128)(2,1)})) %all-reduce.10.cloned.1.call-update) | async-done | bytes 131088 | tf_op jit(solution)/shard_map/psum | solution.py:27
  241.0 181.6 %while.25 = (s32[]{:T(128)}, f32[18,128,256]{1,2,0:T(8,128)}, f32[64,128,256]{2,0,1:T(8,128)}, f32[2,128,256]{1,0,2:T(2,128)}, bf16[4,4,128,256]{3,2,1,0:T(8,128...) while((s32[]{:T(128)}, f32[18,128,256]{1,2,0:T(8,128)}, ...), condition=%wide.region_8.9_spmd.clone, body=%wide.region_3.8_spmd.clone.sunk | while | flops 1932396416 | bytes 146449488 | solution.py:177
  244.2 2.8 gather_fusion
  257.6 2.9 copy.238
  260.6 2.9 slice_reduce_fusion.2
  265.2 6.8 fusion.100
  277.0 6.3 bitcast_add_fusion.2
  286.5 2.8 gather_fusion
  299.8 2.9 copy.238
  302.9 2.9 slice_reduce_fusion.2
  308.6 6.8 fusion.100
  320.4 9.3 %bitcast_add_fusion.2 = f32[64,128,256]{2,0,1:T(8,128)} fusion(f32[64,128,256]{2,0,1:T(8,128)} %get-tuple-element.561, pred[]{:T(512)S(6)} %compare.58, f32[4,3,128,256]{3,0,1,2:T(4,128)S(1)} %copy-done.1, s32[4,3]{0,1:T(4,128)S(1)} %copy.240), kind=kOutput, calls=%fused_computation.4.clone.1 | convolution fusion | flops 306184960 | bytes 18350128 | tf_op jit(solution)/shard_map/while/body/eval_jaxpr/brn,brxc->nxc/dot_general | solution.py:163
  346.3 2.9 copy.238
  349.4 2.9 slice_reduce_fusion.2
  355.0 6.8 fusion.100
  366.8 9.3 %bitcast_add_fusion.2 = f32[64,128,256]{2,0,1:T(8,128)} fusion(f32[64,128,256]{2,0,1:T(8,128)} %get-tuple-element.561, pred[]{:T(512)S(6)} %compare.58, f32[4,3,128,256]{3,0,1,2:T(4,128)S(1)} %copy-done.1, s32[4,3]{0,1:T(4,128)S(1)} %copy.240), kind=kOutput, calls=%fused_computation.4.clone.1 | convolution fusion | flops 306184960 | bytes 18350128 | tf_op jit(solution)/shard_map/while/body/eval_jaxpr/brn,brxc->nxc/dot_general | solution.py:163
  392.7 2.9 copy.238
  395.8 2.9 slice_reduce_fusion.2
  401.4 6.8 fusion.100
  413.3 9.3 %bitcast_add_fusion.2 = f32[64,128,256]{2,0,1:T(8,128)} fusion(f32[64,128,256]{2,0,1:T(8,128)} %get-tuple-element.561, pred[]{:T(512)S(6)} %compare.58, f32[4,3,128,256]{3,0,1,2:T(4,128)S(1)} %copy-done.1, s32[4,3]{0,1:T(4,128)S(1)} %copy.240), kind=kOutput, calls=%fused_computation.4.clone.1 | convolution fusion | flops 306184960 | bytes 18350128 | tf_op jit(solution)/shard_map/while/body/eval_jaxpr/brn,brxc->nxc/dot_general | solution.py:163
  422.6 9.8 %copy.220 = bf16[64,128,256]{2,1,0:T(8,128)(2,1)} copy(f32[64,128,256]{2,0,1:T(8,128)} %get-tuple-element.285) | data formatting | bytes 12582912 | tf_op jit(solution)/shard_map/while | solution.py:177
  432.4 6.9 all-to-all-start.2
  452.1 3.1 collective-permute-start.3
  460.3 76.1 %all-to-all-done.2 = bf16[64,128,256]{2,1,0:T(8,128)(2,1)} async-done(((bf16[64,128,256]{2,1,0:T(8,128)(2,1)}), bf16[64,128,256]{2,1,0:T(8,128)(2,1)}, u32[]{:S(2)}, u32[]{:S(2)}) %all-to-all-start.2) | async-done | bytes 4194336 | tf_op jit(solution)/shard_map/all_to_all | solution.py:198
  536.4 5.9 fusion.32
  542.3 97.8 %all-reduce.6.cloned.1.call-done = f32[2,128,256]{2,0,1:T(2,128)} async-done(((f32[2,128,256]{2,0,1:T(2,128)}), f32[2,128,256]{2,0,1:T(2,128)}) %all-reduce.6.cloned.1.call-update) | async-done | bytes 262160 | tf_op jit(solution)/shard_map/psum | solution.py:188
  640.1 2.9 add_convert_fusion
  644.4 46.6 %all-reduce.8.cloned.1.call-done = bf16[2048,256]{1,0:T(8,128)(2,1)} async-done(((bf16[2048,256]{1,0:T(8,128)(2,1)}), bf16[2048,256]{1,0:T(8,128)(2,1)}) %all-reduce.8.cloned.1.call-update) | async-done | bytes 1048592 | tf_op jit(solution)/shard_map/psum | solution.py:204
  (243 shorter events, 127.8 us)
Async XLA Ops:
  8.9 22.5 %all-to-all-start = ((s32[64,1,1]{2,1,0:T(1,128)}), s32[64,1,1]{2,1,0:T(1,128)S(1)}, u32[]{:S(2)}, u32[]{:S(2)}) async-start(s32[64,1,1]{2,1,0:T(1,128)} %copy.161), calls=%async_computation | async-start | bytes 65536 | tf_op jit(solution)/shard_map/all_to_all | solution.py:60
  36.9 5.9 copy-start.8
  36.9 17.9 %copy-start.5 = (bf16[2048,256]{1,0:T(8,128)(2,1)S(1)}, bf16[2048,256]{1,0:T(8,128)(2,1)}, u32[]{:S(2)}) copy-start(bf16[2048,256]{1,0:T(8,128)(2,1)} %param.18) | copy-start | bytes 3145732
  36.9 202.4 %all-to-all-start.1 = ((bf16[64,128,256]{2,1,0:T(8,128)(2,1)}), bf16[64,128,256]{2,1,0:T(8,128)(2,1)}, u32[]{:S(2)}, u32[]{:S(2)}) async-start(bf16[64,128,256]{2,1,0:T(8,128)(2,1)} %gather_fusion.1), calls=%async_computation.1 | async-start | bytes 8388608 | tf_op jit(solution)/shard_map/all_to_all | solution.py:64
  42.8 13.2 %copy-start.6 = (bf16[2048,256]{1,0:T(8,128)(2,1)S(1)}, bf16[2048,256]{1,0:T(8,128)(2,1)}, u32[]{:S(2)}) copy-start(bf16[2048,256]{1,0:T(8,128)(2,1)} %param.21) | copy-start | bytes 3145732
  42.8 194.5 %all-reduce.10.cloned.1.call-start = ((), (), s32[]{:S(2)}) async-start(), calls=%async_computation.5 | async-start | bytes 262144 | tf_op jit(solution)/shard_map/psum | solution.py:27
  49.4 188.8 %collective-permute-start = (bf16[128,256]{1,0:T(8,128)(2,1)S(1)}, bf16[128,256]{1,0:T(8,128)(2,1)S(1)}, u32[]{:S(2)}, u32[]{:S(2)}) collective-permute-start(bf16[128,256]{1,0:T(8,128)(2,1)S(1)} %get-tuple-element.429), channel_id=1, source_target_pairs={{0,4},{4,8},{8,12},{12,16},{16,20},{20,24},{24,28},{28,32},{32,36}... | collective-permute-start | bytes 196616 | tf_op jit(solution)/shard_map/ppermute | solution.py:19
  52.9 185.3 %collective-permute-start.1 = (bf16[128,256]{1,0:T(8,128)(2,1)S(1)}, bf16[128,256]{1,0:T(8,128)(2,1)S(1)}, u32[]{:S(2)}, u32[]{:S(2)}) collective-permute-start(bf16[128,256]{1,0:T(8,128)(2,1)S(1)} %get-tuple-element.430), channel_id=1, source_target_pairs={{4,0},{8,4},{12,8},{16,12},{20,16},{24,20},{28,24},{32,28},{36,32}... | collective-permute-start | bytes 196616 | tf_op jit(solution)/shard_map/ppermute | solution.py:20
  263.6 8.4 %copy-start = (f32[128,8,8,128]{3,2,1,0:T(8,128)S(1)}, f32[128,8,8,128]{3,2,1,0:T(8,128)}, u32[]{:S(2)}) copy-start(f32[128,8,8,128]{3,2,1,0:T(8,128)} %copy.238) | copy-start | bytes 12582916 | tf_op jit(solution)/shard_map/while
  274.1 1.8 copy-start.2
  275.5 1.5 copy-start.1
  277.0 6.3 copy-start.3
  305.9 9.5 %copy-start = (f32[128,8,8,128]{3,2,1,0:T(8,128)S(1)}, f32[128,8,8,128]{3,2,1,0:T(8,128)}, u32[]{:S(2)}) copy-start(f32[128,8,8,128]{3,2,1,0:T(8,128)} %copy.238) | copy-start | bytes 12582916 | tf_op jit(solution)/shard_map/while
  317.5 1.8 copy-start.2
  318.9 1.5 copy-start.1
  320.4 9.3 %copy-start.3 = (f32[18,128,256]{1,2,0:T(8,128)}, f32[18,128,256]{1,2,0:T(8,128)S(1)}, u32[]{:S(2)}) copy-start(f32[18,128,256]{1,2,0:T(8,128)S(1)} %add_dynamic-update-slice_fusion.5) | copy-start | bytes 7077892 | tf_op jit(solution)/shard_map/while
  352.3 9.5 %copy-start = (f32[128,8,8,128]{3,2,1,0:T(8,128)S(1)}, f32[128,8,8,128]{3,2,1,0:T(8,128)}, u32[]{:S(2)}) copy-start(f32[128,8,8,128]{3,2,1,0:T(8,128)} %copy.238) | copy-start | bytes 12582916 | tf_op jit(solution)/shard_map/while
  363.9 1.8 copy-start.2
  365.3 1.5 copy-start.1
  366.8 9.3 %copy-start.3 = (f32[18,128,256]{1,2,0:T(8,128)}, f32[18,128,256]{1,2,0:T(8,128)S(1)}, u32[]{:S(2)}) copy-start(f32[18,128,256]{1,2,0:T(8,128)S(1)} %add_dynamic-update-slice_fusion.5) | copy-start | bytes 7077892 | tf_op jit(solution)/shard_map/while
  398.7 9.5 %copy-start = (f32[128,8,8,128]{3,2,1,0:T(8,128)S(1)}, f32[128,8,8,128]{3,2,1,0:T(8,128)}, u32[]{:S(2)}) copy-start(f32[128,8,8,128]{3,2,1,0:T(8,128)} %copy.238) | copy-start | bytes 12582916 | tf_op jit(solution)/shard_map/while
  410.4 1.8 copy-start.2
  411.7 1.5 copy-start.1
  413.3 9.3 %copy-start.3 = (f32[18,128,256]{1,2,0:T(8,128)}, f32[18,128,256]{1,2,0:T(8,128)S(1)}, u32[]{:S(2)}) copy-start(f32[18,128,256]{1,2,0:T(8,128)S(1)} %add_dynamic-update-slice_fusion.5) | copy-start | bytes 7077892 | tf_op jit(solution)/shard_map/while
  432.4 7.0 copy-start.9
  432.4 7.0 %copy-start.4 = (f32[18,128,256]{1,2,0:T(8,128)S(1)}, f32[18,128,256]{1,2,0:T(8,128)}, u32[]{:S(2)}) copy-start(f32[18,128,256]{1,2,0:T(8,128)} %get-tuple-element.283) | copy-start | bytes 7077892
  432.4 104.0 %all-to-all-start.2 = ((bf16[64,128,256]{2,1,0:T(8,128)(2,1)}), bf16[64,128,256]{2,1,0:T(8,128)(2,1)}, u32[]{:S(2)}, u32[]{:S(2)}) async-start(bf16[64,128,256]{2,1,0:T(8,128)(2,1)} %copy.220), calls=%async_computation.2 | async-start | bytes 8388608 | tf_op jit(solution)/shard_map/all_to_all | solution.py:198
  439.3 200.7 %all-reduce.6.cloned.1.call-start = ((), (), s32[]{:S(2)}) async-start(), calls=%async_computation.3 | async-start | bytes 524288 | tf_op jit(solution)/shard_map/psum | solution.py:188
  443.2 12.0 %collective-permute-start.2 = (bf16[128,256]{1,0:T(8,128)(2,1)S(1)}, bf16[128,256]{1,0:T(8,128)(2,1)S(1)}, u32[]{:S(2)}, u32[]{:S(2)}) collective-permute-start(bf16[128,256]{1,0:T(8,128)(2,1)S(1)} %get-tuple-element.424), channel_id=1, source_target_pairs={{4,0},{8,4},{12,8},{16,12},{20,16},{24,20},{28,24},{32,28},{36,32}... | collective-permute-start | bytes 196616 | tf_op jit(solution)/shard_map/ppermute | solution.py:33
  449.8 86.6 %copy-start.7 = (s32[64]{0:T(128)S(1)}, s32[64]{0:T(128)}, u32[]{:S(2)}) copy-start(s32[64]{0:T(128)} %get-tuple-element.382) | copy-start | bytes 772
  449.8 241.2 %all-reduce.8.cloned.1.call-start = ((), (), s32[]{:S(2)}) async-start(), calls=%async_computation.4 | async-start | bytes 2097152 | tf_op jit(solution)/shard_map/psum | solution.py:204
  452.1 6.2 collective-permute-start.3
Sparse Core Ops, SparseCore 0:
  49.5 187.7 all-reduce.9
  449.9 190.1 all-reduce.5
  644.5 46.4 all-reduce.7
where the time goes:
time: 702 us; the launch traced here: 700 us
  waiting for transfers between devices  408 us (58%)
  local copies, waits for them, and re-layouts  131 us (19%)
  matrix products  61.8 us (9%)
  other arithmetic  40.1 us (6%)
  starting transfers between devices  37.1 us (5%)
  between operations  19.3 us (3%)
    psum x1, waiting for transfers between devices, from_root(): return lax.psum(kept, axis)  180 us
    psum x1, waiting for transfers between devices, body(): global_total_sum = lax.psum(global_acc, 'seq')  97.8 us
    all_to_all x1, waiting for transfers between devices, body(): lax.all_to_all(random_acc.astype(jnp.bfloat16), 'seq', split_axis=0, conc...  76.1 us
    psum x1, waiting for transfers between devices, body(): finished = lax.psum(local_sum.astype(jnp.bfloat16), 'head')  46.6 us
    while x64, local copies, waits for them, and re-layouts  35.7 us
    dot_general x4, matrix products, advance(): jnp.einsum('brn,brxc->nxc', onehot, gradients[:, 3:3 + R], precision=lax....  34.2 us
    slice x4, local copies, waits for them, and re-layouts, advance(): spread = spread.at[2:group_size + 2].add(gradients[:, 2])  27.3 us
    while x4, local copies, waits for them, and re-layouts, body(): lax.scan(advance, start_totals, jnp.arange(rounds, dtype=jnp.int32))  15.9 us
  transfers between devices with their start and end apart: 10, of which 5 were waited for; matrix products, arithmetic and copies ran while one was open for 4% of the time, Pallas kernels for 0%

commit v1 on v0

v1 whole, which is shorter than its diff:
```python
import functools

import jax
import jax.numpy as jnp
from jax import lax
from jax.experimental import pallas as pl
from jax.experimental.pallas import tpu as pltpu
from jax.sharding import PartitionSpec as P

DH = 128
BLOCK = 128
R = 3
G = 2
PAIR = 2 * DH
LISTED = 3 + R + G
FACTOR = float(DH) ** -0.5
LOG2E = 1.4426950408889634
NEG = -1e30
NT = (((1,), (1,)), ((), ()))
F32 = jnp.float32
BF16 = jnp.bfloat16


def dot(a, b, dims=(((1,), (0,)), ((), ()))):
    return lax.dot_general(a, b, dims, preferred_element_type=F32)


def compute_kernel(
    heads_x, blocks_x, flags, q_ref, do_ref, win_ref, rnd_ref, glb_ref, dq_ref, g_ref,
    kcat, vcat, kt, s_buf, dp_buf, p_buf, ds_buf, acc, wacc, gacc,
):
    quarter = g_ref.shape[2]
    rand_total = blocks_x * R
    wacc[...] = jnp.zeros_like(wacc)
    gacc[...] = jnp.zeros_like(gacc)

    def fold(value, op):
        return op(value.reshape(BLOCK // 8, 8, PAIR), axis=0)

    def block_step(b, _):
        for j in range(LISTED):
            if j < 3:
                kv = win_ref[b + j]
            elif j < 3 + R:
                kv = rnd_ref[b * R + (j - 3)]
            else:
                kv = glb_ref[j - 3 - R]
            kcat[j] = kv[:, :DH]
            vcat[j] = kv[:, DH:]
            kt[:, j * BLOCK : (j + 1) * BLOCK] = kv[:, :DH].T
        acc[...] = jnp.zeros_like(acc)
        rows = pl.ds(pl.multiple_of(b * BLOCK, BLOCK), BLOCK)
        before_ok = jnp.logical_or(b > 0, flags[0] > 0)
        after_ok = jnp.logical_or(b < blocks_x - 1, flags[1] > 0)

        def pair_step(h, _):
            q = jnp.concatenate([q_ref[h, rows, :DH], q_ref[h, rows, DH:]], axis=0)
            do = jnp.concatenate([do_ref[h, rows, :DH], do_ref[h, rows, DH:]], axis=0)
            top = jnp.full((8, PAIR), NEG, F32)
            for j in range(LISTED):
                s = dot(kcat[j], q, NT)
                if j == 0:
                    s = jnp.where(before_ok, s, NEG)
                if j == 2:
                    s = jnp.where(after_ok, s, NEG)
                s_buf[j] = s
                top = jnp.maximum(top, fold(s, jnp.max))
            top = jnp.max(top, axis=0, keepdims=True)
            total = jnp.zeros((8, PAIR), F32)
            inner = jnp.zeros((8, PAIR), F32)
            for j in range(LISTED):
                dp = dot(vcat[j], do, NT)
                e = jnp.exp2((s_buf[j] - top) * (FACTOR * LOG2E))
                total = total + fold(e, jnp.sum)
                inner = inner + fold(e * dp, jnp.sum)
                s_buf[j] = e
                dp_buf[j] = dp
            scale = 1.0 / jnp.sum(total, axis=0, keepdims=True)
            delta = jnp.sum(inner, axis=0, keepdims=True) * scale
            for j in range(LISTED):
                a = s_buf[j] * scale
                p_buf[j] = a.astype(BF16)
                ds_buf[j] = (a * (dp_buf[j] - delta)).astype(BF16)
            for j in range(LISTED):
                acc[j, :, :DH] += dot(ds_buf[j], q)
                acc[j, :, DH:] += dot(p_buf[j], do)
            dqt = dot(kt[...], ds_buf[...].reshape(LISTED * BLOCK, PAIR)) * FACTOR
            dq_ref[h, rows, :DH] = dqt[:, :BLOCK].T.astype(BF16)
            dq_ref[h, rows, DH:] = dqt[:, BLOCK:].T.astype(BF16)
            return 0

        lax.fori_loop(0, heads_x, pair_step, 0)
        for j in range(LISTED):
            grad = acc[j]
            if j < 3:
                wacc[b + j] += grad
            elif j < 3 + R:
                lane = lax.broadcasted_iota(jnp.int32, grad.shape, 1)
                grad = (grad * jnp.where(lane < DH, FACTOR, 1.0)).astype(BF16)
                for part in range(heads_x):
                    g_ref[part, b * R + (j - 3)] = grad[part * quarter : (part + 1) * quarter]
            else:
                gacc[j - 3 - R] += grad
        return 0

    lax.fori_loop(0, blocks_x, block_step, 0)
    lane = lax.broadcasted_iota(jnp.int32, (BLOCK, PAIR), 1)
    scale = jnp.where(lane < DH, FACTOR, 1.0)
    for j in range(blocks_x + 2 + G):
        grad = wacc[j] if j < blocks_x + 2 else gacc[j - blocks_x - 2]
        grad = (grad * scale).astype(BF16)
        for part in range(heads_x):
            g_ref[part, rand_total + j] = grad[part * quarter : (part + 1) * quarter]


def compute(flags, q_all, do_all, win, rnd, glb):
    heads_x, rows_x, _ = q_all.shape
    blocks_x = rows_x // BLOCK
    slots = blocks_x * R + blocks_x + 2 + G
    vmem = pl.BlockSpec(memory_space=pltpu.VMEM)
    flops = 2 * 5 * heads_x * rows_x * 2 * LISTED * BLOCK * DH
    return pl.pallas_call(
        functools.partial(compute_kernel, heads_x, blocks_x),
        out_shape=(
            jax.ShapeDtypeStruct(q_all.shape, BF16),
            jax.ShapeDtypeStruct((heads_x, slots, BLOCK // heads_x, PAIR), BF16),
        ),
        in_specs=[pl.BlockSpec(memory_space=pltpu.SMEM)] + [vmem] * 5,
        out_specs=(vmem, vmem),
        scratch_shapes=[
            pltpu.VMEM((LISTED, BLOCK, DH), BF16),
            pltpu.VMEM((LISTED, BLOCK, DH), BF16),
            pltpu.VMEM((DH, LISTED * BLOCK), BF16),
            pltpu.VMEM((LISTED, BLOCK, PAIR), F32),
            pltpu.VMEM((LISTED, BLOCK, PAIR), F32),
            pltpu.VMEM((LISTED, BLOCK, PAIR), BF16),
            pltpu.VMEM((LISTED, BLOCK, PAIR), BF16),
            pltpu.VMEM((LISTED, BLOCK, PAIR), F32),
            pltpu.VMEM((blocks_x + 2, BLOCK, PAIR), F32),
            pltpu.VMEM((G, BLOCK, PAIR), F32),
        ],
        compiler_params=pltpu.CompilerParams(vmem_limit_bytes=40 * 2**20),
        cost_estimate=pl.CostEstimate(flops=flops, bytes_accessed=8 * 2**20, transcendentals=0),
        name="compute",
    )(flags, q_all, do_all, win, rnd, glb)


def a2a(value, axis):
    return lax.all_to_all(value, axis, split_axis=0, concat_axis=0, tiled=True)


def body(query_vectors, key_vectors, value_vectors, output_grad, random_blocks, global_blocks):
    seq = lax.axis_size("seq")
    heads_x = lax.axis_size("head")
    s = lax.axis_index("seq")
    x = lax.axis_index("head")
    rows = query_vectors.shape[0]
    blocks = rows // BLOCK
    blocks_x = blocks // heads_x
    quarter = BLOCK // heads_x
    entries = blocks_x * R

    kv = jnp.concatenate([key_vectors, value_vectors], axis=1).reshape(blocks, BLOCK, PAIR)
    owners = random_blocks // blocks
    within = random_blocks % blocks
    peers = jnp.arange(seq, dtype=jnp.int32)
    matched = owners[:, :, None] == peers[None, None, :]
    wanted = jnp.max(jnp.where(matched, within[:, :, None], -1), axis=(0, 1))
    requested = a2a(wanted.reshape(seq, 1), "seq")[:, 0]
    kv_part = lax.dynamic_slice_in_dim(kv, x * quarter, quarter, 1)
    served = kv_part[jnp.clip(requested, 0, blocks - 1)]
    fetched = a2a(served, "seq")
    mine = fetched[owners.reshape(heads_x, entries)]
    rnd = a2a(mine, "head").transpose(1, 0, 2, 3).reshape(entries, BLOCK, PAIR)
    q_all = a2a(query_vectors.reshape(heads_x, blocks_x * BLOCK, PAIR), "head")
    do_all = a2a(output_grad.reshape(heads_x, blocks_x * BLOCK, PAIR), "head")
    up = [(i, (i + 1) % seq) for i in range(seq)]
    down = [(j, i) for i, j in up]
    before = lax.ppermute(kv[blocks - 1 :], "seq", up)
    after = lax.ppermute(kv[:1], "seq", down)
    extended = jnp.concatenate([before, kv, after], axis=0)
    win = lax.dynamic_slice_in_dim(extended, x * blocks_x, blocks_x + 2, 0)
    held = jnp.where(
        (global_blocks // blocks == s)[:, None, None], kv[global_blocks % blocks], 0
    ).astype(BF16)
    glb = lax.psum(held, "seq")
    flags = jnp.stack([s + x, seq - 1 - s + heads_x - 1 - x]).astype(jnp.int32)

    dq_all, grads = compute(flags, q_all, do_all, win, rnd, glb)

    query_grad = a2a(dq_all, "head").reshape(rows, PAIR)
    parts = a2a(grads, "head").astype(F32)
    hot = (owners.reshape(-1)[None, :] == peers[:, None]).astype(F32)
    from_entries = parts[:, :entries].reshape(heads_x * entries, quarter, PAIR)
    slots = jnp.einsum("en,nrc->erc", hot, from_entries, precision=lax.Precision.HIGHEST)
    returned = a2a(slots.astype(BF16), "seq").astype(F32)
    served_hot = (requested[None, :] == jnp.arange(blocks)[:, None]).astype(F32)
    total = jnp.einsum("be,erc->brc", served_hot, returned, precision=lax.Precision.HIGHEST)
    window = jnp.zeros((blocks + 2, quarter, PAIR), F32)
    for part in range(heads_x):
        window = window.at[part * blocks_x : part * blocks_x + blocks_x + 2].add(
            parts[part, entries : entries + blocks_x + 2]
        )
    into_last = lax.ppermute(window[0].astype(BF16), "seq", down).astype(F32)
    into_first = lax.ppermute(window[blocks + 1].astype(BF16), "seq", up).astype(F32)
    total = total + window[1 : blocks + 1]
    total = total.at[blocks - 1].add(into_last).at[0].add(into_first)
    glob = lax.psum(jnp.sum(parts[:, entries + blocks_x + 2 :], axis=0), "seq")
    owned = (global_blocks[None, :] == s * blocks + jnp.arange(blocks)[:, None]).astype(F32)
    total = total + jnp.einsum("bg,grc->brc", owned, glob, precision=lax.Precision.HIGHEST)
    final = lax.all_gather(total.astype(BF16), "head", axis=1, tiled=True).reshape(rows, PAIR)
    return query_grad, final[:, :DH], final[:, DH:]


def solution(mesh):
    return jax.shard_map(
        body,
        mesh=mesh,
        in_specs=(
            P("seq", "head"),
            P("seq", None),
            P("seq", None),
            P("seq", "head"),
            P("seq", None),
            P(),
        ),
        out_specs=(P("seq", "head"), P("seq", None), P("seq", None)),
        check_vma=False,
    )
```

time: 702 us -> 558 us (0.79)
  local copies, waits for them, and re-layouts: 131 us -> 18.9 us
  matrix products: 61.8 us -> 2.77 us
  blocking collectives: 0 us -> 55.3 us
  other arithmetic: 40.1 us -> 9.61 us
  Pallas kernels: 0 us -> 24.8 us
  waiting for transfers between devices: 408 us -> 392 us
    dot_general x30 -> x3, matrix products: 61.8 us -> 2.77 us  [the longest x1 1.36 us: body(): jnp.einsum('bg,grc->brc', owned, glob, precision=lax.Precision.HIGHEST)]
    all_to_all x0 -> x2, blocking collectives: none -> 55.3 us  [a2a(): return lax.all_to_all(value, axis, split_axis=0, concat_axis=0, tiled=True)]
    while x68 -> x0, local copies, waits for them, and re-layouts: 51.6 us -> none
    all_to_all x3 -> x6, waiting for transfers between devices: 83.2 us -> 46.8 us  [a2a(): return lax.all_to_all(value, axis, split_axis=0, concat_axis=0, tiled=True)]
    slice x12 -> x3, local copies, waits for them, and re-layouts: 34.2 us -> 2.3 us  [the longest x1 2.23 us: body(): return (query_grad, final[:, :DH], final[:, DH:])]
    pallas_call x0 -> x1, Pallas kernels: none -> 24.8 us  [compute(): pl.pallas_call(functools.partial(compute_kernel, heads_x, blocks_x), out_...]
    psum x3 -> x2, waiting for transfers between devices: 324 us -> 338 us  [the longest x1 171 us: body(): glb = lax.psum(held, 'seq')]
    reduce_sum x4 -> x1, other arithmetic: 11.8 us -> 0.02 us  [body(): glob = lax.psum(jnp.sum(parts[:, entries + blocks_x + 2:], axis=0), 'seq')]
  transfers between devices with their start and end apart: 10 -> 13, of which waited for: 5 -> 8; matrix products, arithmetic and copies ran while one was open for 4% -> 3% of each run, Pallas kernels for 0% -> 0%
where the time goes in v1:
time: 558 us; the launch traced here: 557 us
  waiting for transfers between devices  392 us (70%)
  blocking collectives  55.3 us (10%)
  starting transfers between devices  40.1 us (7%)
  Pallas kernels  24.8 us (4%)
  local copies, waits for them, and re-layouts  18.9 us (3%)
  between operations  14 us (3%)
  other arithmetic  9.61 us (2%)
    psum x1, waiting for transfers between devices, body(): glb = lax.psum(held, 'seq')  171 us
    psum x1, waiting for transfers between devices, body(): glob = lax.psum(jnp.sum(parts[:, entries + blocks_x + 2:], axis=0), 'seq')  167 us
    all_to_all x2, blocking collectives, a2a(): return lax.all_to_all(value, axis, split_axis=0, concat_axis=0, tiled=True)  55.3 us
    all_to_all x6, waiting for transfers between devices, a2a(): return lax.all_to_all(value, axis, split_axis=0, concat_axis=0, tiled=True)  46.8 us
    all_to_all x6, starting transfers between devices, a2a(): return lax.all_to_all(value, axis, split_axis=0, concat_axis=0, tiled=True)  34.3 us
    pallas_call x1, Pallas kernels, compute(): pl.pallas_call(functools.partial(compute_kernel, heads_x, blocks_x), out_...  24.8 us
  transfers between devices with their start and end apart: 13, of which 8 were waited for; matrix products, arithmetic and copies ran while one was open for 3% of the time, Pallas kernels for 0%

profile of v1, /device:TPU:1, one launch (start us, length us, event | category | flops | bytes accessed | tf_op | source)
XLA Modules:
  0.0 557.1 jit_solution(9818403369969052882)
XLA Ops:
  8.7 13.1 %all-to-all-start.2 = ((s32[64,1,1]{2,1,0:T(1,128)}), s32[64,1,1]{2,1,0:T(1,128)S(1)}, u32[]{:S(2)}, u32[]{:S(2)}) async-start(s32[64,1,1]{2,1,0:T(1,128)} %copy.47), calls=%async_computation.2 | async-start | bytes 65536 | tf_op jit(solution)/shard_map/all_to_all | solution.py:149
  21.8 1.1 constant_dynamic-update-slice_fusion.1
  23.0 1.2 constant_dynamic-update-slice_fusion
  24.2 7.0 %all-to-all-done.2 = s32[64,1,1]{2,1,0:T(1,128)S(1)} async-done(((s32[64,1,1]{2,1,0:T(1,128)}), s32[64,1,1]{2,1,0:T(1,128)S(1)}, u32[]{:S(2)}, u32[]{:S(2)}) %all-to-all-start.2) | async-done | bytes 288 | tf_op jit(solution)/shard_map/all_to_all | solution.py:149
  31.2 2.4 fusion.29
  34.2 32.2 %all_to_all.44 = bf16[64,32,256]{2,1,0:T(8,128)(2,1)S(1)} all-to-all(bf16[64,32,256]{2,1,0:T(8,128)(2,1)S(1)} %gather_fusion), channel_id=1, replica_groups=mesh['seq'=64,'head'=4] {'seq'}, dimensions={0} | all-to-all | bytes 2097152 | tf_op jit(solution)/shard_map/all_to_all | solution.py:149
  66.4 4.0 all-to-all-start
  70.7 1.6 gather_fusion.1
  72.3 11.9 %all-to-all-done.q_ref = bf16[4,512,256]{2,1,0:T(8,128)(2,1)S(1)} async-done(((bf16[4,512,256]{2,1,0:T(8,128)(2,1)}), bf16[4,512,256]{2,1,0:T(8,128)(2,1)S(1)}, u32[]{:S(2)}, u32[]{:S(2)}) %all-to-all-start) | async-done | bytes 1048608 | tf_op jit(solution)/shard_map/all_to_all | solution.py:149
  84.2 4.2 all-to-all-start.4
  88.4 9.9 %all-to-all-done.4 = bf16[4,12,32,256]{3,2,1,0:T(8,128)(2,1)} async-done(((bf16[4,12,32,256]{3,2,1,0:T(8,128)(2,1)}), bf16[4,12,32,256]{3,2,1,0:T(8,128)(2,1)}, u32[]{:S(2)}, u32[]{:S(2)}) %all-to-all-start.4) | async-done | bytes 786464 | tf_op jit(solution)/shard_map/all_to_all | solution.py:149
  98.3 3.5 all-to-all-start.1
  103.2 3.5 collective-permute-start.1
  106.9 2.1 collective-permute-done.1
  109.6 1.0 fusion.5.win_ref
  110.6 2.1 copy.49
  112.7 171.0 %all-reduce.4.cloned.1.call-done.glb_ref = bf16[2,128,256]{2,1,0:T(8,128)(2,1)} async-done(((bf16[2,128,256]{2,1,0:T(8,128)(2,1)}), bf16[2,128,256]{2,1,0:T(8,128)(2,1)}) %all-reduce.4.cloned.1.call-update) | async-done | bytes 131088 | tf_op jit(solution)/shard_map/psum | solution.py:186
  283.7 1.1 copy-done
  285.7 24.8 %compute.1 = (bf16[4,512,256]{2,1,0:T(8,128)(2,1)S(1)}, bf16[4,20,32,256]{3,2,1,0:T(8,128)(2,1)}) custom-call(s32[2]{0:T(128)S(1)} %pad_add_fusion.flags, bf16[4,512,256]{2,1,0:T(8,128)(2,1)S(1)} %all-to-all-done.q_ref, bf16[4,512,256]{2,1,0:T(8,128)(2,1)S(1)} %all-to-all-done.1.do_ref, bf16[6,128,256]{2,1,0:T(8,128)(2,1)S(1)} %fusion.5.win_ref, ...), custom_call_target="tpu_custom_call" | custom-call | flops 5368709120 | bytes 8388608 | tf_op jit(solution)/shard_map/compute/pallas_call | solution.py:122
  310.5 4.0 all-to-all-start.6
  314.5 18.0 %all-to-all-done.6 = bf16[4,20,32,256]{3,2,1,0:T(8,128)(2,1)S(1)} async-done(((bf16[4,20,32,256]{3,2,1,0:T(8,128)(2,1)}), bf16[4,20,32,256]{3,2,1,0:T(8,128)(2,1)S(1)}, u32[]{:S(2)}, u32[]{:S(2)}) %all-to-all-start.6) | async-done | bytes 1310752 | tf_op jit(solution)/shard_map/all_to_all | solution.py:149
  333.4 1.6 copy.52
  334.9 5.5 all-to-all-start.7
  340.9 1.5 copy-done.2
  344.1 1.0 fusion.10
  347.8 1.3 collective-permute-start.3
  349.1 167.0 %all-reduce.6.cloned.1.call-done = f32[2,32,256]{2,0,1:T(2,128)} async-done(((f32[2,32,256]{2,0,1:T(2,128)}), f32[2,32,256]{2,0,1:T(2,128)}) %all-reduce.6.cloned.1.call-update) | async-done | bytes 65552 | tf_op jit(solution)/shard_map/psum | solution.py:208
  516.1 1.4 fusion.22
  518.5 1.0 fusion.3
  519.6 23.0 %all_to_all.45 = bf16[4,512,256]{2,1,0:T(8,128)(2,1)S(1)} all-to-all(bf16[4,512,256]{2,1,0:T(8,128)(2,1)S(1)} %get-tuple-element.77), channel_id=1, replica_groups=mesh['seq'=64,'head'=4] {'head'}, dimensions={0} | all-to-all | bytes 2097152 | tf_op jit(solution)/shard_map/all_to_all | solution.py:149
  542.6 4.8 all-gather.2.cloned.1.call-done
  547.4 2.2 fusion.30
  (64 shorter events, 13.3 us)
Async XLA Ops:
  8.7 22.5 %all-to-all-start.2 = ((s32[64,1,1]{2,1,0:T(1,128)}), s32[64,1,1]{2,1,0:T(1,128)S(1)}, u32[]{:S(2)}, u32[]{:S(2)}) async-start(s32[64,1,1]{2,1,0:T(1,128)} %copy.47), calls=%async_computation.2 | async-start | bytes 65536 | tf_op jit(solution)/shard_map/all_to_all | solution.py:149
  24.1 42.3 %copy-start.3 = (bf16[2048,256]{1,0:T(8,128)(2,1)}, bf16[2048,256]{1,0:T(8,128)(2,1)S(1)}, u32[]{:S(2)}) copy-start(bf16[2048,256]{1,0:T(8,128)(2,1)S(1)} %constant_dynamic-update-slice_fusion) | copy-start | bytes 3145732
  34.2 36.5 %copy-start.6 = (s32[2]{0:T(128)S(1)}, s32[2]{0:T(128)}, u32[]{:S(2)}) copy-start(s32[2]{0:T(128)} %param.23) | copy-start | bytes 28
  66.4 17.8 %all-to-all-start = ((bf16[4,512,256]{2,1,0:T(8,128)(2,1)}), bf16[4,512,256]{2,1,0:T(8,128)(2,1)S(1)}, u32[]{:S(2)}, u32[]{:S(2)}) async-start(bf16[4,512,256]{2,1,0:T(8,128)(2,1)} %bitcast.67), calls=%async_computation | async-start | bytes 2097152 | tf_op jit(solution)/shard_map/all_to_all | solution.py:149
  70.7 31.2 %copy-start.4 = (bf16[2048,256]{1,0:T(8,128)(2,1)S(1)}, bf16[2048,256]{1,0:T(8,128)(2,1)}, u32[]{:S(2)}) copy-start(bf16[2048,256]{1,0:T(8,128)(2,1)} %copy-done.3) | copy-start | bytes 3145732
  84.2 14.1 %all-to-all-start.4 = ((bf16[4,12,32,256]{3,2,1,0:T(8,128)(2,1)}), bf16[4,12,32,256]{3,2,1,0:T(8,128)(2,1)}, u32[]{:S(2)}, u32[]{:S(2)}) async-start(bf16[4,12,32,256]{3,2,1,0:T(8,128)(2,1)} %bitcast.65), calls=%async_computation.4 | async-start | bytes 1572864 | tf_op jit(solution)/shard_map/all_to_all | solution.py:149
  98.3 185.4 %all-to-all-start.1 = ((bf16[4,512,256]{2,1,0:T(8,128)(2,1)}), bf16[4,512,256]{2,1,0:T(8,128)(2,1)S(1)}, u32[]{:S(2)}, u32[]{:S(2)}) async-start(bf16[4,512,256]{2,1,0:T(8,128)(2,1)} %bitcast.68), calls=%async_computation.1 | async-start | bytes 2097152 | tf_op jit(solution)/shard_map/all_to_all | solution.py:149
  101.8 181.9 %all-reduce.4.cloned.1.call-start = ((), (), s32[]{:S(2)}) async-start(), calls=%async_computation.8 | async-start | bytes 262144 | tf_op jit(solution)/shard_map/psum | solution.py:186
  103.2 5.8 %collective-permute-start.1 = (bf16[1,128,256]{2,1,0:T(8,128)(2,1)S(1)}, bf16[1,128,256]{2,1,0:T(8,128)(2,1)S(1)}, u32[]{:S(2)}, u32[]{:S(2)}) collective-permute-start(bf16[1,128,256]{2,1,0:T(8,128)(2,1)S(1)} %get-tuple-element.83), channel_id=1, source_target_pairs={{4,0},{8,4},{12,8},{16,12},{20,16},{24,20},{28,24},{32,28},{36,32}... | collective-permute-start | bytes 196616 | tf_op jit(solution)/shard_map/ppermute | solution.py:180
  106.7 2.9 collective-permute-start
  109.0 0.6 copy-start.5
  283.7 1.1 copy-start
  284.8 0.9 copy-start.1
  310.5 22.1 %all-to-all-start.6 = ((bf16[4,20,32,256]{3,2,1,0:T(8,128)(2,1)}), bf16[4,20,32,256]{3,2,1,0:T(8,128)(2,1)S(1)}, u32[]{:S(2)}, u32[]{:S(2)}) async-start(bf16[4,20,32,256]{3,2,1,0:T(8,128)(2,1)} %get-tuple-element.78), calls=%async_computation.6 | async-start | bytes 2621440 | tf_op jit(solution)/shard_map/all_to_all | solution.py:149
  334.9 182.6 %all-to-all-start.7 = ((bf16[64,32,256]{2,1,0:T(8,128)(2,1)}), bf16[64,32,256]{2,1,0:T(8,128)(2,1)S(1)}, u32[]{:S(2)}, u32[]{:S(2)}) async-start(bf16[64,32,256]{2,1,0:T(8,128)(2,1)} %copy.52), calls=%async_computation.7 | async-start | bytes 2097152 | tf_op jit(solution)/shard_map/all_to_all | solution.py:149
  340.4 175.7 %all-reduce.6.cloned.1.call-start = ((), (), s32[]{:S(2)}) async-start(), calls=%async_computation.9 | async-start | bytes 131072 | tf_op jit(solution)/shard_map/psum | solution.py:208
  340.9 1.5 copy-start.2
  342.4 173.8 %copy-start.7 = (s32[2]{0:T(128)S(1)}, s32[2]{0:T(128)}, u32[]{:S(2)}) copy-start(s32[2]{0:T(128)} %param.23) | copy-start | bytes 28
  343.1 204.3 %all-gather.2.cloned.1.call-start = ((), (), s32[]{:S(2)}) async-start(), calls=%async_computation.10 | async-start | bytes 1310720 | tf_op jit(solution)/shard_map/all_gather | solution.py:211
  347.1 171.4 %collective-permute-start.2 = (bf16[32,256]{1,0:T(8,128)(2,1)S(1)}, bf16[32,256]{1,0:T(8,128)(2,1)S(1)}, u32[]{:S(2)}, u32[]{:S(2)}) collective-permute-start(bf16[32,256]{1,0:T(8,128)(2,1)S(1)} %fusion.15), channel_id=1, source_target_pairs={{4,0},{8,4},{12,8},{16,12},{20,16},{24,20},{28,24},{32,28},{36,32}... | collective-permute-start | bytes 49160 | tf_op jit(solution)/shard_map/ppermute | solution.py:204
  347.8 170.7 %collective-permute-start.3 = (bf16[32,256]{1,0:T(8,128)(2,1)S(1)}, bf16[32,256]{1,0:T(8,128)(2,1)S(1)}, u32[]{:S(2)}, u32[]{:S(2)}) collective-permute-start(bf16[32,256]{1,0:T(8,128)(2,1)S(1)} %fusion.16), channel_id=1, source_target_pairs={{0,4},{4,8},{8,12},{12,16},{16,20},{20,24},{24,28},{28,32},{32,36}... | collective-permute-start | bytes 49160 | tf_op jit(solution)/shard_map/ppermute | solution.py:205
Sparse Core Ops, SparseCore 0:
  106.7 176.9 all-reduce.3
  345.3 170.7 all-reduce.5
  519.7 27.6 all-gather.1

commit v2 on v1

--- a/solution.py
+++ b/solution.py
@@ -19,6 +19,7 @@
 NT = (((1,), (1,)), ((), ()))
 F32 = jnp.float32
 BF16 = jnp.bfloat16
+MESH = pl.DeviceIdType.MESH
 
 
 def dot(a, b, dims=(((1,), (0,)), ((), ()))):
@@ -26,11 +27,28 @@
 
 
 def compute_kernel(
-    heads_x, blocks_x, flags, q_ref, do_ref, win_ref, rnd_ref, glb_ref, dq_ref, g_ref,
-    kcat, vcat, kt, s_buf, dp_buf, p_buf, ds_buf, acc, wacc, gacc,
+    heads_x, blocks_x, flags, q_ref, do_ref, k_ref, v_ref, halo_ref, rnd_ref, pieces_ref,
+    dq_ref, g_ref, win_ref, glb_ref, kcat, vcat, kt, s_buf, dp_buf, p_buf, ds_buf, acc, wacc, gacc,
 ):
     quarter = g_ref.shape[2]
     rand_total = blocks_x * R
+    blocks = k_ref.shape[0]
+    for i in range(blocks_x + 2):
+        at = flags[2] * blocks_x + (i - 1)
+        inner_at = jnp.clip(at, 0, blocks - 1)
+        for n, ref in enumerate((k_ref, v_ref)):
+            value = ref[inner_at]
+            if i == 0:
+                value = jnp.where(at < 0, halo_ref[0, n], value)
+            if i == blocks_x + 1:
+                value = jnp.where(at >= blocks, halo_ref[1, n], value)
+            win_ref[i, :, n * DH : (n + 1) * DH] = value
+    per = BLOCK // 16
+    for g in range(G):
+        for n in range(2):
+            first = (g * 2 + n) * per
+            whole = pieces_ref[first : first + per].reshape(BLOCK, DH)
+            glb_ref[g, :, n * DH : (n + 1) * DH] = whole
     wacc[...] = jnp.zeros_like(wacc)
     gacc[...] = jnp.zeros_like(gacc)
 
@@ -113,7 +131,7 @@
             g_ref[part, rand_total + j] = grad[part * quarter : (part + 1) * quarter]
 
 
-def compute(flags, q_all, do_all, win, rnd, glb):
+def compute(flags, q_all, do_all, keys, values, halo, rnd, pieces):
     heads_x, rows_x, _ = q_all.shape
     blocks_x = rows_x // BLOCK
     slots = blocks_x * R + blocks_x + 2 + G
@@ -125,9 +143,11 @@
             jax.ShapeDtypeStruct(q_all.shape, BF16),
             jax.ShapeDtypeStruct((heads_x, slots, BLOCK // heads_x, PAIR), BF16),
         ),
-        in_specs=[pl.BlockSpec(memory_space=pltpu.SMEM)] + [vmem] * 5,
+        in_specs=[pl.BlockSpec(memory_space=pltpu.SMEM)] + [vmem] * 7,
         out_specs=(vmem, vmem),
         scratch_shapes=[
+            pltpu.VMEM((blocks_x + 2, BLOCK, PAIR), BF16),
+            pltpu.VMEM((G, BLOCK, PAIR), BF16),
             pltpu.VMEM((LISTED, BLOCK, DH), BF16),
             pltpu.VMEM((LISTED, BLOCK, DH), BF16),
             pltpu.VMEM((DH, LISTED * BLOCK), BF16),
@@ -142,11 +162,457 @@
         compiler_params=pltpu.CompilerParams(vmem_limit_bytes=40 * 2**20),
         cost_estimate=pl.CostEstimate(flops=flops, bytes_accessed=8 * 2**20, transcendentals=0),
         name="compute",
-    )(flags, q_all, do_all, win, rnd, glb)
-
-
-def a2a(value, axis):
-    return lax.all_to_all(value, axis, split_axis=0, concat_axis=0, tiled=True)
+    )(flags, q_all, do_all, keys, values, halo, rnd, pieces)
+
+
+def arrived(ref, sem):
+    pltpu.make_async_copy(ref, ref, sem).wait()
+
+
+def greet(seq, heads_x, s, x):
+    barrier = pltpu.get_barrier_semaphore()
+
+    def greet_seq(j, _):
+        pl.semaphore_signal(
+            barrier, inc=1, device_id=(lax.rem(s + j, seq), x), device_id_type=MESH
+        )
+        return 0
+
+    lax.fori_loop(1, seq, greet_seq, 0)
+    for d in range(1, heads_x):
+        pl.semaphore_signal(
+            barrier, inc=1, device_id=(s, lax.rem(x + d, heads_x)), device_id_type=MESH
+        )
+    pl.semaphore_wait(barrier, seq - 1 + heads_x - 1)
+
+
+def relays(seq, pieces):
+    return max(1, seq // pieces), max(1, pieces // seq)
+
+
+def fetch_kernel(
+    seq, heads_x, table, wanted_ref, q_ref, do_ref, k_ref, v_ref,
+    wbuf, q_all, do_all, halo, rnd, gout,
+    wsm, send_buf, fq, send2, cand, gin, relay_buf, sem_w, sem_g, sem_b, sem_h, sem_q, sem_d,
+    sem_f, sem_r, local_sem,
+):
+    s = lax.axis_index("seq")
+    x = lax.axis_index("head")
+    blocks = k_ref.shape[0]
+    quarter = BLOCK // heads_x
+    entries = rnd.shape[0]
+    rows_x = q_all.shape[1]
+    pieces = gout.shape[0]
+    per = BLOCK // 16
+    stride, ppr = relays(seq, pieces)
+    count = pieces // ppr
+    part = pl.ds(pl.multiple_of(x * quarter, quarter), quarter)
+
+    def remote(src, dst, sem, to):
+        return pltpu.make_async_remote_copy(
+            src_ref=src, dst_ref=dst, send_sem=sem.at[0], recv_sem=sem.at[1],
+            device_id=to, device_id_type=MESH,
+        )
+
+    for g in range(G):
+        at = table[heads_x * entries + G + g]
+        for n, ref in enumerate((k_ref, v_ref)):
+            first = (g * 2 + n) * per
+            cand[first : first + per] = ref[at].reshape(per, 16, DH)
+    wbuf[s] = wanted_ref[...]
+
+    own_rows = pl.ds(pl.multiple_of(x * rows_x, rows_x), rows_x)
+    own_q = pltpu.make_async_copy(q_ref.at[own_rows], q_all.at[x], local_sem.at[0])
+    own_do = pltpu.make_async_copy(do_ref.at[own_rows], do_all.at[x], local_sem.at[1])
+    own_q.start()
+    own_do.start()
+
+    greet(seq, heads_x, s, x)
+
+    def send_wanted(j, _):
+        remote(wanted_ref, wbuf.at[s], sem_w, (lax.rem(s + j, seq), x)).start()
+        return 0
+
+    lax.fori_loop(1, seq, send_wanted, 0)
+
+    is_relay = lax.rem(s, stride) == 0
+    mine = s // stride
+
+    def send_cand(r, _):
+        @pl.when(r * stride != s)
+        def _():
+            remote(
+                cand.at[pl.ds(r * ppr, ppr)], gin.at[s], sem_g, (r * stride, x)
+            ).start()
+
+        return 0
+
+    lax.fori_loop(0, count, send_cand, 0)
+
+    @pl.when(is_relay)
+    def _():
+        gin[s] = cand[pl.ds(mine * ppr, ppr)]
+
+    for d in range(1, heads_x):
+        to = lax.rem(x + d, heads_x)
+        rows = pl.ds(pl.multiple_of(to * rows_x, rows_x), rows_x)
+        remote(q_ref.at[rows], q_all.at[x], sem_q, (s, to)).start()
+        remote(do_ref.at[rows], do_all.at[x], sem_d, (s, to)).start()
+
+    after = (lax.rem(s + 1, seq), x)
+    before = (lax.rem(s + seq - 1, seq), x)
+    for n, ref in enumerate((k_ref, v_ref)):
+        remote(ref.at[blocks - 1], halo.at[0, n], sem_h, after).start()
+        remote(ref.at[0], halo.at[1, n], sem_h, before).start()
+
+    arrived(wbuf.at[pl.ds(0, seq - 1)], sem_w.at[1])
+    to_smem = pltpu.make_async_copy(wbuf, wsm, local_sem.at[2])
+    to_smem.start()
+    to_smem.wait()
+
+    def serve(e, _):
+        at = wsm[e, 0, s]
+        send_buf[e, :, :DH] = k_ref[at, part, :]
+        send_buf[e, :, DH:] = v_ref[at, part, :]
+        return 0
+
+    lax.fori_loop(0, seq, serve, 0)
+    fq[s] = send_buf[s]
+
+    def send_served(j, _):
+        e = lax.rem(s + j, seq)
+        remote(send_buf.at[e], fq.at[s], sem_f, (e, x)).start()
+        return 0
+
+    lax.fori_loop(1, seq, send_served, 0)
+
+    @pl.when(is_relay)
+    def _():
+        arrived(gin.at[pl.ds(0, seq - 1)], sem_g.at[1])
+        for i in range(ppr):
+            g = (mine * ppr + i) // (2 * per)
+            relay_buf[i] = gin[table[heads_x * entries + g], i]
+        gout[pl.ds(mine * ppr, ppr)] = relay_buf[...]
+
+        def send_piece(j, _):
+            remote(
+                relay_buf, gout.at[pl.ds(mine * ppr, ppr)], sem_b, (lax.rem(s + j, seq), x)
+            ).start()
+            return 0
+
+        lax.fori_loop(1, seq, send_piece, 0)
+
+    arrived(fq.at[pl.ds(0, seq - 1)], sem_f.at[1])
+    for d in range(1, heads_x):
+        to = lax.rem(x + d, heads_x)
+        for j in range(entries):
+            send2[d - 1, j] = fq[table[to * entries + j]]
+    for d in range(1, heads_x):
+        to = lax.rem(x + d, heads_x)
+        remote(send2.at[d - 1], rnd.at[:, part, :], sem_r, (s, to)).start()
+    for j in range(entries):
+        rnd[j, part, :] = fq[table[x * entries + j]]
+
+    arrived(send2, sem_r.at[1])
+    arrived(q_all.at[pl.ds(0, heads_x - 1)], sem_q.at[1])
+    arrived(do_all.at[pl.ds(0, heads_x - 1)], sem_d.at[1])
+    arrived(halo, sem_h.at[1])
+    own_q.wait()
+    own_do.wait()
+
+    @pl.when(is_relay)
+    def _():
+        arrived(gout.at[pl.ds(0, (count - 1) * ppr)], sem_b.at[1])
+        arrived(gin.at[pl.ds(0, seq - 1)], sem_b.at[0])
+        if count > 1:
+            arrived(gin.at[pl.ds(0, count - 1)], sem_g.at[0])
+
+    @pl.when(jnp.logical_not(is_relay))
+    def _():
+        arrived(gout, sem_b.at[1])
+        arrived(gin.at[pl.ds(0, count)], sem_g.at[0])
+
+    arrived(wbuf.at[pl.ds(0, seq - 1)], sem_w.at[0])
+    arrived(send_buf.at[pl.ds(0, seq - 1)], sem_f.at[0])
+    arrived(send2, sem_r.at[0])
+    arrived(q_all.at[pl.ds(0, heads_x - 1)], sem_q.at[0])
+    arrived(do_all.at[pl.ds(0, heads_x - 1)], sem_d.at[0])
+    arrived(halo, sem_h.at[0])
+
+
+def fetch(seq, heads_x, table, wanted, query, grad, keys, values):
+    rows, width = query.shape
+    rows_x = rows // heads_x
+    entries = rows_x // BLOCK * R
+    quarter = BLOCK // heads_x
+    pieces = G * 2 * BLOCK // 16
+    _, ppr = relays(seq, pieces)
+    vmem = pl.BlockSpec(memory_space=pltpu.VMEM)
+    anyspec = pl.BlockSpec(memory_space=pl.ANY)
+    pair = pltpu.SemaphoreType.DMA((2,))
+    return pl.pallas_call(
+        functools.partial(fetch_kernel, seq, heads_x),
+        out_shape=(
+            jax.ShapeDtypeStruct((seq, 1, 128), jnp.int32),
+            jax.ShapeDtypeStruct((heads_x, rows_x, width), BF16),
+            jax.ShapeDtypeStruct((heads_x, rows_x, width), BF16),
+            jax.ShapeDtypeStruct((2, 2, BLOCK, DH), BF16),
+            jax.ShapeDtypeStruct((entries, BLOCK, PAIR), BF16),
+            jax.ShapeDtypeStruct((pieces, 16, DH), BF16),
+        ),
+        in_specs=[pl.BlockSpec(memory_space=pltpu.SMEM), vmem, anyspec, anyspec, vmem, vmem],
+        out_specs=(vmem,) * 6,
+        scratch_shapes=[
+            pltpu.SMEM((seq, 1, 128), jnp.int32),
+            pltpu.VMEM((seq, quarter, PAIR), BF16),
+            pltpu.VMEM((seq, quarter, PAIR), BF16),
+            pltpu.VMEM((heads_x - 1, entries, quarter, PAIR), BF16),
+            pltpu.VMEM((pieces, 16, DH), BF16),
+            pltpu.VMEM((seq, ppr, 16, DH), BF16),
+            pltpu.VMEM((ppr, 16, DH), BF16),
+            pair, pair, pair, pair, pair, pair, pair, pair,
+            pltpu.SemaphoreType.DMA((3,)),
+        ],
+        compiler_params=pltpu.CompilerParams(
+            vmem_limit_bytes=30 * 2**20, collective_id=0, has_side_effects=True
+        ),
+        name="fetch",
+    )(table, wanted, query, grad, keys, values)
+
+
+def return_kernel(
+    seq, heads_x, table, own, g_ref, dq_ref, qg, kg, vg,
+    parts, run, sbuf, rbuf, run2, edge, gp, gin, relay_buf, gtot,
+    sem_e, sem_a, sem_q, sem_s, sem_n, sem_g, sem_b, sem_k, sem_v, local_sem,
+):
+    s = lax.axis_index("seq")
+    x = lax.axis_index("head")
+    rows_x = dq_ref.shape[1]
+    blocks_x = rows_x // BLOCK
+    blocks = blocks_x * heads_x
+    entries = blocks_x * R
+    quarter = BLOCK // heads_x
+    slots = g_ref.shape[1]
+    rest = slots - entries
+    pieces = gp.shape[0]
+    stride, ppr = relays(seq, pieces)
+    count = pieces // ppr
+    total_entries = heads_x * entries
+    last_e = total_entries
+    prev_r = last_e + seq
+    last_r = prev_r + seq
+    part = pl.ds(pl.multiple_of(x * quarter, quarter), quarter)
+    rand_part = pl.ds(0, entries)
+    rest_part = pl.ds(entries, rest)
+
+    def remote(src, dst, sem, to):
+        return pltpu.make_async_remote_copy(
+            src_ref=src, dst_ref=dst, send_sem=sem.at[0], recv_sem=sem.at[1],
+            device_id=to, device_id_type=MESH,
+        )
+
+    greet(seq, heads_x, s, x)
+    for d in range(1, heads_x):
+        to = lax.rem(x + d, heads_x)
+        remote(g_ref.at[to, rand_part], parts.at[x, rand_part], sem_e, (s, to)).start()
+    for d in range(1, heads_x):
+        to = lax.rem(x + d, heads_x)
+        remote(g_ref.at[to, rest_part], parts.at[x, rest_part], sem_a, (s, to)).start()
+    out_rows = pl.ds(pl.multiple_of(x * rows_x, rows_x), rows_x)
+    for d in range(1, heads_x):
+        to = lax.rem(x + d, heads_x)
+        remote(dq_ref.at[to], qg.at[out_rows], sem_q, (s, to)).start()
+    own_q = pltpu.make_async_copy(dq_ref.at[x], qg.at[out_rows], local_sem)
+    own_q.start()
+    parts[x] = g_ref[x]
+    run[0] = jnp.zeros((quarter, PAIR), F32)
+    run2[0] = jnp.zeros((quarter, PAIR), F32)
+
+    arrived(g_ref.at[pl.ds(0, heads_x - 1), rand_part], sem_e.at[1])
+    for src in range(heads_x):
+
+        def chain(j, _, src=src):
+            at = src * entries + j
+            run[at + 1] = parts[src, j].astype(F32) + run[table[at]]
+            return 0
+
+        lax.fori_loop(0, entries, chain, 0)
+
+    def fill(e, _):
+        sbuf[e] = run[table[last_e + e]].astype(BF16)
+        return 0
+
+    lax.fori_loop(0, seq, fill, 0)
+    rbuf[s] = sbuf[s]
+
+    def send_slot(j, _):
+        e = lax.rem(s + j, seq)
+        remote(sbuf.at[e], rbuf.at[s], sem_s, (e, x)).start()
+        return 0
+
+    lax.fori_loop(1, seq, send_slot, 0)
+
+    arrived(g_ref.at[pl.ds(0, heads_x - 1), rest_part], sem_a.at[1])
+    after = (lax.rem(s + 1, seq), x)
+    before = (lax.rem(s + seq - 1, seq), x)
+    remote(parts.at[0, entries], edge.at[1], sem_n, before).start()
+    remote(
+        parts.at[heads_x - 1, entries + blocks_x + 1], edge.at[0], sem_n, after
+    ).start()
+
+    chunks = quarter // 8
+    for g in range(G):
+        value = parts[0, entries + blocks_x + 2 + g].astype(F32)
+        for src in range(1, heads_x):
+            value = value + parts[src, entries + blocks_x + 2 + g].astype(F32)
+        for c in range(chunks):
+            for n in range(2):
+                gp[(g * chunks + c) * 2 + n] = value[
+                    c * 8 : (c + 1) * 8, n * DH : (n + 1) * DH
+                ]
+
+    is_relay = lax.rem(s, stride) == 0
+    mine = s // stride
+
+    @pl.when(is_relay)
+    def _():
+        gin[s] = gp[pl.ds(mine * ppr, ppr)]
+
+    def send_global(r, _):
+        @pl.when(r * stride != s)
+        def _():
+            remote(gp.at[pl.ds(r * ppr, ppr)], gin.at[s], sem_g, (r * stride, x)).start()
+
+        return 0
+
+    lax.fori_loop(0, count, send_global, 0)
+
+    @pl.when(is_relay)
+    def _():
+        arrived(gin.at[pl.ds(0, seq - 1)], sem_g.at[1])
+        relay_buf[...] = jnp.zeros_like(relay_buf)
+
+        def add(e, _):
+            relay_buf[...] += gin[e]
+            return 0
+
+        lax.fori_loop(0, seq, add, 0)
+        gtot[pl.ds(mine * ppr, ppr)] = relay_buf[...]
+
+        def send_piece(j, _):
+            remote(
+                relay_buf, gtot.at[pl.ds(mine * ppr, ppr)], sem_b, (lax.rem(s + j, seq), x)
+            ).start()
+            return 0
+
+        lax.fori_loop(1, seq, send_piece, 0)
+
+    arrived(edge, sem_n.at[1])
+
+    @pl.when(is_relay)
+    def _():
+        arrived(gtot.at[pl.ds(0, (count - 1) * ppr)], sem_b.at[1])
+        arrived(gin.at[pl.ds(0, seq - 1)], sem_b.at[0])
+        if count > 1:
+            arrived(gin.at[pl.ds(0, count - 1)], sem_g.at[0])
+
+    @pl.when(jnp.logical_not(is_relay))
+    def _():
+        arrived(gtot, sem_b.at[1])
+        arrived(gin.at[pl.ds(0, count)], sem_g.at[0])
+
+    arrived(rbuf.at[pl.ds(0, seq - 1)], sem_s.at[1])
+
+    def gather(e, _):
+        run2[e + 1] = rbuf[e].astype(F32) + run2[table[prev_r + e]]
+        return 0
+
+    lax.fori_loop(0, seq, gather, 0)
+    for b in range(blocks):
+        src, i = b // blocks_x, b % blocks_x
+        total = run2[table[last_r + b]] + parts[src, entries + 1 + i].astype(F32)
+        if i == 0:
+            more = edge[0] if src == 0 else parts[src - 1, entries + blocks_x + 1]
+            total = total + more.astype(F32)
+        if i == blocks_x - 1:
+            more = edge[1] if src == heads_x - 1 else parts[src + 1, entries]
+            total = total + more.astype(F32)
+        for c in range(chunks):
+            lines = pl.ds(pl.multiple_of(x * quarter + c * 8, 8), 8)
+            for n, ref in enumerate((kg, vg)):
+                value = total[c * 8 : (c + 1) * 8, n * DH : (n + 1) * DH]
+                for g in range(G):
+                    value = value + own[g * blocks + b] * gtot[(g * chunks + c) * 2 + n]
+                run[b, c * 8 : (c + 1) * 8, n * DH : (n + 1) * DH] = value
+        kg[b, part, :] = run[b, :, :DH].astype(BF16)
+        vg[b, part, :] = run[b, :, DH:].astype(BF16)
+    for d in range(1, heads_x):
+        to = (s, lax.rem(x + d, heads_x))
+        remote(kg.at[:, part, :], kg.at[:, part, :], sem_k, to).start()
+        remote(vg.at[:, part, :], vg.at[:, part, :], sem_v, to).start()
+
+    arrived(g_ref.at[pl.ds(0, heads_x - 1), rand_part], sem_e.at[0])
+    arrived(g_ref.at[pl.ds(0, heads_x - 1), rest_part], sem_a.at[0])
+    arrived(edge, sem_n.at[0])
+    arrived(rbuf.at[pl.ds(0, seq - 1)], sem_s.at[0])
+    arrived(dq_ref.at[pl.ds(0, heads_x - 1)], sem_q.at[0])
+    arrived(dq_ref.at[pl.ds(0, heads_x - 1)], sem_q.at[1])
+    own_q.wait()
+    others = pl.ds(0, (heads_x - 1) * quarter)
+    for sem, ref in ((sem_k, kg), (sem_v, vg)):
+        arrived(ref.at[:, others, :], sem.at[0])
+        arrived(ref.at[:, others, :], sem.at[1])
+
+
+def give_back(seq, heads_x, table, own, grads, dq_all):
+    _, rows_x, width = dq_all.shape
+    _, slots, quarter, _ = grads.shape
+    blocks_x = rows_x // BLOCK
+    blocks = blocks_x * heads_x
+    total_entries = blocks * R
+    pieces = G * (quarter // 8) * 2
+    _, ppr = relays(seq, pieces)
+    vmem = pl.BlockSpec(memory_space=pltpu.VMEM)
+    smem = pl.BlockSpec(memory_space=pltpu.SMEM)
+    pair = pltpu.SemaphoreType.DMA((2,))
+    return pl.pallas_call(
+        functools.partial(return_kernel, seq, heads_x),
+        out_shape=(
+            jax.ShapeDtypeStruct((heads_x * rows_x, width), BF16),
+            jax.ShapeDtypeStruct((blocks, BLOCK, DH), BF16),
+            jax.ShapeDtypeStruct((blocks, BLOCK, DH), BF16),
+        ),
+        in_specs=[smem, smem, vmem, vmem],
+        out_specs=(pl.BlockSpec(memory_space=pl.ANY), vmem, vmem),
+        scratch_shapes=[
+            pltpu.VMEM((heads_x, slots, quarter, PAIR), BF16),
+            pltpu.VMEM((total_entries + 1, quarter, PAIR), F32),
+            pltpu.VMEM((seq, quarter, PAIR), BF16),
+            pltpu.VMEM((seq, quarter, PAIR), BF16),
+            pltpu.VMEM((seq + 1, quarter, PAIR), F32),
+            pltpu.VMEM((2, quarter, PAIR), BF16),
+            pltpu.VMEM((pieces, 8, DH), F32),
+            pltpu.VMEM((seq, ppr, 8, DH), F32),
+            pltpu.VMEM((ppr, 8, DH), F32),
+            pltpu.VMEM((pieces, 8, DH), F32),
+            pair, pair, pair, pair, pair, pair, pair, pair, pair,
+            pltpu.SemaphoreType.DMA,
+        ],
+        compiler_params=pltpu.CompilerParams(
+            vmem_limit_bytes=30 * 2**20, collective_id=1, has_side_effects=True
+        ),
+        name="give_back",
+    )(table, own, grads, dq_all)
+
+
+def chain_of(keys, groups):
+    count = keys.shape[0]
+    order = jnp.arange(count, dtype=jnp.int32)
+    same = (keys[:, None] == keys[None, :]) & (order[None, :] < order[:, None])
+    previous = jnp.max(jnp.where(same, order[None, :] + 1, 0), axis=1)
+    hit = keys[None, :] == jnp.arange(groups, dtype=jnp.int32)[:, None]
+    last = jnp.max(jnp.where(hit, order[None, :] + 1, 0), axis=1)
+    return previous, last
 
 
 def body(query_vectors, key_vectors, value_vectors, output_grad, random_blocks, global_blocks):
@@ -156,60 +622,29 @@
     x = lax.axis_index("head")
     rows = query_vectors.shape[0]
     blocks = rows // BLOCK
-    blocks_x = blocks // heads_x
-    quarter = BLOCK // heads_x
-    entries = blocks_x * R
-
-    kv = jnp.concatenate([key_vectors, value_vectors], axis=1).reshape(blocks, BLOCK, PAIR)
-    owners = random_blocks // blocks
-    within = random_blocks % blocks
-    peers = jnp.arange(seq, dtype=jnp.int32)
-    matched = owners[:, :, None] == peers[None, None, :]
-    wanted = jnp.max(jnp.where(matched, within[:, :, None], -1), axis=(0, 1))
-    requested = a2a(wanted.reshape(seq, 1), "seq")[:, 0]
-    kv_part = lax.dynamic_slice_in_dim(kv, x * quarter, quarter, 1)
-    served = kv_part[jnp.clip(requested, 0, blocks - 1)]
-    fetched = a2a(served, "seq")
-    mine = fetched[owners.reshape(heads_x, entries)]
-    rnd = a2a(mine, "head").transpose(1, 0, 2, 3).reshape(entries, BLOCK, PAIR)
-    q_all = a2a(query_vectors.reshape(heads_x, blocks_x * BLOCK, PAIR), "head")
-    do_all = a2a(output_grad.reshape(heads_x, blocks_x * BLOCK, PAIR), "head")
-    up = [(i, (i + 1) % seq) for i in range(seq)]
-    down = [(j, i) for i, j in up]
-    before = lax.ppermute(kv[blocks - 1 :], "seq", up)
-    after = lax.ppermute(kv[:1], "seq", down)
-    extended = jnp.concatenate([before, kv, after], axis=0)
-    win = lax.dynamic_slice_in_dim(extended, x * blocks_x, blocks_x + 2, 0)
-    held = jnp.where(
-        (global_blocks // blocks == s)[:, None, None], kv[global_blocks % blocks], 0
-    ).astype(BF16)
-    glb = lax.psum(held, "seq")
-    flags = jnp.stack([s + x, seq - 1 - s + heads_x - 1 - x]).astype(jnp.int32)
-
-    dq_all, grads = compute(flags, q_all, do_all, win, rnd, glb)
-
-    query_grad = a2a(dq_all, "head").reshape(rows, PAIR)
-    parts = a2a(grads, "head").astype(F32)
-    hot = (owners.reshape(-1)[None, :] == peers[:, None]).astype(F32)
-    from_entries = parts[:, :entries].reshape(heads_x * entries, quarter, PAIR)
-    slots = jnp.einsum("en,nrc->erc", hot, from_entries, precision=lax.Precision.HIGHEST)
-    returned = a2a(slots.astype(BF16), "seq").astype(F32)
-    served_hot = (requested[None, :] == jnp.arange(blocks)[:, None]).astype(F32)
-    total = jnp.einsum("be,erc->brc", served_hot, returned, precision=lax.Precision.HIGHEST)
-    window = jnp.zeros((blocks + 2, quarter, PAIR), F32)
-    for part in range(heads_x):
-        window = window.at[part * blocks_x : part * blocks_x + blocks_x + 2].add(
-            parts[part, entries : entries + blocks_x + 2]
-        )
-    into_last = lax.ppermute(window[0].astype(BF16), "seq", down).astype(F32)
-    into_first = lax.ppermute(window[blocks + 1].astype(BF16), "seq", up).astype(F32)
-    total = total + window[1 : blocks + 1]
-    total = total.at[blocks - 1].add(into_last).at[0].add(into_first)
-    glob = lax.psum(jnp.sum(parts[:, entries + blocks_x + 2 :], axis=0), "seq")
-    owned = (global_blocks[None, :] == s * blocks + jnp.arange(blocks)[:, None]).astype(F32)
-    total = total + jnp.einsum("bg,grc->brc", owned, glob, precision=lax.Precision.HIGHEST)
-    final = lax.all_gather(total.astype(BF16), "head", axis=1, tiled=True).reshape(rows, PAIR)
-    return query_grad, final[:, :DH], final[:, DH:]
+
+    owners = (random_blocks // blocks).reshape(-1)
+    within = (random_blocks % blocks).reshape(-1)
+    peers = jnp.arange(128, dtype=jnp.int32)
+    matched = owners[:, None] == peers[None, :]
+    wanted = jnp.max(jnp.where(matched, within[:, None], 0), axis=0, keepdims=True)
+    table = jnp.concatenate([owners, global_blocks // blocks, global_blocks % blocks])
+    keys = key_vectors.reshape(blocks, BLOCK, DH)
+    values = value_vectors.reshape(blocks, BLOCK, DH)
+    wbuf, q_all, do_all, halo, rnd, pieces = fetch(
+        seq, heads_x, table, wanted, query_vectors, output_grad, keys, values
+    )
+    flags = jnp.stack([s + x, seq - 1 - s + heads_x - 1 - x, x]).astype(jnp.int32)
+    dq_all, grads = compute(flags, q_all, do_all, keys, values, halo, rnd, pieces)
+    requested = lax.dynamic_index_in_dim(wbuf[:, 0, :], s, 1, keepdims=False)
+    prev_e, last_e = chain_of(owners, seq)
+    prev_r, last_r = chain_of(requested, blocks)
+    chains = jnp.concatenate([prev_e, last_e, prev_r, last_r])
+    owned = global_blocks[:, None] == (s * blocks + jnp.arange(blocks, dtype=jnp.int32))[None, :]
+    query_grad, key_grad, value_grad = give_back(
+        seq, heads_x, chains, owned.reshape(-1).astype(F32), grads, dq_all
+    )
+    return query_grad, key_grad.reshape(rows, DH), value_grad.reshape(rows, DH)
 
 
 def solution(mesh):

time: 558 us -> 163 us (0.29)
  waiting for transfers between devices: 392 us -> 0 us
  Pallas kernels: 24.8 us -> 151 us
  blocking collectives: 55.3 us -> 0 us
  starting transfers between devices: 40.1 us -> 0 us
  between operations: 14 us -> 0.7 us
  local copies, waits for them, and re-layouts: 18.9 us -> 8.83 us
  other arithmetic: 9.61 us -> 3 us
    psum x2 -> x0, waiting for transfers between devices: 338 us -> none  [the longest x1 171 us: body(): glb = lax.psum(held, 'seq')]
    pallas_call x0 -> x2, Pallas kernels: none -> 127 us  [the longest x1 69.5 us: give_back(): pl.pallas_call(functools.partial(return_kernel, seq, heads_x), out_shape=...]
    all_to_all x2 -> x0, blocking collectives: 55.3 us -> none  [a2a(): return lax.all_to_all(value, axis, split_axis=0, concat_axis=0, tiled=True)]
    all_to_all x6 -> x0, waiting for transfers between devices: 46.8 us -> none  [a2a(): return lax.all_to_all(value, axis, split_axis=0, concat_axis=0, tiled=True)]
    all_to_all x6 -> x0, starting transfers between devices: 34.3 us -> none  [a2a(): return lax.all_to_all(value, axis, split_axis=0, concat_axis=0, tiled=True)]
    ppermute x4 -> x0, starting transfers between devices: 5.63 us -> none  [the longest x1 3.49 us: body(): after = lax.ppermute(kv[:1], 'seq', down)]
  transfers between devices with their start and end apart: 13 -> 0, of which waited for: 8 -> 0; matrix products, arithmetic and copies ran while one was open for 3% -> 0% of each run, Pallas kernels for 0% -> 0%
where the time goes in v2:
time: 163 us
  Pallas kernels  151 us (93%)
  local copies, waits for them, and re-layouts  8.83 us (5%)
  other arithmetic  3 us (2%)
    pallas_call x1, Pallas kernels, give_back(): pl.pallas_call(functools.partial(return_kernel, seq, heads_x), out_shape=...  69.5 us
    pallas_call x1, Pallas kernels, fetch(): pl.pallas_call(functools.partial(fetch_kernel, seq, heads_x), out_shape=(...  57.2 us
    pallas_call x1, Pallas kernels, compute(): pl.pallas_call(functools.partial(compute_kernel, heads_x, blocks_x), out_...  23.7 us
    unnamed x15, local copies, waits for them, and re-layouts  7.09 us

profile of v2, /device:TPU:1, one launch (start us, length us, event | category | flops | bytes accessed | tf_op | source)
XLA Modules:
  0.0 163.1 jit_solution(4808004412619398865)
XLA Ops:
  0.6 0.1 pad_add_fusion.2.flags
  0.7 0.7 compare_convert_fusion
  1.5 0.1 reshape.52.own
  1.5 0.7 and_select_fusion.1
  2.2 0.7 add_select_fusion
  2.9 0.1 copy.14
  3.0 0.1 broadcast_in_dim.85
  3.1 0.1 copy.13
  3.2 0.1 eq.88
  3.2 0.1 pad_add_fusion.1.table
  3.3 0.1 select_reduce_fusion.1
  3.4 0.1 select_reduce_fusion.2
  3.5 0.2 select_reduce_fusion.3
  3.7 0.0 copy-start
  3.7 1.2 copy-done
  4.9 0.0 copy-start.1
  4.9 1.2 copy-done.1
  6.2 0.0 copy-start.2
  6.2 1.0 copy-done.2
  7.2 1.0 copy-done.4
  8.2 57.2 %fetch.1 = (s32[64,1,128]{2,1,0:T(1,128)S(1)}, bf16[4,512,256]{2,1,0:T(8,128)(2,1)S(1)}, bf16[4,512,256]{2,1,0:T(8,128)(2,1)S(1)}, bf16[2,2,128,128]{3,2,1,0:T(8...) custom-call(s32[52]{0:T(128)S(1)} %pad_add_fusion.1.table, s32[1,128]{1,0:T(1,128)S(1)} %bitcast.14, ...), custom_call_target="tpu_custom_call" | custom-call | tf_op jit(solution)/shard_map/fetch/pallas_call | solution.py:353
  65.5 1.3 dynamic-slice_reduce_fusion
  66.8 0.2 select_reduce_fusion
  67.0 0.1 select_reduce_fusion.4
  67.1 0.1 pad_add_fusion.table
  67.2 0.0 copy-done.3
  67.2 0.0 copy-done.5
  67.2 23.7 %compute.1 = (bf16[4,512,256]{2,1,0:T(8,128)(2,1)S(1)}, bf16[4,20,32,256]{3,2,1,0:T(8,128)(2,1)S(1)}) custom-call(s32[3]{0:T(128)S(1)} %pad_add_fusion.2.flags, bf16[4,512,256]{2,1,0:T(8,128)(2,1)S(1)} %get-tuple-element.15.q_ref, bf16[4,512,256]{2,1,0:T(8,128)(2,1)S(1)} %get-tuple-element.16.do_ref, bf16[16,128,128]{2,1,0:T(8,128)(2,1)S(1)} %bitcast.11, ...), custom_call_target="tpu_custom_call" | custom-call | flops 5368709120 | bytes 8388608 | tf_op jit(solution)/shard_map/compute/pallas_call | solution.py:140
  90.9 69.5 %give_back.1 = (bf16[2048,256]{1,0:T(8,128)(2,1)S(1)}, bf16[16,128,128]{2,1,0:T(8,128)(2,1)S(1)}, bf16[16,128,128]{2,1,0:T(8,128)(2,1)S(1)}) custom-call(s32[192]{0:T(256)S(1)} %pad_add_fusion.table, f32[32]{0:T(128)S(1)} %reshape.52.own, bf16[4,20,32,256]{3,2,1,0:T(8,128)(2,1)S(1)} %get-tuple-element.20.g_ref, bf16[4,512,256]{2,1,0:T(8,128)(2,1)S(1)} %get-tuple-element.21.dq_ref), custom_call_target="tpu_custom_call" | custom-call | tf_op jit(solution)/shard_map/give_back/pallas_call | solution.py:578
  160.5 1.0 copy.18
  161.5 0.8 copy.19
  162.3 0.8 copy.20
  (6 shorter events, 0.0 us)
Async XLA Ops:
  3.7 1.2 copy-start
  4.9 1.2 copy-start.1
  6.2 1.0 copy-start.2
  7.2 1.0 copy-start.4
  8.2 59.0 %copy-start.3 = (bf16[2048,128]{1,0:T(8,128)(2,1)S(1)}, bf16[2048,128]{1,0:T(8,128)(2,1)}, u32[]{:S(2)}) copy-start(bf16[2048,128]{1,0:T(8,128)(2,1)} %param.7) | copy-start | bytes 1572868
  8.2 59.0 %copy-start.5 = (bf16[2048,128]{1,0:T(8,128)(2,1)S(1)}, bf16[2048,128]{1,0:T(8,128)(2,1)}, u32[]{:S(2)}) copy-start(bf16[2048,128]{1,0:T(8,128)(2,1)} %param.8) | copy-start | bytes 1572868

commit v3 on v1

v3 whole, which is shorter than its diff:
```python
import functools
import types

import jax
import jax.numpy as jnp
from jax import lax
from jax.experimental import pallas as pl
from jax.experimental.pallas import tpu as pltpu
from jax.sharding import PartitionSpec as P

DH = 128
BLOCK = 128
R = 3
G = 2
NEAR = 3 + G
PAIR = 2 * DH
FACTOR = float(DH) ** -0.5
LOG2E = 1.4426950408889634
NEG = -1e30
NT = (((1,), (1,)), ((), ()))
F32 = jnp.float32
BF16 = jnp.bfloat16
I32 = jnp.int32
MESH = pl.DeviceIdType.MESH


def dot(a, b, dims=(((1,), (0,)), ((), ()))):
    return lax.dot_general(a, b, dims, preferred_element_type=F32)


def fold(value, op):
    return op(value.reshape(BLOCK // 8, 8, PAIR), axis=0)


def arrived(ref, sem):
    pltpu.make_async_copy(ref, ref, sem).wait()


def relays(seq, pieces):
    return max(1, seq // pieces), max(1, pieces // seq)


def loop(count, step, first=0):
    def run(i, carry):
        step(i)
        return carry

    lax.fori_loop(first, count, run, 0)


def shapes(seq, heads_x, blocks):
    blocks_x = blocks // heads_x
    quarter = BLOCK // heads_x
    rows_x = blocks_x * BLOCK
    chunks = heads_x * blocks_x
    pieces = G * 2 * BLOCK // 16
    ppr = relays(seq, pieces)[1]
    pieces2 = G * (quarter // 8) * 2
    ppr2 = relays(seq, pieces2)[1]
    v, dma = pltpu.VMEM, pltpu.SemaphoreType.DMA
    return dict(
        k=v((blocks, BLOCK, DH), BF16),
        v=v((blocks, BLOCK, DH), BF16),
        q=v((heads_x, rows_x, PAIR), BF16),
        do=v((heads_x, rows_x, PAIR), BF16),
        near=v((2, blocks_x + 2, BLOCK, DH), BF16),
        glob=v((G * 2 * BLOCK // 16, 16, DH), BF16),
        halo=v((2, 2, BLOCK, DH), BF16),
        rnd=v((blocks_x, R, BLOCK, PAIR), BF16),
        tcol=v((blocks * R, 128), I32),
        tvec=v((3, 1, 128), I32),
        tsm=pltpu.SMEM((3, 1, 128), I32),
        wvec=v((1, 128), I32),
        wbuf=v((seq, 1, 128), I32),
        wsm=pltpu.SMEM((seq, 1, 128), I32),
        rvec=v((2, 1, 128), I32),
        rsm=pltpu.SMEM((2, 1, 128), I32),
        served=v((seq, quarter, PAIR), BF16),
        fetched=v((seq, quarter, PAIR), BF16),
        picked=v((blocks_x, heads_x - 1, R, quarter, PAIR), BF16),
        cand=v((pieces, 16, DH), BF16),
        gin=v((seq, ppr, 16, DH), BF16),
        relay=v((ppr, 16, DH), BF16),
        e1=v((chunks, NEAR, BLOCK, PAIR), F32),
        dp1=v((chunks, NEAR, BLOCK, PAIR), F32),
        stats=v((chunks, 8, PAIR), F32),
        s_buf=v((NEAR, BLOCK, PAIR), F32),
        dp_buf=v((R, BLOCK, PAIR), F32),
        ds_far=v((chunks, R * BLOCK, PAIR), BF16),
        ds=v((NEAR * BLOCK, PAIR), BF16),
        p=v((NEAR, BLOCK, PAIR), BF16),
        kt=v((DH, (NEAR + R) * BLOCK), BF16),
        acc=v((R, BLOCK, PAIR), F32),
        wacc=v((blocks_x + 2 + G, BLOCK, PAIR), F32),
        dq=v((heads_x, rows_x, PAIR), BF16),
        far_out=v((heads_x, blocks_x, R, quarter, PAIR), BF16),
        far_in=v((heads_x, blocks_x, R, quarter, PAIR), BF16),
        near_out=v((heads_x, blocks_x + 2 + G, quarter, PAIR), BF16),
        near_in=v((heads_x, blocks_x + 2 + G, quarter, PAIR), BF16),
        run=v((blocks * R + 1, quarter, PAIR), F32),
        sbuf=v((seq, quarter, PAIR), BF16),
        rbuf=v((seq, quarter, PAIR), BF16),
        run2=v((seq + 1, quarter, PAIR), F32),
        edge=v((2, quarter, PAIR), BF16),
        gp=v((pieces2, 8, DH), F32),
        gin2=v((seq, ppr2, 8, DH), F32),
        relay2=v((ppr2, 8, DH), F32),
        gtot=v((pieces2, 8, DH), F32),
        fin=v((blocks, quarter, PAIR), F32),
        sem_l=dma((8,)),
        sem_w=dma((2,)),
        sem_g=dma((2,)),
        sem_b=dma((2,)),
        sem_h=dma((2,)),
        sem_q=dma((heads_x, 2)),
        sem_f=dma((2,)),
        sem_r=dma((blocks_x, 2)),
        sem_e=dma((blocks_x, 2)),
        sem_d=dma((2,)),
        sem_s=dma((2,)),
        sem_ng=dma((2,)),
        sem_nw=dma((2,)),
        sem_n=dma((2,)),
        sem_g2=dma((2,)),
        sem_b2=dma((2,)),
        sem_k=dma((2,)),
        sem_v=dma((2,)),
    )


def kernel(seq, heads_x, names, gb_ref, rb_ref, q_hbm, do_hbm, k_hbm, v_hbm, qg, kg, vg, *scratch):
    m = types.SimpleNamespace(**dict(zip(names, scratch)))
    s = lax.axis_index("seq")
    x = lax.axis_index("head")
    blocks = m.k.shape[0]
    blocks_x = blocks // heads_x
    rows_x = blocks_x * BLOCK
    quarter = BLOCK // heads_x
    per = BLOCK // 16
    entries = blocks * R
    part = pl.ds(pl.multiple_of(x * quarter, quarter), quarter)
    own_rows = pl.ds(pl.multiple_of(x * rows_x, rows_x), rows_x)

    def peer(d):
        return lax.rem(x + d, heads_x)

    def remote(src, dst, sems, to):
        pltpu.make_async_remote_copy(
            src_ref=src, dst_ref=dst, send_sem=sems.at[0], recv_sem=sems.at[1],
            device_id=to, device_id_type=MESH,
        ).start()

    barrier = pltpu.get_barrier_semaphore()

    def greet(j):
        pl.semaphore_signal(
            barrier, inc=1, device_id=(lax.rem(s + j, seq), x), device_id_type=MESH
        )

    loop(seq, greet, 1)
    for d in range(1, heads_x):
        pl.semaphore_signal(barrier, inc=1, device_id=(s, peer(d)), device_id_type=MESH)

    local = [
        pltpu.make_async_copy(k_hbm, m.k, m.sem_l.at[0]),
        pltpu.make_async_copy(v_hbm, m.v, m.sem_l.at[1]),
        pltpu.make_async_copy(q_hbm.at[own_rows], m.q.at[x], m.sem_l.at[2]),
        pltpu.make_async_copy(do_hbm.at[own_rows], m.do.at[x], m.sem_l.at[3]),
    ]
    for copy in local:
        copy.start()

    for r in range(R):
        m.tcol[r * blocks : (r + 1) * blocks] = jnp.broadcast_to(
            rb_ref[:, r : r + 1], (blocks, 128)
        )
    column = m.tcol[...]
    owner = lax.div(column, jnp.full_like(column, blocks))
    within = column - owner * blocks
    at = lax.broadcasted_iota(I32, column.shape, 0)
    lane = lax.broadcasted_iota(I32, column.shape, 1)

    def pick(cond, value):
        return jnp.max(jnp.where(cond, value, 0), axis=0, keepdims=True)

    owner_row = pick(at == lane, owner)
    m.wvec[...] = pick(owner == lane, within)
    m.tvec[0] = owner_row
    m.tvec[1] = pick((owner == owner_row) & (at < lane), at + 1)
    m.tvec[2] = pick(owner == lane, at + 1)
    table = pltpu.make_async_copy(m.tvec, m.tsm, m.sem_l.at[4])
    table.start()
    m.wbuf[s] = m.wvec[...]
    local[0].wait()
    local[1].wait()
    for g in range(G):
        for n, ref in enumerate((m.k, m.v)):
            first = (g * 2 + n) * per
            m.cand[first : first + per] = ref[lax.rem(gb_ref[g], blocks)].reshape(per, 16, DH)
    table.wait()

    pl.semaphore_wait(barrier, seq - 1 + heads_x - 1)

    loop(
        seq,
        lambda j: remote(m.wvec, m.wbuf.at[s], m.sem_w, (lax.rem(s + j, seq), x)),
        1,
    )
    pieces = m.cand.shape[0]
    stride, ppr = relays(seq, pieces)
    count = pieces // ppr
    is_relay = lax.rem(s, stride) == 0
    mine = s // stride

    def send_cand(r):
        @pl.when(r * stride != s)
        def _():
            remote(m.cand.at[pl.ds(r * ppr, ppr)], m.gin.at[s], m.sem_g, (r * stride, x))

    loop(count, send_cand)

    @pl.when(is_relay)
    def _():
        m.gin[s] = m.cand[pl.ds(mine * ppr, ppr)]

    for d in range(1, heads_x):
        rows = pl.ds(pl.multiple_of(peer(d) * rows_x, rows_x), rows_x)
        remote(q_hbm.at[rows], m.q.at[x], m.sem_q.at[d], (s, peer(d)))
        remote(do_hbm.at[rows], m.do.at[x], m.sem_q.at[d], (s, peer(d)))
    after = (lax.rem(s + 1, seq), x)
    before = (lax.rem(s + seq - 1, seq), x)
    for n, ref in enumerate((m.k, m.v)):
        remote(ref.at[blocks - 1], m.halo.at[0, n], m.sem_h, after)
        remote(ref.at[0], m.halo.at[1, n], m.sem_h, before)

    arrived(m.wbuf.at[pl.ds(0, seq - 1)], m.sem_w.at[1])
    to_smem = pltpu.make_async_copy(m.wbuf, m.wsm, m.sem_l.at[5])
    to_smem.start()
    to_smem.wait()

    def serve(e):
        block = m.wsm[e, 0, s]
        m.served[e, :, :DH] = m.k[block, part, :]
        m.served[e, :, DH:] = m.v[block, part, :]

    loop(seq, serve)
    m.fetched[s] = m.served[s]
    loop(
        seq,
        lambda j: remote(
            m.served.at[lax.rem(s + j, seq)], m.fetched.at[s], m.sem_f, (lax.rem(s + j, seq), x)
        ),
        1,
    )

    @pl.when(is_relay)
    def _():
        arrived(m.gin.at[pl.ds(0, seq - 1)], m.sem_g.at[1])
        for i in range(ppr):
            g = (mine * ppr + i) // (2 * per)
            m.relay[i] = m.gin[lax.div(gb_ref[g], blocks), i]
        m.glob[pl.ds(mine * ppr, ppr)] = m.relay[...]
        loop(
            seq,
            lambda j: remote(
                m.relay, m.glob.at[pl.ds(mine * ppr, ppr)], m.sem_b, (lax.rem(s + j, seq), x)
            ),
            1,
        )

    asked = m.wbuf[...].reshape(seq, 128)
    at = lax.broadcasted_iota(I32, asked.shape, 0)
    lane = lax.broadcasted_iota(I32, asked.shape, 1)
    asked = jnp.max(jnp.where(lane == s, asked, 0), axis=1, keepdims=True)
    asked = jnp.broadcast_to(asked, (seq, 128))
    asked_row = jnp.max(jnp.where(at == lane, asked, -1), axis=0, keepdims=True)
    m.rvec[0] = pick((asked == asked_row) & (at < lane), at + 1)
    m.rvec[1] = pick(asked == lane, at + 1)
    table = pltpu.make_async_copy(m.rvec, m.rsm, m.sem_l.at[6])
    table.start()

    arrived(m.halo, m.sem_h.at[1])
    for i in range(blocks_x + 2):
        place = x * blocks_x + (i - 1)
        inner = jnp.clip(place, 0, blocks - 1)
        for n, ref in enumerate((m.k, m.v)):
            value = ref[inner]
            if i == 0:
                value = jnp.where(place < 0, m.halo[0, n], value)
            if i == blocks_x + 1:
                value = jnp.where(place >= blocks, m.halo[1, n], value)
            m.near[n, i] = value
    m.wacc[...] = jnp.zeros_like(m.wacc)

    @pl.when(is_relay)
    def _():
        arrived(m.glob.at[pl.ds(0, (count - 1) * ppr)], m.sem_b.at[1])

    @pl.when(jnp.logical_not(is_relay))
    def _():
        arrived(m.glob, m.sem_b.at[1])

    local[2].wait()
    local[3].wait()

    def near_block(n, b, j):
        if j < 3:
            return m.near[n, b + j]
        first = ((j - 3) * 2 + n) * per
        return m.glob[first : first + per].reshape(BLOCK, DH)

    def rows_of(b):
        return pl.ds(pl.multiple_of(b * BLOCK, BLOCK), BLOCK)

    def stacked(ref, h, b):
        return jnp.concatenate([ref[h, rows_of(b), :DH], ref[h, rows_of(b), DH:]], axis=0)

    def source(d):
        return lax.rem(x + heads_x - d, heads_x)

    def near_scores(d):
        @pl.when(d > 0)
        def _():
            arrived(m.q.at[pl.ds(0, 2)], m.sem_q.at[d, 1])

        def step(b):
            i = b * heads_x + d
            q = stacked(m.q, source(d), b)
            do = stacked(m.do, source(d), b)
            before_ok = (s + x + b) > 0
            after_ok = (seq - s + heads_x - x + blocks_x - b) > 3
            top = jnp.full((8, PAIR), NEG, F32)
            for j in range(NEAR):
                score = dot(near_block(0, b, j), q, NT)
                if j == 0:
                    score = jnp.where(before_ok, score, NEG)
                if j == 2:
                    score = jnp.where(after_ok, score, NEG)
                m.s_buf[j] = score
                top = jnp.maximum(top, fold(score, jnp.max))
            top = jnp.max(top, axis=0, keepdims=True)
            total = jnp.zeros((8, PAIR), F32)
            inner = jnp.zeros((8, PAIR), F32)
            for j in range(NEAR):
                dp = dot(near_block(1, b, j), do, NT)
                e = jnp.exp2((m.s_buf[j] - top) * (FACTOR * LOG2E))
                total = total + fold(e, jnp.sum)
                inner = inner + fold(e * dp, jnp.sum)
                m.e1[i, j] = e
                m.dp1[i, j] = dp
            m.stats[i, 0:1] = top
            m.stats[i, 1:2] = jnp.sum(total, axis=0, keepdims=True)
            m.stats[i, 2:3] = jnp.sum(inner, axis=0, keepdims=True)

        loop(blocks_x, step)

    loop(heads_x, near_scores)

    arrived(m.fetched.at[pl.ds(0, seq - 1)], m.sem_f.at[1])

    def hand_out(b):
        for d in range(1, heads_x):
            for j in range(R):
                m.picked[b, d - 1, j] = m.fetched[m.tsm[0, 0, j * blocks + peer(d) * blocks_x + b]]
        for j in range(R):
            m.rnd[b, j, part, :] = m.fetched[m.tsm[0, 0, j * blocks + x * blocks_x + b]]
        for d in range(1, heads_x):
            remote(m.picked.at[b, d - 1], m.rnd.at[b, :, part, :], m.sem_r.at[b], (s, peer(d)))

    loop(blocks_x, hand_out)

    lane = lax.broadcasted_iota(I32, (BLOCK, PAIR), 1)
    scale_lanes = jnp.where(lane < DH, FACTOR, 1.0)

    def far_block(b):
        arrived(m.rnd.at[b, :, pl.ds(0, (heads_x - 1) * quarter), :], m.sem_r.at[b, 1])
        m.acc[...] = jnp.zeros_like(m.acc)

        def step(d):
            i = b * heads_x + d
            q = stacked(m.q, source(d), b)
            do = stacked(m.do, source(d), b)
            top1, total1, inner1 = m.stats[i, 0:1], m.stats[i, 1:2], m.stats[i, 2:3]
            top = jnp.full((8, PAIR), NEG, F32)
            for j in range(R):
                score = dot(m.rnd[b, j, :, :DH], q, NT)
                m.s_buf[j] = score
                top = jnp.maximum(top, fold(score, jnp.max))
            top = jnp.maximum(jnp.max(top, axis=0, keepdims=True), top1)
            total = jnp.zeros((8, PAIR), F32)
            inner = jnp.zeros((8, PAIR), F32)
            for j in range(R):
                dp = dot(m.rnd[b, j, :, DH:], do, NT)
                e = jnp.exp2((m.s_buf[j] - top) * (FACTOR * LOG2E))
                total = total + fold(e, jnp.sum)
                inner = inner + fold(e * dp, jnp.sum)
                m.s_buf[j] = e
                m.dp_buf[j] = dp
            shrink = jnp.exp2((top1 - top) * (FACTOR * LOG2E))
            total = jnp.sum(total, axis=0, keepdims=True) + total1 * shrink
            inner = jnp.sum(inner, axis=0, keepdims=True) + inner1 * shrink
            scale = 1.0 / total
            delta = inner * scale
            m.stats[i, 3:4] = shrink * scale
            m.stats[i, 4:5] = delta
            for j in range(R):
                a = m.s_buf[j] * scale
                ds = (a * (m.dp_buf[j] - delta)).astype(BF16)
                m.ds_far[i, j * BLOCK : (j + 1) * BLOCK] = ds
                m.acc[j, :, :DH] += dot(ds, q)
                m.acc[j, :, DH:] += dot(a.astype(BF16), do)

        loop(heads_x, step)
        for j in range(R):
            grad = (m.acc[j] * scale_lanes).astype(BF16)
            for to in range(heads_x):
                m.far_out[to, b, j] = grad[to * quarter : (to + 1) * quarter]
        m.far_in[x, b] = m.far_out[x, b]
        for d in range(1, heads_x):
            remote(m.far_out.at[peer(d), b], m.far_in.at[x, b], m.sem_e.at[b], (s, peer(d)))

    loop(blocks_x, far_block)

    m.run[0] = jnp.zeros((quarter, PAIR), F32)
    m.run2[0] = jnp.zeros((quarter, PAIR), F32)
    for b in range(blocks_x):
        arrived(m.far_out.at[pl.ds(0, heads_x - 1), b], m.sem_e.at[b, 1])
    for j in range(R):

        def chain(i, j=j):
            entry = j * blocks + i
            grad = m.far_in[i // blocks_x, lax.rem(i, blocks_x), j].astype(F32)
            m.run[entry + 1] = grad + m.run[m.tsm[1, 0, entry]]

        loop(blocks, chain)

    def fill(e):
        m.sbuf[e] = m.run[m.tsm[2, 0, e]].astype(BF16)

    loop(seq, fill)
    m.rbuf[s] = m.sbuf[s]
    loop(
        seq,
        lambda j: remote(
            m.sbuf.at[lax.rem(s + j, seq)], m.rbuf.at[s], m.sem_s, (lax.rem(s + j, seq), x)
        ),
        1,
    )

    def near_grads(b):
        for j in range(NEAR):
            m.kt[:, j * BLOCK : (j + 1) * BLOCK] = near_block(0, b, j).T
        for j in range(R):
            at = NEAR + j
            m.kt[:, at * BLOCK : (at + 1) * BLOCK] = m.rnd[b, j, :, :DH].T

        def step(d):
            i = b * heads_x + d
            h = source(d)
            q = stacked(m.q, h, b)
            do = stacked(m.do, h, b)
            scale, delta = m.stats[i, 3:4], m.stats[i, 4:5]
            for j in range(NEAR):
                a = m.e1[i, j] * scale
                m.p[j] = a.astype(BF16)
                m.ds[j * BLOCK : (j + 1) * BLOCK] = (a * (m.dp1[i, j] - delta)).astype(BF16)
            for j in range(NEAR):
                at = b + j if j < 3 else blocks_x + 2 + (j - 3)
                m.wacc[at, :, :DH] += dot(m.ds[j * BLOCK : (j + 1) * BLOCK], q)
                m.wacc[at, :, DH:] += dot(m.p[j], do)
            dqt = dot(m.kt[:, : NEAR * BLOCK], m.ds[...])
            dqt = (dqt + dot(m.kt[:, NEAR * BLOCK :], m.ds_far[i])) * FACTOR
            m.dq[h, rows_of(b), :DH] = dqt[:, :BLOCK].T.astype(BF16)
            m.dq[h, rows_of(b), DH:] = dqt[:, BLOCK:].T.astype(BF16)

        loop(heads_x, step)
        out = pl.ds(pl.multiple_of(x * rows_x + b * BLOCK, BLOCK), BLOCK)
        for d in range(1, heads_x):
            remote(m.dq.at[peer(d), rows_of(b)], qg.at[out], m.sem_d, (s, peer(d)))
        pltpu.make_async_copy(m.dq.at[x, rows_of(b)], qg.at[out], m.sem_l.at[7]).start()

    loop(blocks_x, near_grads)
    near_slots = blocks_x + 2
    for j in list(range(near_slots, near_slots + G)) + list(range(near_slots)):
        grad = (m.wacc[j] * scale_lanes).astype(BF16)
        for to in range(heads_x):
            m.near_out[to, j] = grad[to * quarter : (to + 1) * quarter]
    glob_part = pl.ds(near_slots, G)
    near_part = pl.ds(0, near_slots)
    for d in range(1, heads_x):
        remote(
            m.near_out.at[peer(d), glob_part], m.near_in.at[x, glob_part], m.sem_ng, (s, peer(d))
        )
    for d in range(1, heads_x):
        remote(
            m.near_out.at[peer(d), near_part], m.near_in.at[x, near_part], m.sem_nw, (s, peer(d))
        )
    m.near_in[x] = m.near_out[x]

    arrived(m.near_out.at[pl.ds(0, heads_x - 1), glob_part], m.sem_ng.at[1])
    lines = quarter // 8
    for g in range(G):
        value = m.near_in[0, near_slots + g].astype(F32)
        for src in range(1, heads_x):
            value = value + m.near_in[src, near_slots + g].astype(F32)
        for c in range(lines):
            for n in range(2):
                m.gp[(g * lines + c) * 2 + n] = value[
                    c * 8 : (c + 1) * 8, n * DH : (n + 1) * DH
                ]
    pieces2 = m.gp.shape[0]
    stride2, ppr2 = relays(seq, pieces2)
    count2 = pieces2 // ppr2
    is_relay2 = lax.rem(s, stride2) == 0
    mine2 = s // stride2

    @pl.when(is_relay2)
    def _():
        m.gin2[s] = m.gp[pl.ds(mine2 * ppr2, ppr2)]

    def send_global(r):
        @pl.when(r * stride2 != s)
        def _():
            remote(m.gp.at[pl.ds(r * ppr2, ppr2)], m.gin2.at[s], m.sem_g2, (r * stride2, x))

    loop(count2, send_global)
    arrived(m.near_out.at[pl.ds(0, heads_x - 1), near_part], m.sem_nw.at[1])
    remote(m.near_in.at[0, 0], m.edge.at[1], m.sem_n, before)
    remote(m.near_in.at[heads_x - 1, blocks_x + 1], m.edge.at[0], m.sem_n, after)

    @pl.when(is_relay2)
    def _():
        arrived(m.gin2.at[pl.ds(0, seq - 1)], m.sem_g2.at[1])
        m.relay2[...] = jnp.zeros_like(m.relay2)

        def add(e):
            m.relay2[...] += m.gin2[e]

        loop(seq, add)
        m.gtot[pl.ds(mine2 * ppr2, ppr2)] = m.relay2[...]
        loop(
            seq,
            lambda j: remote(
                m.relay2, m.gtot.at[pl.ds(mine2 * ppr2, ppr2)], m.sem_b2, (lax.rem(s + j, seq), x)
            ),
            1,
        )

    arrived(m.edge, m.sem_n.at[1])

    @pl.when(is_relay2)
    def _():
        arrived(m.gtot.at[pl.ds(0, (count2 - 1) * ppr2)], m.sem_b2.at[1])

    @pl.when(jnp.logical_not(is_relay2))
    def _():
        arrived(m.gtot, m.sem_b2.at[1])

    for b in range(blocks):
        src, i = b // blocks_x, b % blocks_x
        total = m.near_in[src, 1 + i].astype(F32)
        if i == 0:
            more = m.edge[0] if src == 0 else m.near_in[src - 1, blocks_x + 1]
            total = total + more.astype(F32)
        if i == blocks_x - 1:
            more = m.edge[1] if src == heads_x - 1 else m.near_in[src + 1, 0]
            total = total + more.astype(F32)
        held = [jnp.where(gb_ref[g] == s * blocks + b, 1.0, 0.0) for g in range(G)]
        for c in range(lines):
            for n in range(2):
                value = total[c * 8 : (c + 1) * 8, n * DH : (n + 1) * DH]
                for g in range(G):
                    value = value + held[g] * m.gtot[(g * lines + c) * 2 + n]
                m.fin[b, c * 8 : (c + 1) * 8, n * DH : (n + 1) * DH] = value

    table.wait()
    arrived(m.rbuf.at[pl.ds(0, seq - 1)], m.sem_s.at[1])

    def gather(e):
        m.run2[e + 1] = m.rbuf[e].astype(F32) + m.run2[m.rsm[0, 0, e]]

    loop(seq, gather)
    for b in range(blocks):
        total = m.fin[b] + m.run2[m.rsm[1, 0, b]]
        kg[b, part, :] = total[:, :DH].astype(BF16)
        vg[b, part, :] = total[:, DH:].astype(BF16)
    for d in range(1, heads_x):
        remote(kg.at[:, part, :], kg.at[:, part, :], m.sem_k, (s, peer(d)))
        remote(vg.at[:, part, :], vg.at[:, part, :], m.sem_v, (s, peer(d)))

    others = pl.ds(0, heads_x - 1)
    arrived(m.wbuf.at[pl.ds(0, seq - 1)], m.sem_w.at[0])
    arrived(m.served.at[pl.ds(0, seq - 1)], m.sem_f.at[0])
    for d in range(1, heads_x):
        arrived(m.q.at[pl.ds(0, 2)], m.sem_q.at[d, 0])
    arrived(m.halo, m.sem_h.at[0])
    for b in range(blocks_x):
        arrived(m.picked.at[b], m.sem_r.at[b, 0])
        arrived(m.far_out.at[others, b], m.sem_e.at[b, 0])
    arrived(m.near_out.at[others, glob_part], m.sem_ng.at[0])
    arrived(m.near_out.at[others, near_part], m.sem_nw.at[0])
    arrived(m.edge, m.sem_n.at[0])
    arrived(m.rbuf.at[pl.ds(0, seq - 1)], m.sem_s.at[0])
    arrived(m.dq.at[others], m.sem_d.at[0])
    arrived(m.dq.at[others], m.sem_d.at[1])
    arrived(m.dq.at[0], m.sem_l.at[7])

    def drain(relay, count, gin, send_sem, relay_sem):
        @pl.when(relay)
        def _():
            arrived(gin.at[pl.ds(0, seq - 1)], relay_sem.at[0])
            if count > 1:
                arrived(gin.at[pl.ds(0, count - 1)], send_sem.at[0])

        @pl.when(jnp.logical_not(relay))
        def _():
            arrived(gin.at[pl.ds(0, count)], send_sem.at[0])

    drain(is_relay, count, m.gin, m.sem_g, m.sem_b)
    drain(is_relay2, count2, m.gin2, m.sem_g2, m.sem_b2)
    rest = pl.ds(0, (heads_x - 1) * quarter)
    for sem, ref in ((m.sem_k, kg), (m.sem_v, vg)):
        arrived(ref.at[:, rest, :], sem.at[0])
        arrived(ref.at[:, rest, :], sem.at[1])


def body(query_vectors, key_vectors, value_vectors, output_grad, random_blocks, global_blocks):
    seq = lax.axis_size("seq")
    heads_x = lax.axis_size("head")
    rows, width = query_vectors.shape
    blocks = rows // BLOCK
    scratch = shapes(seq, heads_x, blocks)
    vmem = pl.BlockSpec(memory_space=pltpu.VMEM)
    anyspec = pl.BlockSpec(memory_space=pl.ANY)
    folded = jax.ShapeDtypeStruct((blocks, BLOCK, DH), BF16)
    query_grad, key_grad, value_grad = pl.pallas_call(
        functools.partial(kernel, seq, heads_x, tuple(scratch)),
        out_shape=(jax.ShapeDtypeStruct((rows, width), BF16), folded, folded),
        in_specs=[pl.BlockSpec(memory_space=pltpu.SMEM), vmem] + [anyspec] * 4,
        out_specs=(anyspec, vmem, vmem),
        scratch_shapes=tuple(scratch.values()),
        compiler_params=pltpu.CompilerParams(
            vmem_limit_bytes=60 * 2**20, collective_id=0, has_side_effects=True
        ),
        name="attention_grad",
    )(
        global_blocks,
        random_blocks,
        query_vectors,
        output_grad,
        key_vectors.reshape(blocks, BLOCK, DH),
        value_vectors.reshape(blocks, BLOCK, DH),
    )
    return query_grad, key_grad.reshape(rows, DH), value_grad.reshape(rows, DH)


def solution(mesh):
    return jax.shard_map(
        body,
        mesh=mesh,
        in_specs=(
            P("seq", "head"),
            P("seq", None),
            P("seq", None),
            P("seq", "head"),
            P("seq", None),
            P(),
        ),
        out_specs=(P("seq", "head"), P("seq", None), P("seq", None)),
        check_vma=False,
    )
```

time: 558 us -> 136 us (0.24)
  waiting for transfers between devices: 392 us -> 0 us
  Pallas kernels: 24.8 us -> 129 us
  blocking collectives: 55.3 us -> 0 us
  starting transfers between devices: 40.1 us -> 0 us
  between operations: 14 us -> 0.66 us
  local copies, waits for them, and re-layouts: 18.9 us -> 5.7 us
  other arithmetic: 9.61 us -> 0 us
    psum x2 -> x0, waiting for transfers between devices: 338 us -> none  [the longest x1 171 us: body(): glb = lax.psum(held, 'seq')]
    pallas_call x1, Pallas kernels: 24.8 us -> 129 us  [body(): pl.pallas_call(functools.partial(kernel, seq, heads_x, tuple(scratch)), o...]
    all_to_all x2 -> x0, blocking collectives: 55.3 us -> none  [a2a(): return lax.all_to_all(value, axis, split_axis=0, concat_axis=0, tiled=True)]
    all_to_all x6 -> x0, waiting for transfers between devices: 46.8 us -> none  [a2a(): return lax.all_to_all(value, axis, split_axis=0, concat_axis=0, tiled=True)]
    all_to_all x6 -> x0, starting transfers between devices: 34.3 us -> none  [a2a(): return lax.all_to_all(value, axis, split_axis=0, concat_axis=0, tiled=True)]
    ppermute x4 -> x0, starting transfers between devices: 5.63 us -> none  [the longest x1 3.49 us: body(): after = lax.ppermute(kv[:1], 'seq', down)]
  transfers between devices with their start and end apart: 13 -> 0, of which waited for: 8 -> 0; matrix products, arithmetic and copies ran while one was open for 3% -> 0% of each run, Pallas kernels for 0% -> 0%
where the time goes in v3:
time: 136 us
  Pallas kernels  129 us (95%)
  local copies, waits for them, and re-layouts  5.7 us (4%)
    pallas_call x1, Pallas kernels, body(): pl.pallas_call(functools.partial(kernel, seq, heads_x, tuple(scratch)), o...  129 us
    unnamed x10, local copies, waits for them, and re-layouts  5.7 us

profile of v3, /device:TPU:1, one launch (start us, length us, event | category | flops | bytes accessed | tf_op | source)
XLA Modules:
  0.0 135.6 jit_solution(6702673479090253268)
XLA Ops:
  0.6 0.0 copy-start.2
  0.6 0.7 copy-done.2
  1.3 0.7 copy.9.rb_ref
  2.0 129.2 %attention_grad.1 = (bf16[2048,256]{1,0:T(8,128)(2,1)}, bf16[16,128,128]{2,1,0:T(8,128)(2,1)}, bf16[16,128,128]{2,1,0:T(8,128)(2,1)}) custom-call(s32[2]{0:T(128)} %gb_ref.1, s32[16,3]{1,0:T(8,128)} %copy.9.rb_ref, bf16[2048,256]{1,0:T(8,128)(2,1)} %q_hbm.1, bf16[2048,256]{1,0:T(8,128)(2,1)} %do_hbm.1, bf16[16,128,128]{2,1,0:T(8,128)(2,1)} %bitcast.6, ...), custom_call_target="tpu_custom_call" | custom-call | tf_op jit(solution)/shard_map/attention_grad/pallas_call | solution.py:636
  131.2 0.0 copy-start.1
  131.2 2.3 %copy.13 = bf16[2048,256]{1,0:T(8,128)(2,1)} copy(bf16[2048,256]{1,0:T(8,128)(2,1)} %get-tuple-element.12) | data formatting | bytes 2097152
  133.5 0.0 copy-done.1
  133.5 0.0 copy-start
  133.5 0.8 copy.14
  134.3 0.4 copy-done
  134.8 0.8 copy.15
Async XLA Ops:
  0.6 0.7 copy-start.2
  131.2 2.3 %copy-start.1 = (bf16[16,128,128]{2,1,0:T(8,128)(2,1)S(1)}, bf16[16,128,128]{2,1,0:T(8,128)(2,1)}, u32[]{:S(2)}) copy-start(bf16[16,128,128]{2,1,0:T(8,128)(2,1)} %get-tuple-element.7) | copy-start | bytes 1572868
  133.5 1.2 copy-start

commit v4 on v3

--- a/solution.py
+++ b/solution.py
@@ -66,7 +66,7 @@
         near=v((2, blocks_x + 2, BLOCK, DH), BF16),
         glob=v((G * 2 * BLOCK // 16, 16, DH), BF16),
         halo=v((2, 2, BLOCK, DH), BF16),
-        rnd=v((blocks_x, R, BLOCK, PAIR), BF16),
+        rnd=v((2, blocks_x, R, BLOCK, DH), BF16),
         tcol=v((blocks * R, 128), I32),
         tvec=v((3, 1, 128), I32),
         tsm=pltpu.SMEM((3, 1, 128), I32),
@@ -75,9 +75,10 @@
         wsm=pltpu.SMEM((seq, 1, 128), I32),
         rvec=v((2, 1, 128), I32),
         rsm=pltpu.SMEM((2, 1, 128), I32),
-        served=v((seq, quarter, PAIR), BF16),
-        fetched=v((seq, quarter, PAIR), BF16),
-        picked=v((blocks_x, heads_x - 1, R, quarter, PAIR), BF16),
+        served=v((2, seq, quarter, DH), BF16),
+        fetched_k=v((seq, quarter, DH), BF16),
+        fetched_v=v((seq, quarter, DH), BF16),
+        picked=v((2, blocks_x, heads_x - 1, R, quarter, DH), BF16),
         cand=v((pieces, 16, DH), BF16),
         gin=v((seq, ppr, 16, DH), BF16),
         relay=v((ppr, 16, DH), BF16),
@@ -86,9 +87,10 @@
         stats=v((chunks, 8, PAIR), F32),
         s_buf=v((NEAR, BLOCK, PAIR), F32),
         dp_buf=v((R, BLOCK, PAIR), F32),
-        ds_far=v((chunks, R * BLOCK, PAIR), BF16),
-        ds=v((NEAR * BLOCK, PAIR), BF16),
-        p=v((NEAR, BLOCK, PAIR), BF16),
+        s_far=v((chunks, R, BLOCK, PAIR), F32),
+        ds_far=v((chunks, (R + G) * BLOCK, PAIR), BF16),
+        ds=v((3 * BLOCK, PAIR), BF16),
+        p=v((3, BLOCK, PAIR), BF16),
         kt=v((DH, (NEAR + R) * BLOCK), BF16),
         acc=v((R, BLOCK, PAIR), F32),
         wacc=v((blocks_x + 2 + G, BLOCK, PAIR), F32),
@@ -98,38 +100,38 @@
         near_out=v((heads_x, blocks_x + 2 + G, quarter, PAIR), BF16),
         near_in=v((heads_x, blocks_x + 2 + G, quarter, PAIR), BF16),
         run=v((blocks * R + 1, quarter, PAIR), F32),
-        sbuf=v((seq, quarter, PAIR), BF16),
-        rbuf=v((seq, quarter, PAIR), BF16),
-        run2=v((seq + 1, quarter, PAIR), F32),
+        sbuf=v((2, seq, quarter, DH), BF16),
+        rbuf=v((2, seq, quarter, DH), BF16),
+        run2=v((2, seq + 1, quarter, DH), F32),
         edge=v((2, quarter, PAIR), BF16),
         gp=v((pieces2, 8, DH), F32),
         gin2=v((seq, ppr2, 8, DH), F32),
         relay2=v((ppr2, 8, DH), F32),
         gtot=v((pieces2, 8, DH), F32),
-        fin=v((blocks, quarter, PAIR), F32),
+        fin=v((2, blocks, quarter, DH), F32),
         sem_l=dma((8,)),
         sem_w=dma((2,)),
         sem_g=dma((2,)),
         sem_b=dma((2,)),
         sem_h=dma((2,)),
         sem_q=dma((heads_x, 2)),
-        sem_f=dma((2,)),
-        sem_r=dma((blocks_x, 2)),
+        sem_f=dma((2, 2)),
+        sem_r=dma((2, blocks_x, 2)),
         sem_e=dma((blocks_x, 2)),
         sem_d=dma((2,)),
-        sem_s=dma((2,)),
+        sem_s=dma((2, 2)),
         sem_ng=dma((2,)),
         sem_nw=dma((2,)),
         sem_n=dma((2,)),
         sem_g2=dma((2,)),
         sem_b2=dma((2,)),
-        sem_k=dma((2,)),
-        sem_v=dma((2,)),
+        sem_o=dma((2, 2)),
     )
 
 
 def kernel(seq, heads_x, names, gb_ref, rb_ref, q_hbm, do_hbm, k_hbm, v_hbm, qg, kg, vg, *scratch):
     m = types.SimpleNamespace(**dict(zip(names, scratch)))
+    fetched = (m.fetched_k, m.fetched_v)
     s = lax.axis_index("seq")
     x = lax.axis_index("head")
     blocks = m.k.shape[0]
@@ -236,22 +238,6 @@
     arrived(m.wbuf.at[pl.ds(0, seq - 1)], m.sem_w.at[1])
     to_smem = pltpu.make_async_copy(m.wbuf, m.wsm, m.sem_l.at[5])
     to_smem.start()
-    to_smem.wait()
-
-    def serve(e):
-        block = m.wsm[e, 0, s]
-        m.served[e, :, :DH] = m.k[block, part, :]
-        m.served[e, :, DH:] = m.v[block, part, :]
-
-    loop(seq, serve)
-    m.fetched[s] = m.served[s]
-    loop(
-        seq,
-        lambda j: remote(
-            m.served.at[lax.rem(s + j, seq)], m.fetched.at[s], m.sem_f, (lax.rem(s + j, seq), x)
-        ),
-        1,
-    )
 
     @pl.when(is_relay)
     def _():
@@ -260,6 +246,31 @@
             g = (mine * ppr + i) // (2 * per)
             m.relay[i] = m.gin[lax.div(gb_ref[g], blocks), i]
         m.glob[pl.ds(mine * ppr, ppr)] = m.relay[...]
+
+    def serve(n, ref):
+        def step(e):
+            m.served[n, e] = ref[m.wsm[e, 0, s], part, :]
+
+        loop(seq, step)
+        fetched[n][s] = m.served[n, s]
+
+    def send_served(n):
+        loop(
+            seq,
+            lambda j: remote(
+                m.served.at[n, lax.rem(s + j, seq)],
+                fetched[n].at[s],
+                m.sem_f.at[n],
+                (lax.rem(s + j, seq), x),
+            ),
+            1,
+        )
+
+    to_smem.wait()
+    serve(0, m.k)
+
+    @pl.when(is_relay)
+    def _():
         loop(
             seq,
             lambda j: remote(
@@ -267,6 +278,10 @@
             ),
             1,
         )
+
+    send_served(0)
+    serve(1, m.v)
+    send_served(1)
 
     asked = m.wbuf[...].reshape(seq, 128)
     at = lax.broadcasted_iota(I32, asked.shape, 0)
@@ -356,24 +371,58 @@
 
     loop(heads_x, near_scores)
 
-    arrived(m.fetched.at[pl.ds(0, seq - 1)], m.sem_f.at[1])
-
-    def hand_out(b):
-        for d in range(1, heads_x):
+    def hand_out(n):
+        arrived(fetched[n].at[pl.ds(0, seq - 1)], m.sem_f.at[n, 1])
+
+        def step(b):
+            for d in range(1, heads_x):
+                for j in range(R):
+                    entry = m.tsm[0, 0, j * blocks + peer(d) * blocks_x + b]
+                    m.picked[n, b, d - 1, j] = fetched[n][entry]
             for j in range(R):
-                m.picked[b, d - 1, j] = m.fetched[m.tsm[0, 0, j * blocks + peer(d) * blocks_x + b]]
-        for j in range(R):
-            m.rnd[b, j, part, :] = m.fetched[m.tsm[0, 0, j * blocks + x * blocks_x + b]]
-        for d in range(1, heads_x):
-            remote(m.picked.at[b, d - 1], m.rnd.at[b, :, part, :], m.sem_r.at[b], (s, peer(d)))
-
-    loop(blocks_x, hand_out)
+                entry = m.tsm[0, 0, j * blocks + x * blocks_x + b]
+                m.rnd[n, b, j, part, :] = fetched[n][entry]
+            for d in range(1, heads_x):
+                remote(
+                    m.picked.at[n, b, d - 1],
+                    m.rnd.at[n, b, :, part, :],
+                    m.sem_r.at[n, b],
+                    (s, peer(d)),
+                )
+
+        loop(blocks_x, step)
+
+    def rnd_ready(n, b):
+        rest = pl.ds(0, (heads_x - 1) * quarter)
+        arrived(m.rnd.at[n, b, :, rest, :], m.sem_r.at[n, b, 1])
+
+    hand_out(0)
+
+    def far_scores(b):
+        rnd_ready(0, b)
+
+        def step(d):
+            i = b * heads_x + d
+            q = stacked(m.q, source(d), b)
+            top = jnp.full((8, PAIR), NEG, F32)
+            for j in range(R):
+                score = dot(m.rnd[0, b, j], q, NT)
+                m.s_far[i, j] = score
+                top = jnp.maximum(top, fold(score, jnp.max))
+            m.stats[i, 5:6] = jnp.max(top, axis=0, keepdims=True)
+
+        loop(heads_x, step)
+
+    loop(blocks_x, far_scores)
+    hand_out(1)
 
     lane = lax.broadcasted_iota(I32, (BLOCK, PAIR), 1)
     scale_lanes = jnp.where(lane < DH, FACTOR, 1.0)
 
+    near_slots = blocks_x + 2
+
     def far_block(b):
-        arrived(m.rnd.at[b, :, pl.ds(0, (heads_x - 1) * quarter), :], m.sem_r.at[b, 1])
+        rnd_ready(1, b)
         m.acc[...] = jnp.zeros_like(m.acc)
 
         def step(d):
@@ -381,17 +430,12 @@
             q = stacked(m.q, source(d), b)
             do = stacked(m.do, source(d), b)
             top1, total1, inner1 = m.stats[i, 0:1], m.stats[i, 1:2], m.stats[i, 2:3]
-            top = jnp.full((8, PAIR), NEG, F32)
-            for j in range(R):
-                score = dot(m.rnd[b, j, :, :DH], q, NT)
-                m.s_buf[j] = score
-                top = jnp.maximum(top, fold(score, jnp.max))
-            top = jnp.maximum(jnp.max(top, axis=0, keepdims=True), top1)
+            top = jnp.maximum(m.stats[i, 5:6], top1)
             total = jnp.zeros((8, PAIR), F32)
             inner = jnp.zeros((8, PAIR), F32)
             for j in range(R):
-                dp = dot(m.rnd[b, j, :, DH:], do, NT)
-                e = jnp.exp2((m.s_buf[j] - top) * (FACTOR * LOG2E))
+                dp = dot(m.rnd[1, b, j], do, NT)
+                e = jnp.exp2((m.s_far[i, j] - top) * (FACTOR * LOG2E))
                 total = total + fold(e, jnp.sum)
                 inner = inner + fold(e * dp, jnp.sum)
                 m.s_buf[j] = e
@@ -401,7 +445,8 @@
             inner = jnp.sum(inner, axis=0, keepdims=True) + inner1 * shrink
             scale = 1.0 / total
             delta = inner * scale
-            m.stats[i, 3:4] = shrink * scale
+            near_scale = shrink * scale
+            m.stats[i, 3:4] = near_scale
             m.stats[i, 4:5] = delta
             for j in range(R):
                 a = m.s_buf[j] * scale
@@ -409,6 +454,12 @@
                 m.ds_far[i, j * BLOCK : (j + 1) * BLOCK] = ds
                 m.acc[j, :, :DH] += dot(ds, q)
                 m.acc[j, :, DH:] += dot(a.astype(BF16), do)
+            for g in range(G):
+                a = m.e1[i, 3 + g] * near_scale
+                ds = (a * (m.dp1[i, 3 + g] - delta)).astype(BF16)
+                m.ds_far[i, (R + g) * BLOCK : (R + g + 1) * BLOCK] = ds
+                m.wacc[near_slots + g, :, :DH] += dot(ds, q)
+                m.wacc[near_slots + g, :, DH:] += dot(a.astype(BF16), do)
 
         loop(heads_x, step)
         for j in range(R):
@@ -421,8 +472,25 @@
 
     loop(blocks_x, far_block)
 
+    glob_part = pl.ds(near_slots, G)
+    near_part = pl.ds(0, near_slots)
+
+    def near_grad_out(j):
+        grad = (m.wacc[j] * scale_lanes).astype(BF16)
+        for to in range(heads_x):
+            m.near_out[to, j] = grad[to * quarter : (to + 1) * quarter]
+        m.near_in[x, j] = m.near_out[x, j]
+
+    for g in range(G):
+        near_grad_out(near_slots + g)
+    for d in range(1, heads_x):
+        remote(
+            m.near_out.at[peer(d), glob_part], m.near_in.at[x, glob_part], m.sem_ng, (s, peer(d))
+        )
+
     m.run[0] = jnp.zeros((quarter, PAIR), F32)
-    m.run2[0] = jnp.zeros((quarter, PAIR), F32)
+    for n in range(2):
+        m.run2[n, 0] = jnp.zeros((quarter, DH), F32)
     for b in range(blocks_x):
         arrived(m.far_out.at[pl.ds(0, heads_x - 1), b], m.sem_e.at[b, 1])
     for j in range(R):
@@ -435,70 +503,25 @@
         loop(blocks, chain)
 
     def fill(e):
-        m.sbuf[e] = m.run[m.tsm[2, 0, e]].astype(BF16)
+        value = m.run[m.tsm[2, 0, e]].astype(BF16)
+        m.sbuf[0, e] = value[:, :DH]
+        m.sbuf[1, e] = value[:, DH:]
 
     loop(seq, fill)
-    m.rbuf[s] = m.sbuf[s]
-    loop(
-        seq,
-        lambda j: remote(
-            m.sbuf.at[lax.rem(s + j, seq)], m.rbuf.at[s], m.sem_s, (lax.rem(s + j, seq), x)
-        ),
-        1,
-    )
-
-    def near_grads(b):
-        for j in range(NEAR):
-            m.kt[:, j * BLOCK : (j + 1) * BLOCK] = near_block(0, b, j).T
-        for j in range(R):
-            at = NEAR + j
-            m.kt[:, at * BLOCK : (at + 1) * BLOCK] = m.rnd[b, j, :, :DH].T
-
-        def step(d):
-            i = b * heads_x + d
-            h = source(d)
-            q = stacked(m.q, h, b)
-            do = stacked(m.do, h, b)
-            scale, delta = m.stats[i, 3:4], m.stats[i, 4:5]
-            for j in range(NEAR):
-                a = m.e1[i, j] * scale
-                m.p[j] = a.astype(BF16)
-                m.ds[j * BLOCK : (j + 1) * BLOCK] = (a * (m.dp1[i, j] - delta)).astype(BF16)
-            for j in range(NEAR):
-                at = b + j if j < 3 else blocks_x + 2 + (j - 3)
-                m.wacc[at, :, :DH] += dot(m.ds[j * BLOCK : (j + 1) * BLOCK], q)
-                m.wacc[at, :, DH:] += dot(m.p[j], do)
-            dqt = dot(m.kt[:, : NEAR * BLOCK], m.ds[...])
-            dqt = (dqt + dot(m.kt[:, NEAR * BLOCK :], m.ds_far[i])) * FACTOR
-            m.dq[h, rows_of(b), :DH] = dqt[:, :BLOCK].T.astype(BF16)
-            m.dq[h, rows_of(b), DH:] = dqt[:, BLOCK:].T.astype(BF16)
-
-        loop(heads_x, step)
-        out = pl.ds(pl.multiple_of(x * rows_x + b * BLOCK, BLOCK), BLOCK)
-        for d in range(1, heads_x):
-            remote(m.dq.at[peer(d), rows_of(b)], qg.at[out], m.sem_d, (s, peer(d)))
-        pltpu.make_async_copy(m.dq.at[x, rows_of(b)], qg.at[out], m.sem_l.at[7]).start()
-
-    loop(blocks_x, near_grads)
-    near_slots = blocks_x + 2
-    for j in list(range(near_slots, near_slots + G)) + list(range(near_slots)):
-        grad = (m.wacc[j] * scale_lanes).astype(BF16)
-        for to in range(heads_x):
-            m.near_out[to, j] = grad[to * quarter : (to + 1) * quarter]
-    glob_part = pl.ds(near_slots, G)
-    near_part = pl.ds(0, near_slots)
-    for d in range(1, heads_x):
-        remote(
-            m.near_out.at[peer(d), glob_part], m.near_in.at[x, glob_part], m.sem_ng, (s, peer(d))
-        )
-    for d in range(1, heads_x):
-        remote(
-            m.near_out.at[peer(d), near_part], m.near_in.at[x, near_part], m.sem_nw, (s, peer(d))
-        )
-    m.near_in[x] = m.near_out[x]
-
+    for n in range(2):
+        m.rbuf[n, s] = m.sbuf[n, s]
+
+    def send_slot(n, j):
+        to = lax.rem(s + j, seq)
+        remote(m.sbuf.at[n, to], m.rbuf.at[n, s], m.sem_s.at[n], (to, x))
+
+    lines = quarter // 8
+    pieces2 = m.gp.shape[0]
+    stride2, ppr2 = relays(seq, pieces2)
+    count2 = pieces2 // ppr2
+    is_relay2 = lax.rem(s, stride2) == 0
+    mine2 = s // stride2
     arrived(m.near_out.at[pl.ds(0, heads_x - 1), glob_part], m.sem_ng.at[1])
-    lines = quarter // 8
     for g in range(G):
         value = m.near_in[0, near_slots + g].astype(F32)
         for src in range(1, heads_x):
@@ -508,15 +531,12 @@
                 m.gp[(g * lines + c) * 2 + n] = value[
                     c * 8 : (c + 1) * 8, n * DH : (n + 1) * DH
                 ]
-    pieces2 = m.gp.shape[0]
-    stride2, ppr2 = relays(seq, pieces2)
-    count2 = pieces2 // ppr2
-    is_relay2 = lax.rem(s, stride2) == 0
-    mine2 = s // stride2
 
     @pl.when(is_relay2)
     def _():
         m.gin2[s] = m.gp[pl.ds(mine2 * ppr2, ppr2)]
+
+    loop(seq // 2, lambda j: send_slot(1, 2 * j + 1))
 
     def send_global(r):
         @pl.when(r * stride2 != s)
@@ -524,9 +544,43 @@
             remote(m.gp.at[pl.ds(r * ppr2, ppr2)], m.gin2.at[s], m.sem_g2, (r * stride2, x))
 
     loop(count2, send_global)
-    arrived(m.near_out.at[pl.ds(0, heads_x - 1), near_part], m.sem_nw.at[1])
-    remote(m.near_in.at[0, 0], m.edge.at[1], m.sem_n, before)
-    remote(m.near_in.at[heads_x - 1, blocks_x + 1], m.edge.at[0], m.sem_n, after)
+    loop(seq // 2, lambda j: send_slot(1, 2 * j), 1)
+
+    def near_grads(b):
+        for j in range(3 + R + G):
+            if j < 3:
+                keys = near_block(0, b, j)
+            elif j < 3 + R:
+                keys = m.rnd[0, b, j - 3]
+            else:
+                keys = near_block(0, b, j - R)
+            m.kt[:, j * BLOCK : (j + 1) * BLOCK] = keys.T
+
+        def step(d):
+            i = b * heads_x + d
+            h = source(d)
+            q = stacked(m.q, h, b)
+            do = stacked(m.do, h, b)
+            scale, delta = m.stats[i, 3:4], m.stats[i, 4:5]
+            for j in range(3):
+                a = m.e1[i, j] * scale
+                m.p[j] = a.astype(BF16)
+                m.ds[j * BLOCK : (j + 1) * BLOCK] = (a * (m.dp1[i, j] - delta)).astype(BF16)
+            for j in range(3):
+                m.wacc[b + j, :, :DH] += dot(m.ds[j * BLOCK : (j + 1) * BLOCK], q)
+                m.wacc[b + j, :, DH:] += dot(m.p[j], do)
+            dqt = dot(m.kt[:, : 3 * BLOCK], m.ds[...])
+            dqt = (dqt + dot(m.kt[:, 3 * BLOCK :], m.ds_far[i])) * FACTOR
+            m.dq[h, rows_of(b), :DH] = dqt[:, :BLOCK].T.astype(BF16)
+            m.dq[h, rows_of(b), DH:] = dqt[:, BLOCK:].T.astype(BF16)
+
+        loop(heads_x, step)
+        out = pl.ds(pl.multiple_of(x * rows_x + b * BLOCK, BLOCK), BLOCK)
+        for d in range(1, heads_x):
+            remote(m.dq.at[peer(d), rows_of(b)], qg.at[out], m.sem_d, (s, peer(d)))
+        pltpu.make_async_copy(m.dq.at[x, rows_of(b)], qg.at[out], m.sem_l.at[7]).start()
+
+    loop(1, near_grads)
 
     @pl.when(is_relay2)
     def _():
@@ -546,6 +600,18 @@
             1,
         )
 
+    loop(seq // 2, lambda j: send_slot(0, 2 * j + 1))
+    loop(blocks_x, near_grads, 1)
+    for j in range(near_slots):
+        near_grad_out(j)
+    for d in range(1, heads_x):
+        remote(
+            m.near_out.at[peer(d), near_part], m.near_in.at[x, near_part], m.sem_nw, (s, peer(d))
+        )
+    arrived(m.near_out.at[pl.ds(0, heads_x - 1), near_part], m.sem_nw.at[1])
+    remote(m.near_in.at[0, 0], m.edge.at[1], m.sem_n, before)
+    remote(m.near_in.at[heads_x - 1, blocks_x + 1], m.edge.at[0], m.sem_n, after)
+    loop(seq // 2, lambda j: send_slot(0, 2 * j), 1)
     arrived(m.edge, m.sem_n.at[1])
 
     @pl.when(is_relay2)
@@ -571,36 +637,40 @@
                 value = total[c * 8 : (c + 1) * 8, n * DH : (n + 1) * DH]
                 for g in range(G):
                     value = value + held[g] * m.gtot[(g * lines + c) * 2 + n]
-                m.fin[b, c * 8 : (c + 1) * 8, n * DH : (n + 1) * DH] = value
+                m.fin[n, b, c * 8 : (c + 1) * 8] = value
 
     table.wait()
-    arrived(m.rbuf.at[pl.ds(0, seq - 1)], m.sem_s.at[1])
-
-    def gather(e):
-        m.run2[e + 1] = m.rbuf[e].astype(F32) + m.run2[m.rsm[0, 0, e]]
-
-    loop(seq, gather)
-    for b in range(blocks):
-        total = m.fin[b] + m.run2[m.rsm[1, 0, b]]
-        kg[b, part, :] = total[:, :DH].astype(BF16)
-        vg[b, part, :] = total[:, DH:].astype(BF16)
-    for d in range(1, heads_x):
-        remote(kg.at[:, part, :], kg.at[:, part, :], m.sem_k, (s, peer(d)))
-        remote(vg.at[:, part, :], vg.at[:, part, :], m.sem_v, (s, peer(d)))
+
+    def finish(n, ref):
+        arrived(m.rbuf.at[n, pl.ds(0, seq - 1)], m.sem_s.at[n, 1])
+
+        def gather(e):
+            m.run2[n, e + 1] = m.rbuf[n, e].astype(F32) + m.run2[n, m.rsm[0, 0, e]]
+
+        loop(seq, gather)
+        for b in range(blocks):
+            ref[b, part, :] = (m.fin[n, b] + m.run2[n, m.rsm[1, 0, b]]).astype(BF16)
+        for d in range(1, heads_x):
+            remote(ref.at[:, part, :], ref.at[:, part, :], m.sem_o.at[n], (s, peer(d)))
+
+    finish(1, vg)
+    finish(0, kg)
 
     others = pl.ds(0, heads_x - 1)
     arrived(m.wbuf.at[pl.ds(0, seq - 1)], m.sem_w.at[0])
-    arrived(m.served.at[pl.ds(0, seq - 1)], m.sem_f.at[0])
+    for n in range(2):
+        arrived(m.served.at[n, pl.ds(0, seq - 1)], m.sem_f.at[n, 0])
+        arrived(m.rbuf.at[n, pl.ds(0, seq - 1)], m.sem_s.at[n, 0])
     for d in range(1, heads_x):
         arrived(m.q.at[pl.ds(0, 2)], m.sem_q.at[d, 0])
     arrived(m.halo, m.sem_h.at[0])
     for b in range(blocks_x):
-        arrived(m.picked.at[b], m.sem_r.at[b, 0])
+        for n in range(2):
+            arrived(m.picked.at[n, b], m.sem_r.at[n, b, 0])
         arrived(m.far_out.at[others, b], m.sem_e.at[b, 0])
     arrived(m.near_out.at[others, glob_part], m.sem_ng.at[0])
     arrived(m.near_out.at[others, near_part], m.sem_nw.at[0])
     arrived(m.edge, m.sem_n.at[0])
-    arrived(m.rbuf.at[pl.ds(0, seq - 1)], m.sem_s.at[0])
     arrived(m.dq.at[others], m.sem_d.at[0])
     arrived(m.dq.at[others], m.sem_d.at[1])
     arrived(m.dq.at[0], m.sem_l.at[7])
@@ -619,9 +689,9 @@
     drain(is_relay, count, m.gin, m.sem_g, m.sem_b)
     drain(is_relay2, count2, m.gin2, m.sem_g2, m.sem_b2)
     rest = pl.ds(0, (heads_x - 1) * quarter)
-    for sem, ref in ((m.sem_k, kg), (m.sem_v, vg)):
-        arrived(ref.at[:, rest, :], sem.at[0])
-        arrived(ref.at[:, rest, :], sem.at[1])
+    for n, ref in enumerate((kg, vg)):
+        arrived(ref.at[:, rest, :], m.sem_o.at[n, 0])
+        arrived(ref.at[:, rest, :], m.sem_o.at[n, 1])
 
 
 def body(query_vectors, key_vectors, value_vectors, output_grad, random_blocks, global_blocks):
@@ -637,7 +707,7 @@
         functools.partial(kernel, seq, heads_x, tuple(scratch)),
         out_shape=(jax.ShapeDtypeStruct((rows, width), BF16), folded, folded),
         in_specs=[pl.BlockSpec(memory_space=pltpu.SMEM), vmem] + [anyspec] * 4,
-        out_specs=(anyspec, vmem, vmem),
+        out_specs=(vmem, vmem, vmem),
         scratch_shapes=tuple(scratch.values()),
         compiler_params=pltpu.CompilerParams(
             vmem_limit_bytes=60 * 2**20, collective_id=0, has_side_effects=True

time: 136 us -> 122 us (0.90); the launches traced: 136 us -> 120 us
  Pallas kernels: 129 us -> 113 us
    pallas_call x1, Pallas kernels: 129 us -> 113 us  [body(): pl.pallas_call(functools.partial(kernel, seq, heads_x, tuple(scratch)), o...]
where the time goes in v4:
time: 122 us; the launch traced here: 120 us
  Pallas kernels  113 us (93%)
  local copies, waits for them, and re-layouts  5.7 us (5%)
    pallas_call x1, Pallas kernels, body(): pl.pallas_call(functools.partial(kernel, seq, heads_x, tuple(scratch)), o...  113 us
    unnamed x10, local copies, waits for them, and re-layouts  5.7 us

profile of v4, /device:TPU:1, one launch (start us, length us, event | category | flops | bytes accessed | tf_op | source)
XLA Modules:
  0.0 119.6 jit_solution(4360932873513836293)
XLA Ops:
  0.6 0.0 copy-start.2
  0.6 0.7 copy-done.2
  1.3 0.7 copy.9.rb_ref
  2.0 113.3 %attention_grad.1 = (bf16[2048,256]{1,0:T(8,128)(2,1)}, bf16[16,128,128]{2,1,0:T(8,128)(2,1)}, bf16[16,128,128]{2,1,0:T(8,128)(2,1)}) custom-call(s32[2]{0:T(128)} %gb_ref.1, s32[16,3]{1,0:T(8,128)} %copy.9.rb_ref, bf16[2048,256]{1,0:T(8,128)(2,1)} %q_hbm.1, bf16[2048,256]{1,0:T(8,128)(2,1)} %do_hbm.1, bf16[16,128,128]{2,1,0:T(8,128)(2,1)} %bitcast.6, ...), custom_call_target="tpu_custom_call" | custom-call | tf_op jit(solution)/shard_map/attention_grad/pallas_call | solution.py:706
  115.3 0.0 copy-start.1
  115.3 2.3 %copy.13 = bf16[2048,256]{1,0:T(8,128)(2,1)} copy(bf16[2048,256]{1,0:T(8,128)(2,1)} %get-tuple-element.12) | data formatting | bytes 2097152
  117.6 0.0 copy-done.1
  117.6 0.0 copy-start
  117.6 0.8 copy.14
  118.4 0.4 copy-done
  118.9 0.8 copy.15
Async XLA Ops:
  0.6 0.7 copy-start.2
  115.3 2.3 %copy-start.1 = (bf16[16,128,128]{2,1,0:T(8,128)(2,1)S(1)}, bf16[16,128,128]{2,1,0:T(8,128)(2,1)}, u32[]{:S(2)}) copy-start(bf16[16,128,128]{2,1,0:T(8,128)(2,1)} %get-tuple-element.7) | copy-start | bytes 1572868
  117.6 1.2 %copy-start = (bf16[16,128,128]{2,1,0:T(8,128)(2,1)S(1)}, bf16[16,128,128]{2,1,0:T(8,128)(2,1)}, u32[]{:S(2)}) copy-start(bf16[16,128,128]{2,1,0:T(8,128)(2,1)} %get-tuple-element.8) | copy-start | bytes 1572868

commit v5 on v4

--- a/solution.py
+++ b/solution.py
@@ -55,7 +55,7 @@
     chunks = heads_x * blocks_x
     pieces = G * 2 * BLOCK // 16
     ppr = relays(seq, pieces)[1]
-    pieces2 = G * (quarter // 8) * 2
+    pieces2 = G * (quarter // 8)
     ppr2 = relays(seq, pieces2)[1]
     v, dma = pltpu.VMEM, pltpu.SemaphoreType.DMA
     return dict(
@@ -92,23 +92,22 @@
         ds=v((3 * BLOCK, PAIR), BF16),
         p=v((3, BLOCK, PAIR), BF16),
         kt=v((DH, (NEAR + R) * BLOCK), BF16),
-        acc=v((R, BLOCK, PAIR), F32),
-        wacc=v((blocks_x + 2 + G, BLOCK, PAIR), F32),
+        acc=v((2, R, BLOCK, DH), F32),
+        wacc=v((2, blocks_x + 2 + G, BLOCK, DH), F32),
         dq=v((heads_x, rows_x, PAIR), BF16),
-        far_out=v((heads_x, blocks_x, R, quarter, PAIR), BF16),
-        far_in=v((heads_x, blocks_x, R, quarter, PAIR), BF16),
-        near_out=v((heads_x, blocks_x + 2 + G, quarter, PAIR), BF16),
-        near_in=v((heads_x, blocks_x + 2 + G, quarter, PAIR), BF16),
-        run=v((blocks * R + 1, quarter, PAIR), F32),
+        far_out=v((2, heads_x, blocks_x, R, quarter, DH), BF16),
+        far_in=v((2, heads_x, blocks_x, R, quarter, DH), BF16),
+        near_out=v((2, heads_x, blocks_x + 2 + G, quarter, DH), BF16),
+        near_in=v((2, heads_x, blocks_x + 2 + G, quarter, DH), BF16),
+        run=v((2, blocks * R + 1, quarter, DH), F32),
         sbuf=v((2, seq, quarter, DH), BF16),
         rbuf=v((2, seq, quarter, DH), BF16),
         run2=v((2, seq + 1, quarter, DH), F32),
-        edge=v((2, quarter, PAIR), BF16),
-        gp=v((pieces2, 8, DH), F32),
-        gin2=v((seq, ppr2, 8, DH), F32),
-        relay2=v((ppr2, 8, DH), F32),
-        gtot=v((pieces2, 8, DH), F32),
-        fin=v((2, blocks, quarter, DH), F32),
+        edge=v((2, 2, quarter, DH), BF16),
+        gp=v((2, pieces2, 8, DH), F32),
+        gin2=v((2, seq, ppr2, 8, DH), F32),
+        relay2=v((2, ppr2, 8, DH), F32),
+        gtot=v((2, pieces2, 8, DH), F32),
         sem_l=dma((8,)),
         sem_w=dma((2,)),
         sem_g=dma((2,)),
@@ -117,14 +116,15 @@
         sem_q=dma((heads_x, 2)),
         sem_f=dma((2, 2)),
         sem_r=dma((2, blocks_x, 2)),
-        sem_e=dma((blocks_x, 2)),
+        sem_e=dma((2, blocks_x, 2)),
         sem_d=dma((2,)),
         sem_s=dma((2, 2)),
+        sem_nv=dma((2,)),
         sem_ng=dma((2,)),
         sem_nw=dma((2,)),
-        sem_n=dma((2,)),
-        sem_g2=dma((2,)),
-        sem_b2=dma((2,)),
+        sem_n=dma((2, 2)),
+        sem_g2=dma((2, 2)),
+        sem_b2=dma((2, 2)),
         sem_o=dma((2, 2)),
     )
 
@@ -397,156 +397,226 @@
         arrived(m.rnd.at[n, b, :, rest, :], m.sem_r.at[n, b, 1])
 
     hand_out(0)
-
-    def far_scores(b):
+    near_slots = blocks_x + 2
+    all_slots = near_slots + G
+    others = pl.ds(0, heads_x - 1)
+
+    def far_send(n, b):
+        for j in range(R):
+            grad = m.acc[n, j] * FACTOR if n == 0 else m.acc[n, j]
+            grad = grad.astype(BF16)
+            for to in range(heads_x):
+                m.far_out[n, to, b, j] = grad[to * quarter : (to + 1) * quarter]
+        m.far_in[n, x, b] = m.far_out[n, x, b]
+        for d in range(1, heads_x):
+            remote(
+                m.far_out.at[n, peer(d), b], m.far_in.at[n, x, b], m.sem_e.at[n, b], (s, peer(d))
+            )
+
+    def far_probs(b):
         rnd_ready(0, b)
-
-        def step(d):
-            i = b * heads_x + d
-            q = stacked(m.q, source(d), b)
-            top = jnp.full((8, PAIR), NEG, F32)
-            for j in range(R):
-                score = dot(m.rnd[0, b, j], q, NT)
-                m.s_far[i, j] = score
-                top = jnp.maximum(top, fold(score, jnp.max))
-            m.stats[i, 5:6] = jnp.max(top, axis=0, keepdims=True)
-
-        loop(heads_x, step)
-
-    loop(blocks_x, far_scores)
-    hand_out(1)
-
-    lane = lax.broadcasted_iota(I32, (BLOCK, PAIR), 1)
-    scale_lanes = jnp.where(lane < DH, FACTOR, 1.0)
-
-    near_slots = blocks_x + 2
-
-    def far_block(b):
-        rnd_ready(1, b)
-        m.acc[...] = jnp.zeros_like(m.acc)
+        m.acc[1] = jnp.zeros_like(m.acc[1])
 
         def step(d):
             i = b * heads_x + d
             q = stacked(m.q, source(d), b)
             do = stacked(m.do, source(d), b)
-            top1, total1, inner1 = m.stats[i, 0:1], m.stats[i, 1:2], m.stats[i, 2:3]
-            top = jnp.maximum(m.stats[i, 5:6], top1)
+            top1, total1 = m.stats[i, 0:1], m.stats[i, 1:2]
+            top = jnp.full((8, PAIR), NEG, F32)
+            for j in range(R):
+                score = dot(m.rnd[0, b, j], q, NT)
+                m.s_buf[j] = score
+                top = jnp.maximum(top, fold(score, jnp.max))
+            top = jnp.maximum(jnp.max(top, axis=0, keepdims=True), top1)
             total = jnp.zeros((8, PAIR), F32)
+            for j in range(R):
+                e = jnp.exp2((m.s_buf[j] - top) * (FACTOR * LOG2E))
+                total = total + fold(e, jnp.sum)
+                m.s_buf[j] = e
+            shrink = jnp.exp2((top1 - top) * (FACTOR * LOG2E))
+            scale = 1.0 / (jnp.sum(total, axis=0, keepdims=True) + total1 * shrink)
+            m.stats[i, 3:4] = shrink * scale
+            for j in range(R):
+                a = m.s_buf[j] * scale
+                m.s_far[i, j] = a
+                m.acc[1, j] += dot(a.astype(BF16), do)
+
+        loop(heads_x, step)
+        far_send(1, b)
+
+    loop(blocks_x, far_probs)
+    hand_out(1)
+
+    for n in range(2):
+        m.run[n, 0] = jnp.zeros((quarter, DH), F32)
+        m.run2[n, 0] = jnp.zeros((quarter, DH), F32)
+
+    def merge(n):
+        for b in range(blocks_x):
+            arrived(m.far_out.at[n, others, b], m.sem_e.at[n, b, 1])
+        for j in range(R):
+
+            def chain(i, j=j):
+                entry = j * blocks + i
+                grad = m.far_in[n, i // blocks_x, lax.rem(i, blocks_x), j].astype(F32)
+                m.run[n, entry + 1] = grad + m.run[n, m.tsm[1, 0, entry]]
+
+            loop(blocks, chain)
+
+        def fill(e):
+            m.sbuf[n, e] = m.run[n, m.tsm[2, 0, e]].astype(BF16)
+
+        loop(seq, fill)
+        m.rbuf[n, s] = m.sbuf[n, s]
+
+    def send_slots(n):
+        def step(j):
+            to = lax.rem(s + j, seq)
+            remote(m.sbuf.at[n, to], m.rbuf.at[n, s], m.sem_s.at[n], (to, x))
+
+        loop(seq, step, 1)
+
+    merge(1)
+    send_slots(1)
+
+    def near_slot(b, j):
+        return b + j if j < 3 else near_slots + (j - 3)
+
+    def near_values(b):
+        def step(d):
+            i = b * heads_x + d
+            do = stacked(m.do, source(d), b)
+            scale = m.stats[i, 3:4]
+            for j in range(NEAR):
+                p = (m.e1[i, j] * scale).astype(BF16)
+                m.wacc[1, near_slot(b, j)] += dot(p, do)
+
+        loop(heads_x, step)
+
+    loop(blocks_x, near_values)
+
+    def near_grad_out(n, j):
+        grad = m.wacc[n, j] * FACTOR if n == 0 else m.wacc[n, j]
+        grad = grad.astype(BF16)
+        for to in range(heads_x):
+            m.near_out[n, to, j] = grad[to * quarter : (to + 1) * quarter]
+        m.near_in[n, x, j] = m.near_out[n, x, j]
+
+    def near_send(n, slots, sem):
+        for j in range(slots[0], slots[1]):
+            near_grad_out(n, j)
+        span = pl.ds(slots[0], slots[1] - slots[0])
+        for d in range(1, heads_x):
+            remote(
+                m.near_out.at[n, peer(d), span], m.near_in.at[n, x, span], sem, (s, peer(d))
+            )
+
+    def near_arrived(n, slots, sem, way):
+        span = pl.ds(slots[0], slots[1] - slots[0])
+        arrived(m.near_out.at[n, others, span], sem.at[way])
+
+    every, window, globs = (0, all_slots), (0, near_slots), (near_slots, all_slots)
+    near_send(1, every, m.sem_nv)
+
+    def far_keys(b):
+        rnd_ready(1, b)
+        m.acc[0] = jnp.zeros_like(m.acc[0])
+
+        def step(d):
+            i = b * heads_x + d
+            q = stacked(m.q, source(d), b)
+            do = stacked(m.do, source(d), b)
+            near_scale = m.stats[i, 3:4]
             inner = jnp.zeros((8, PAIR), F32)
             for j in range(R):
                 dp = dot(m.rnd[1, b, j], do, NT)
-                e = jnp.exp2((m.s_far[i, j] - top) * (FACTOR * LOG2E))
-                total = total + fold(e, jnp.sum)
-                inner = inner + fold(e * dp, jnp.sum)
-                m.s_buf[j] = e
+                inner = inner + fold(m.s_far[i, j] * dp, jnp.sum)
                 m.dp_buf[j] = dp
-            shrink = jnp.exp2((top1 - top) * (FACTOR * LOG2E))
-            total = jnp.sum(total, axis=0, keepdims=True) + total1 * shrink
-            inner = jnp.sum(inner, axis=0, keepdims=True) + inner1 * shrink
-            scale = 1.0 / total
-            delta = inner * scale
-            near_scale = shrink * scale
-            m.stats[i, 3:4] = near_scale
+            delta = jnp.sum(inner, axis=0, keepdims=True) + m.stats[i, 2:3] * near_scale
             m.stats[i, 4:5] = delta
             for j in range(R):
-                a = m.s_buf[j] * scale
-                ds = (a * (m.dp_buf[j] - delta)).astype(BF16)
+                ds = (m.s_far[i, j] * (m.dp_buf[j] - delta)).astype(BF16)
                 m.ds_far[i, j * BLOCK : (j + 1) * BLOCK] = ds
-                m.acc[j, :, :DH] += dot(ds, q)
-                m.acc[j, :, DH:] += dot(a.astype(BF16), do)
+                m.acc[0, j] += dot(ds, q)
             for g in range(G):
                 a = m.e1[i, 3 + g] * near_scale
                 ds = (a * (m.dp1[i, 3 + g] - delta)).astype(BF16)
                 m.ds_far[i, (R + g) * BLOCK : (R + g + 1) * BLOCK] = ds
-                m.wacc[near_slots + g, :, :DH] += dot(ds, q)
-                m.wacc[near_slots + g, :, DH:] += dot(a.astype(BF16), do)
+                m.wacc[0, near_slots + g] += dot(ds, q)
 
         loop(heads_x, step)
-        for j in range(R):
-            grad = (m.acc[j] * scale_lanes).astype(BF16)
-            for to in range(heads_x):
-                m.far_out[to, b, j] = grad[to * quarter : (to + 1) * quarter]
-        m.far_in[x, b] = m.far_out[x, b]
-        for d in range(1, heads_x):
-            remote(m.far_out.at[peer(d), b], m.far_in.at[x, b], m.sem_e.at[b], (s, peer(d)))
-
-    loop(blocks_x, far_block)
-
-    glob_part = pl.ds(near_slots, G)
-    near_part = pl.ds(0, near_slots)
-
-    def near_grad_out(j):
-        grad = (m.wacc[j] * scale_lanes).astype(BF16)
-        for to in range(heads_x):
-            m.near_out[to, j] = grad[to * quarter : (to + 1) * quarter]
-        m.near_in[x, j] = m.near_out[x, j]
-
-    for g in range(G):
-        near_grad_out(near_slots + g)
-    for d in range(1, heads_x):
-        remote(
-            m.near_out.at[peer(d), glob_part], m.near_in.at[x, glob_part], m.sem_ng, (s, peer(d))
-        )
-
-    m.run[0] = jnp.zeros((quarter, PAIR), F32)
-    for n in range(2):
-        m.run2[n, 0] = jnp.zeros((quarter, DH), F32)
-    for b in range(blocks_x):
-        arrived(m.far_out.at[pl.ds(0, heads_x - 1), b], m.sem_e.at[b, 1])
-    for j in range(R):
-
-        def chain(i, j=j):
-            entry = j * blocks + i
-            grad = m.far_in[i // blocks_x, lax.rem(i, blocks_x), j].astype(F32)
-            m.run[entry + 1] = grad + m.run[m.tsm[1, 0, entry]]
-
-        loop(blocks, chain)
-
-    def fill(e):
-        value = m.run[m.tsm[2, 0, e]].astype(BF16)
-        m.sbuf[0, e] = value[:, :DH]
-        m.sbuf[1, e] = value[:, DH:]
-
-    loop(seq, fill)
-    for n in range(2):
-        m.rbuf[n, s] = m.sbuf[n, s]
-
-    def send_slot(n, j):
-        to = lax.rem(s + j, seq)
-        remote(m.sbuf.at[n, to], m.rbuf.at[n, s], m.sem_s.at[n], (to, x))
+        far_send(0, b)
+
+    loop(blocks_x, far_keys)
+    near_send(0, globs, m.sem_ng)
 
     lines = quarter // 8
-    pieces2 = m.gp.shape[0]
+    pieces2 = m.gp.shape[1]
     stride2, ppr2 = relays(seq, pieces2)
     count2 = pieces2 // ppr2
-    is_relay2 = lax.rem(s, stride2) == 0
     mine2 = s // stride2
-    arrived(m.near_out.at[pl.ds(0, heads_x - 1), glob_part], m.sem_ng.at[1])
-    for g in range(G):
-        value = m.near_in[0, near_slots + g].astype(F32)
-        for src in range(1, heads_x):
-            value = value + m.near_in[src, near_slots + g].astype(F32)
-        for c in range(lines):
-            for n in range(2):
-                m.gp[(g * lines + c) * 2 + n] = value[
-                    c * 8 : (c + 1) * 8, n * DH : (n + 1) * DH
-                ]
-
-    @pl.when(is_relay2)
-    def _():
-        m.gin2[s] = m.gp[pl.ds(mine2 * ppr2, ppr2)]
-
-    loop(seq // 2, lambda j: send_slot(1, 2 * j + 1))
-
-    def send_global(r):
-        @pl.when(r * stride2 != s)
+    first_relay = (0, stride2 // 2)
+    is_relay2 = [lax.rem(s, stride2) == first_relay[n] for n in range(2)]
+
+    def global_parts(n):
+        for g in range(G):
+            value = m.near_in[n, 0, near_slots + g].astype(F32)
+            for src in range(1, heads_x):
+                value = value + m.near_in[n, src, near_slots + g].astype(F32)
+            for c in range(lines):
+                m.gp[n, g * lines + c] = value[c * 8 : (c + 1) * 8]
+
+        @pl.when(is_relay2[n])
         def _():
-            remote(m.gp.at[pl.ds(r * ppr2, ppr2)], m.gin2.at[s], m.sem_g2, (r * stride2, x))
-
-    loop(count2, send_global)
-    loop(seq // 2, lambda j: send_slot(1, 2 * j), 1)
-
-    def near_grads(b):
+            m.gin2[n, s] = m.gp[n, pl.ds(mine2 * ppr2, ppr2)]
+
+        def send_global(r):
+            to = r * stride2 + first_relay[n]
+
+            @pl.when(to != s)
+            def _():
+                remote(
+                    m.gp.at[n, pl.ds(r * ppr2, ppr2)], m.gin2.at[n, s], m.sem_g2.at[n], (to, x)
+                )
+
+        loop(count2, send_global)
+
+    def global_totals(n):
+        @pl.when(is_relay2[n])
+        def _():
+            arrived(m.gin2.at[n, pl.ds(0, seq - 1)], m.sem_g2.at[n, 1])
+            m.relay2[n] = jnp.zeros_like(m.relay2[n])
+
+            def add(e):
+                m.relay2[n] += m.gin2[n, e]
+
+            loop(seq, add)
+            m.gtot[n, pl.ds(mine2 * ppr2, ppr2)] = m.relay2[n]
+            loop(
+                seq,
+                lambda j: remote(
+                    m.relay2.at[n],
+                    m.gtot.at[n, pl.ds(mine2 * ppr2, ppr2)],
+                    m.sem_b2.at[n],
+                    (lax.rem(s + j, seq), x),
+                ),
+                1,
+            )
+
+    def send_edges(n):
+        remote(m.near_in.at[n, 0, 0], m.edge.at[n, 1], m.sem_n.at[n], before)
+        remote(m.near_in.at[n, heads_x - 1, blocks_x + 1], m.edge.at[n, 0], m.sem_n.at[n], after)
+
+    near_arrived(1, every, m.sem_nv, 1)
+    global_parts(1)
+    send_edges(1)
+    merge(0)
+    near_arrived(0, globs, m.sem_ng, 1)
+    global_parts(0)
+    global_totals(1)
+    send_slots(0)
+
+    def near_keys(b):
         for j in range(3 + R + G):
             if j < 3:
                 keys = near_block(0, b, j)
@@ -560,15 +630,12 @@
             i = b * heads_x + d
             h = source(d)
             q = stacked(m.q, h, b)
-            do = stacked(m.do, h, b)
             scale, delta = m.stats[i, 3:4], m.stats[i, 4:5]
             for j in range(3):
                 a = m.e1[i, j] * scale
-                m.p[j] = a.astype(BF16)
-                m.ds[j * BLOCK : (j + 1) * BLOCK] = (a * (m.dp1[i, j] - delta)).astype(BF16)
-            for j in range(3):
-                m.wacc[b + j, :, :DH] += dot(m.ds[j * BLOCK : (j + 1) * BLOCK], q)
-                m.wacc[b + j, :, DH:] += dot(m.p[j], do)
+                ds = (a * (m.dp1[i, j] - delta)).astype(BF16)
+                m.ds[j * BLOCK : (j + 1) * BLOCK] = ds
+                m.wacc[0, b + j] += dot(ds, q)
             dqt = dot(m.kt[:, : 3 * BLOCK], m.ds[...])
             dqt = (dqt + dot(m.kt[:, 3 * BLOCK :], m.ds_far[i])) * FACTOR
             m.dq[h, rows_of(b), :DH] = dqt[:, :BLOCK].T.astype(BF16)
@@ -580,68 +647,17 @@
             remote(m.dq.at[peer(d), rows_of(b)], qg.at[out], m.sem_d, (s, peer(d)))
         pltpu.make_async_copy(m.dq.at[x, rows_of(b)], qg.at[out], m.sem_l.at[7]).start()
 
-    loop(1, near_grads)
-
-    @pl.when(is_relay2)
-    def _():
-        arrived(m.gin2.at[pl.ds(0, seq - 1)], m.sem_g2.at[1])
-        m.relay2[...] = jnp.zeros_like(m.relay2)
-
-        def add(e):
-            m.relay2[...] += m.gin2[e]
-
-        loop(seq, add)
-        m.gtot[pl.ds(mine2 * ppr2, ppr2)] = m.relay2[...]
-        loop(
-            seq,
-            lambda j: remote(
-                m.relay2, m.gtot.at[pl.ds(mine2 * ppr2, ppr2)], m.sem_b2, (lax.rem(s + j, seq), x)
-            ),
-            1,
-        )
-
-    loop(seq // 2, lambda j: send_slot(0, 2 * j + 1))
-    loop(blocks_x, near_grads, 1)
-    for j in range(near_slots):
-        near_grad_out(j)
-    for d in range(1, heads_x):
-        remote(
-            m.near_out.at[peer(d), near_part], m.near_in.at[x, near_part], m.sem_nw, (s, peer(d))
-        )
-    arrived(m.near_out.at[pl.ds(0, heads_x - 1), near_part], m.sem_nw.at[1])
-    remote(m.near_in.at[0, 0], m.edge.at[1], m.sem_n, before)
-    remote(m.near_in.at[heads_x - 1, blocks_x + 1], m.edge.at[0], m.sem_n, after)
-    loop(seq // 2, lambda j: send_slot(0, 2 * j), 1)
-    arrived(m.edge, m.sem_n.at[1])
-
-    @pl.when(is_relay2)
-    def _():
-        arrived(m.gtot.at[pl.ds(0, (count2 - 1) * ppr2)], m.sem_b2.at[1])
-
-    @pl.when(jnp.logical_not(is_relay2))
-    def _():
-        arrived(m.gtot, m.sem_b2.at[1])
-
-    for b in range(blocks):
-        src, i = b // blocks_x, b % blocks_x
-        total = m.near_in[src, 1 + i].astype(F32)
-        if i == 0:
-            more = m.edge[0] if src == 0 else m.near_in[src - 1, blocks_x + 1]
-            total = total + more.astype(F32)
-        if i == blocks_x - 1:
-            more = m.edge[1] if src == heads_x - 1 else m.near_in[src + 1, 0]
-            total = total + more.astype(F32)
-        held = [jnp.where(gb_ref[g] == s * blocks + b, 1.0, 0.0) for g in range(G)]
-        for c in range(lines):
-            for n in range(2):
-                value = total[c * 8 : (c + 1) * 8, n * DH : (n + 1) * DH]
-                for g in range(G):
-                    value = value + held[g] * m.gtot[(g * lines + c) * 2 + n]
-                m.fin[n, b, c * 8 : (c + 1) * 8] = value
-
-    table.wait()
-
     def finish(n, ref):
+        arrived(m.edge.at[n], m.sem_n.at[n, 1])
+
+        @pl.when(is_relay2[n])
+        def _():
+            arrived(m.gtot.at[n, pl.ds(0, (count2 - 1) * ppr2)], m.sem_b2.at[n, 1])
+
+        @pl.when(jnp.logical_not(is_relay2[n]))
+        def _():
+            arrived(m.gtot.at[n], m.sem_b2.at[n, 1])
+
         arrived(m.rbuf.at[n, pl.ds(0, seq - 1)], m.sem_s.at[n, 1])
 
         def gather(e):
@@ -649,14 +665,32 @@
 
         loop(seq, gather)
         for b in range(blocks):
-            ref[b, part, :] = (m.fin[n, b] + m.run2[n, m.rsm[1, 0, b]]).astype(BF16)
+            src, i = b // blocks_x, b % blocks_x
+            total = m.near_in[n, src, 1 + i].astype(F32)
+            if i == 0:
+                more = m.edge[n, 0] if src == 0 else m.near_in[n, src - 1, blocks_x + 1]
+                total = total + more.astype(F32)
+            if i == blocks_x - 1:
+                more = m.edge[n, 1] if src == heads_x - 1 else m.near_in[n, src + 1, 0]
+                total = total + more.astype(F32)
+            total = total + m.run2[n, m.rsm[1, 0, b]]
+            for g in range(G):
+                held = jnp.where(gb_ref[g] == s * blocks + b, 1.0, 0.0)
+                total = total + held * m.gtot[n, g * lines : (g + 1) * lines].reshape(quarter, DH)
+            ref[b, part, :] = total.astype(BF16)
         for d in range(1, heads_x):
             remote(ref.at[:, part, :], ref.at[:, part, :], m.sem_o.at[n], (s, peer(d)))
 
+    loop(1, near_keys)
+    global_totals(0)
+    table.wait()
     finish(1, vg)
+    loop(blocks_x, near_keys, 1)
+    near_send(0, window, m.sem_nw)
+    near_arrived(0, window, m.sem_nw, 1)
+    send_edges(0)
     finish(0, kg)
 
-    others = pl.ds(0, heads_x - 1)
     arrived(m.wbuf.at[pl.ds(0, seq - 1)], m.sem_w.at[0])
     for n in range(2):
         arrived(m.served.at[n, pl.ds(0, seq - 1)], m.sem_f.at[n, 0])
@@ -667,10 +701,13 @@
     for b in range(blocks_x):
         for n in range(2):
             arrived(m.picked.at[n, b], m.sem_r.at[n, b, 0])
-        arrived(m.far_out.at[others, b], m.sem_e.at[b, 0])
-    arrived(m.near_out.at[others, glob_part], m.sem_ng.at[0])
-    arrived(m.near_out.at[others, near_part], m.sem_nw.at[0])
-    arrived(m.edge, m.sem_n.at[0])
+        for n in range(2):
+            arrived(m.far_out.at[n, others, b], m.sem_e.at[n, b, 0])
+    near_arrived(1, every, m.sem_nv, 0)
+    near_arrived(0, globs, m.sem_ng, 0)
+    near_arrived(0, window, m.sem_nw, 0)
+    for n in range(2):
+        arrived(m.edge.at[n], m.sem_n.at[n, 0])
     arrived(m.dq.at[others], m.sem_d.at[0])
     arrived(m.dq.at[others], m.sem_d.at[1])
     arrived(m.dq.at[0], m.sem_l.at[7])
@@ -687,7 +724,8 @@
             arrived(gin.at[pl.ds(0, count)], send_sem.at[0])
 
     drain(is_relay, count, m.gin, m.sem_g, m.sem_b)
-    drain(is_relay2, count2, m.gin2, m.sem_g2, m.sem_b2)
+    for n in range(2):
+        drain(is_relay2[n], count2, m.gin2.at[n], m.sem_g2.at[n], m.sem_b2.at[n])
     rest = pl.ds(0, (heads_x - 1) * quarter)
     for n, ref in enumerate((kg, vg)):
         arrived(ref.at[:, rest, :], m.sem_o.at[n, 0])

time: 122 us -> 129 us (1.057); the launches traced: 120 us -> 128 us
  Pallas kernels: 113 us -> 122 us
    pallas_call x1, Pallas kernels: 113 us -> 122 us  [body(): pl.pallas_call(functools.partial(kernel, seq, heads_x, tuple(scratch)), o...]
where the time goes in v5:
time: 129 us; the launch traced here: 128 us
  Pallas kernels  122 us (95%)
  local copies, waits for them, and re-layouts  5.7 us (4%)
    pallas_call x1, Pallas kernels, body(): pl.pallas_call(functools.partial(kernel, seq, heads_x, tuple(scratch)), o...  122 us
    unnamed x10, local copies, waits for them, and re-layouts  5.7 us

profile of v5, /device:TPU:1, one launch (start us, length us, event | category | flops | bytes accessed | tf_op | source)
XLA Modules:
  0.0 128.1 jit_solution(14703105089415417694)
XLA Ops:
  0.6 0.0 copy-start.2
  0.6 0.7 copy-done.2
  1.3 0.7 copy.9.rb_ref
  2.0 121.7 %attention_grad.1 = (bf16[2048,256]{1,0:T(8,128)(2,1)}, bf16[16,128,128]{2,1,0:T(8,128)(2,1)}, bf16[16,128,128]{2,1,0:T(8,128)(2,1)}) custom-call(s32[2]{0:T(128)} %gb_ref.1, s32[16,3]{1,0:T(8,128)} %copy.9.rb_ref, bf16[2048,256]{1,0:T(8,128)(2,1)} %q_hbm.1, bf16[2048,256]{1,0:T(8,128)(2,1)} %do_hbm.1, bf16[16,128,128]{2,1,0:T(8,128)(2,1)} %bitcast.6, ...), custom_call_target="tpu_custom_call" | custom-call | tf_op jit(solution)/shard_map/attention_grad/pallas_call | solution.py:744
  123.7 0.0 copy-start.1
  123.8 2.3 %copy.13 = bf16[2048,256]{1,0:T(8,128)(2,1)} copy(bf16[2048,256]{1,0:T(8,128)(2,1)} %get-tuple-element.12) | data formatting | bytes 2097152
  126.1 0.0 copy-done.1
  126.1 0.0 copy-start
  126.1 0.8 copy.14
  126.9 0.4 copy-done
  127.3 0.8 copy.15
Async XLA Ops:
  0.6 0.7 copy-start.2
  123.7 2.3 %copy-start.1 = (bf16[16,128,128]{2,1,0:T(8,128)(2,1)S(1)}, bf16[16,128,128]{2,1,0:T(8,128)(2,1)}, u32[]{:S(2)}) copy-start(bf16[16,128,128]{2,1,0:T(8,128)(2,1)} %get-tuple-element.7) | copy-start | bytes 1572868
  126.1 1.2 copy-start

commit v6 on v4

--- a/solution.py
+++ b/solution.py
@@ -54,7 +54,7 @@
     rows_x = blocks_x * BLOCK
     chunks = heads_x * blocks_x
     pieces = G * 2 * BLOCK // 16
-    ppr = relays(seq, pieces)[1]
+    ppr = relays(seq, pieces // heads_x)[1]
     pieces2 = G * (quarter // 8) * 2
     ppr2 = relays(seq, pieces2)[1]
     v, dma = pltpu.VMEM, pltpu.SemaphoreType.DMA
@@ -113,6 +113,8 @@
         sem_w=dma((2,)),
         sem_g=dma((2,)),
         sem_b=dma((2,)),
+        sem_x=dma((2,)),
+        sem_ne=dma((2,)),
         sem_h=dma((2,)),
         sem_q=dma((heads_x, 2)),
         sem_f=dma((2, 2)),
@@ -208,7 +210,8 @@
         lambda j: remote(m.wvec, m.wbuf.at[s], m.sem_w, (lax.rem(s + j, seq), x)),
         1,
     )
-    pieces = m.cand.shape[0]
+    pieces = m.cand.shape[0] // heads_x
+    base = x * pieces
     stride, ppr = relays(seq, pieces)
     count = pieces // ppr
     is_relay = lax.rem(s, stride) == 0
@@ -217,13 +220,13 @@
     def send_cand(r):
         @pl.when(r * stride != s)
         def _():
-            remote(m.cand.at[pl.ds(r * ppr, ppr)], m.gin.at[s], m.sem_g, (r * stride, x))
+            remote(m.cand.at[pl.ds(base + r * ppr, ppr)], m.gin.at[s], m.sem_g, (r * stride, x))
 
     loop(count, send_cand)
 
     @pl.when(is_relay)
     def _():
-        m.gin[s] = m.cand[pl.ds(mine * ppr, ppr)]
+        m.gin[s] = m.cand[pl.ds(base + mine * ppr, ppr)]
 
     for d in range(1, heads_x):
         rows = pl.ds(pl.multiple_of(peer(d) * rows_x, rows_x), rows_x)
@@ -243,9 +246,9 @@
     def _():
         arrived(m.gin.at[pl.ds(0, seq - 1)], m.sem_g.at[1])
         for i in range(ppr):
-            g = (mine * ppr + i) // (2 * per)
+            g = (base + mine * ppr + i) // (2 * per)
             m.relay[i] = m.gin[lax.div(gb_ref[g], blocks), i]
-        m.glob[pl.ds(mine * ppr, ppr)] = m.relay[...]
+        m.glob[pl.ds(base + mine * ppr, ppr)] = m.relay[...]
 
     def serve(n, ref):
         def step(e):
@@ -274,7 +277,10 @@
         loop(
             seq,
             lambda j: remote(
-                m.relay, m.glob.at[pl.ds(mine * ppr, ppr)], m.sem_b, (lax.rem(s + j, seq), x)
+                m.relay,
+                m.glob.at[pl.ds(base + mine * ppr, ppr)],
+                m.sem_b,
+                (lax.rem(s + j, seq), x),
             ),
             1,
         )
@@ -293,6 +299,18 @@
     m.rvec[1] = pick(asked == lane, at + 1)
     table = pltpu.make_async_copy(m.rvec, m.rsm, m.sem_l.at[6])
     table.start()
+
+    @pl.when(is_relay)
+    def _():
+        arrived(m.glob.at[pl.ds(0, (count - 1) * ppr)], m.sem_b.at[1])
+
+    @pl.when(jnp.logical_not(is_relay))
+    def _():
+        arrived(m.glob.at[pl.ds(0, pieces)], m.sem_b.at[1])
+
+    plane = pl.ds(base, pieces)
+    for d in range(1, heads_x):
+        remote(m.glob.at[plane], m.glob.at[plane], m.sem_x, (s, peer(d)))
 
     arrived(m.halo, m.sem_h.at[1])
     for i in range(blocks_x + 2):
@@ -307,14 +325,7 @@
             m.near[n, i] = value
     m.wacc[...] = jnp.zeros_like(m.wacc)
 
-    @pl.when(is_relay)
-    def _():
-        arrived(m.glob.at[pl.ds(0, (count - 1) * ppr)], m.sem_b.at[1])
-
-    @pl.when(jnp.logical_not(is_relay))
-    def _():
-        arrived(m.glob, m.sem_b.at[1])
-
+    arrived(m.glob.at[pl.ds(0, (heads_x - 1) * pieces)], m.sem_x.at[1])
     local[2].wait()
     local[3].wait()
 
@@ -473,7 +484,7 @@
     loop(blocks_x, far_block)
 
     glob_part = pl.ds(near_slots, G)
-    near_part = pl.ds(0, near_slots)
+    near_part = pl.ds(1, blocks_x)
 
     def near_grad_out(j):
         grad = (m.wacc[j] * scale_lanes).astype(BF16)
@@ -575,12 +586,25 @@
             m.dq[h, rows_of(b), DH:] = dqt[:, BLOCK:].T.astype(BF16)
 
         loop(heads_x, step)
+
+    def send_dq(b):
         out = pl.ds(pl.multiple_of(x * rows_x + b * BLOCK, BLOCK), BLOCK)
         for d in range(1, heads_x):
             remote(m.dq.at[peer(d), rows_of(b)], qg.at[out], m.sem_d, (s, peer(d)))
         pltpu.make_async_copy(m.dq.at[x, rows_of(b)], qg.at[out], m.sem_l.at[7]).start()
 
-    loop(1, near_grads)
+    last = blocks_x - 1
+
+    def near_all(b):
+        near_grads(b)
+        send_dq(b)
+
+    loop(1, near_all)
+    loop(blocks_x, near_all, max(last, 1))
+    for j in (0, near_slots - 1):
+        near_grad_out(j)
+        for d in range(1, heads_x):
+            remote(m.near_out.at[peer(d), j], m.near_in.at[x, j], m.sem_ne, (s, peer(d)))
 
     @pl.when(is_relay2)
     def _():
@@ -600,18 +624,23 @@
             1,
         )
 
-    loop(seq // 2, lambda j: send_slot(0, 2 * j + 1))
-    loop(blocks_x, near_grads, 1)
-    for j in range(near_slots):
+    if last > 2:
+        loop(last - 1, near_all, 1)
+    arrived(m.near_out.at[pl.ds(0, heads_x - 1), pl.ds(0, 2)], m.sem_ne.at[1])
+    remote(m.near_in.at[0, 0], m.edge.at[1], m.sem_n, before)
+    remote(m.near_in.at[heads_x - 1, blocks_x + 1], m.edge.at[0], m.sem_n, after)
+    loop(seq, lambda j: send_slot(0, j), 1)
+    if last > 1:
+        loop(last, near_grads, last - 1)
+    for j in range(1, near_slots - 1):
         near_grad_out(j)
     for d in range(1, heads_x):
         remote(
             m.near_out.at[peer(d), near_part], m.near_in.at[x, near_part], m.sem_nw, (s, peer(d))
         )
+    if last > 1:
+        loop(last, send_dq, last - 1)
     arrived(m.near_out.at[pl.ds(0, heads_x - 1), near_part], m.sem_nw.at[1])
-    remote(m.near_in.at[0, 0], m.edge.at[1], m.sem_n, before)
-    remote(m.near_in.at[heads_x - 1, blocks_x + 1], m.edge.at[0], m.sem_n, after)
-    loop(seq // 2, lambda j: send_slot(0, 2 * j), 1)
     arrived(m.edge, m.sem_n.at[1])
 
     @pl.when(is_relay2)
@@ -664,12 +693,14 @@
     for d in range(1, heads_x):
         arrived(m.q.at[pl.ds(0, 2)], m.sem_q.at[d, 0])
     arrived(m.halo, m.sem_h.at[0])
+    arrived(m.glob.at[pl.ds(0, (heads_x - 1) * pieces)], m.sem_x.at[0])
     for b in range(blocks_x):
         for n in range(2):
             arrived(m.picked.at[n, b], m.sem_r.at[n, b, 0])
         arrived(m.far_out.at[others, b], m.sem_e.at[b, 0])
     arrived(m.near_out.at[others, glob_part], m.sem_ng.at[0])
     arrived(m.near_out.at[others, near_part], m.sem_nw.at[0])
+    arrived(m.near_out.at[others, pl.ds(0, 2)], m.sem_ne.at[0])
     arrived(m.edge, m.sem_n.at[0])
     arrived(m.dq.at[others], m.sem_d.at[0])
     arrived(m.dq.at[others], m.sem_d.at[1])

time: 122 us -> 119 us (0.975); the launches traced: 120 us -> 119 us
  no operation moved by 1% of the time
where the time goes in v6:
time: 119 us
  Pallas kernels  113 us (95%)
  local copies, waits for them, and re-layouts  5.7 us (5%)
    pallas_call x1, Pallas kernels, body(): pl.pallas_call(functools.partial(kernel, seq, heads_x, tuple(scratch)), o...  113 us
    unnamed x10, local copies, waits for them, and re-layouts  5.7 us

profile of v6, /device:TPU:1, one launch (start us, length us, event | category | flops | bytes accessed | tf_op | source)
XLA Modules:
  0.0 119.1 jit_solution(8825319450951626813)
XLA Ops:
  0.6 0.0 copy-start.2
  0.6 0.7 copy-done.2
  1.3 0.7 copy.9.rb_ref
  2.0 112.7 %attention_grad.1 = (bf16[2048,256]{1,0:T(8,128)(2,1)}, bf16[16,128,128]{2,1,0:T(8,128)(2,1)}, bf16[16,128,128]{2,1,0:T(8,128)(2,1)}) custom-call(s32[2]{0:T(128)} %gb_ref.1, s32[16,3]{1,0:T(8,128)} %copy.9.rb_ref, bf16[2048,256]{1,0:T(8,128)(2,1)} %q_hbm.1, bf16[2048,256]{1,0:T(8,128)(2,1)} %do_hbm.1, bf16[16,128,128]{2,1,0:T(8,128)(2,1)} %bitcast.6, ...), custom_call_target="tpu_custom_call" | custom-call | tf_op jit(solution)/shard_map/attention_grad/pallas_call | solution.py:737
  114.7 0.0 copy-start.1
  114.7 2.3 %copy.13 = bf16[2048,256]{1,0:T(8,128)(2,1)} copy(bf16[2048,256]{1,0:T(8,128)(2,1)} %get-tuple-element.12) | data formatting | bytes 2097152
  117.0 0.0 copy-done.1
  117.0 0.0 copy-start
  117.0 0.8 copy.14
  117.8 0.4 copy-done
  118.3 0.8 copy.15
Async XLA Ops:
  0.6 0.7 copy-start.2
  114.7 2.3 %copy-start.1 = (bf16[16,128,128]{2,1,0:T(8,128)(2,1)S(1)}, bf16[16,128,128]{2,1,0:T(8,128)(2,1)}, u32[]{:S(2)}) copy-start(bf16[16,128,128]{2,1,0:T(8,128)(2,1)} %get-tuple-element.7) | copy-start | bytes 1572868
  117.0 1.2 %copy-start = (bf16[16,128,128]{2,1,0:T(8,128)(2,1)S(1)}, bf16[16,128,128]{2,1,0:T(8,128)(2,1)}, u32[]{:S(2)}) copy-start(bf16[16,128,128]{2,1,0:T(8,128)(2,1)} %get-tuple-element.8) | copy-start | bytes 1572868

commit v7 on v6

--- a/solution.py
+++ b/solution.py
@@ -38,6 +38,11 @@
 
 def relays(seq, pieces):
     return max(1, seq // pieces), max(1, pieces // seq)
+
+
+def unrolled(count, step):
+    for i in range(count):
+        step(i)
 
 
 def loop(count, step, first=0):
@@ -85,12 +90,11 @@
         e1=v((chunks, NEAR, BLOCK, PAIR), F32),
         dp1=v((chunks, NEAR, BLOCK, PAIR), F32),
         stats=v((chunks, 8, PAIR), F32),
-        s_buf=v((NEAR, BLOCK, PAIR), F32),
-        dp_buf=v((R, BLOCK, PAIR), F32),
+        dp_buf=v((heads_x, R, BLOCK, PAIR), F32),
         s_far=v((chunks, R, BLOCK, PAIR), F32),
         ds_far=v((chunks, (R + G) * BLOCK, PAIR), BF16),
-        ds=v((3 * BLOCK, PAIR), BF16),
-        p=v((3, BLOCK, PAIR), BF16),
+        ds=v((heads_x, 3 * BLOCK, PAIR), BF16),
+        p=v((heads_x, 3, BLOCK, PAIR), BF16),
         kt=v((DH, (NEAR + R) * BLOCK), BF16),
         acc=v((R, BLOCK, PAIR), F32),
         wacc=v((blocks_x + 2 + G, BLOCK, PAIR), F32),
@@ -175,9 +179,10 @@
         copy.start()
 
     for r in range(R):
-        m.tcol[r * blocks : (r + 1) * blocks] = jnp.broadcast_to(
-            rb_ref[:, r : r + 1], (blocks, 128)
-        )
+        row = jnp.broadcast_to(rb_ref[r : r + 1, :], (blocks, blocks))
+        mine = lax.broadcasted_iota(I32, row.shape, 0) == lax.broadcasted_iota(I32, row.shape, 1)
+        picked = jnp.max(jnp.where(mine, row, 0), axis=1, keepdims=True)
+        m.tcol[r * blocks : (r + 1) * blocks] = jnp.broadcast_to(picked, (blocks, 128))
     column = m.tcol[...]
     owner = lax.div(column, jnp.full_like(column, blocks))
     within = column - owner * blocks
@@ -362,14 +367,14 @@
                     score = jnp.where(before_ok, score, NEG)
                 if j == 2:
                     score = jnp.where(after_ok, score, NEG)
-                m.s_buf[j] = score
+                m.e1[i, j] = score
                 top = jnp.maximum(top, fold(score, jnp.max))
             top = jnp.max(top, axis=0, keepdims=True)
             total = jnp.zeros((8, PAIR), F32)
             inner = jnp.zeros((8, PAIR), F32)
             for j in range(NEAR):
                 dp = dot(near_block(1, b, j), do, NT)
-                e = jnp.exp2((m.s_buf[j] - top) * (FACTOR * LOG2E))
+                e = jnp.exp2((m.e1[i, j] - top) * (FACTOR * LOG2E))
                 total = total + fold(e, jnp.sum)
                 inner = inner + fold(e * dp, jnp.sum)
                 m.e1[i, j] = e
@@ -378,7 +383,7 @@
             m.stats[i, 1:2] = jnp.sum(total, axis=0, keepdims=True)
             m.stats[i, 2:3] = jnp.sum(inner, axis=0, keepdims=True)
 
-        loop(blocks_x, step)
+        unrolled(blocks_x, step)
 
     loop(heads_x, near_scores)
 
@@ -422,7 +427,7 @@
                 top = jnp.maximum(top, fold(score, jnp.max))
             m.stats[i, 5:6] = jnp.max(top, axis=0, keepdims=True)
 
-        loop(heads_x, step)
+        unrolled(heads_x, step)
 
     loop(blocks_x, far_scores)
     hand_out(1)
@@ -449,8 +454,8 @@
                 e = jnp.exp2((m.s_far[i, j] - top) * (FACTOR * LOG2E))
                 total = total + fold(e, jnp.sum)
                 inner = inner + fold(e * dp, jnp.sum)
-                m.s_buf[j] = e
-                m.dp_buf[j] = dp
+                m.s_far[i, j] = e
+                m.dp_buf[d, j] = dp
             shrink = jnp.exp2((top1 - top) * (FACTOR * LOG2E))
             total = jnp.sum(total, axis=0, keepdims=True) + total1 * shrink
             inner = jnp.sum(inner, axis=0, keepdims=True) + inner1 * shrink
@@ -460,8 +465,8 @@
             m.stats[i, 3:4] = near_scale
             m.stats[i, 4:5] = delta
             for j in range(R):
-                a = m.s_buf[j] * scale
-                ds = (a * (m.dp_buf[j] - delta)).astype(BF16)
+                a = m.s_far[i, j] * scale
+                ds = (a * (m.dp_buf[d, j] - delta)).astype(BF16)
                 m.ds_far[i, j * BLOCK : (j + 1) * BLOCK] = ds
                 m.acc[j, :, :DH] += dot(ds, q)
                 m.acc[j, :, DH:] += dot(a.astype(BF16), do)
@@ -472,7 +477,7 @@
                 m.wacc[near_slots + g, :, :DH] += dot(ds, q)
                 m.wacc[near_slots + g, :, DH:] += dot(a.astype(BF16), do)
 
-        loop(heads_x, step)
+        unrolled(heads_x, step)
         for j in range(R):
             grad = (m.acc[j] * scale_lanes).astype(BF16)
             for to in range(heads_x):
@@ -575,17 +580,17 @@
             scale, delta = m.stats[i, 3:4], m.stats[i, 4:5]
             for j in range(3):
                 a = m.e1[i, j] * scale
-                m.p[j] = a.astype(BF16)
-                m.ds[j * BLOCK : (j + 1) * BLOCK] = (a * (m.dp1[i, j] - delta)).astype(BF16)
+                m.p[d, j] = a.astype(BF16)
+                m.ds[d, j * BLOCK : (j + 1) * BLOCK] = (a * (m.dp1[i, j] - delta)).astype(BF16)
             for j in range(3):
-                m.wacc[b + j, :, :DH] += dot(m.ds[j * BLOCK : (j + 1) * BLOCK], q)
-                m.wacc[b + j, :, DH:] += dot(m.p[j], do)
-            dqt = dot(m.kt[:, : 3 * BLOCK], m.ds[...])
+                m.wacc[b + j, :, :DH] += dot(m.ds[d, j * BLOCK : (j + 1) * BLOCK], q)
+                m.wacc[b + j, :, DH:] += dot(m.p[d, j], do)
+            dqt = dot(m.kt[:, : 3 * BLOCK], m.ds[d])
             dqt = (dqt + dot(m.kt[:, 3 * BLOCK :], m.ds_far[i])) * FACTOR
             m.dq[h, rows_of(b), :DH] = dqt[:, :BLOCK].T.astype(BF16)
             m.dq[h, rows_of(b), DH:] = dqt[:, BLOCK:].T.astype(BF16)
 
-        loop(heads_x, step)
+        unrolled(heads_x, step)
 
     def send_dq(b):
         out = pl.ds(pl.multiple_of(x * rows_x + b * BLOCK, BLOCK), BLOCK)
@@ -746,7 +751,7 @@
         name="attention_grad",
     )(
         global_blocks,
-        random_blocks,
+        random_blocks.T,
         query_vectors,
         output_grad,
         key_vectors.reshape(blocks, BLOCK, DH),

time: 119 us -> 113 us (0.950)
  Pallas kernels: 113 us -> 108 us
  local copies, waits for them, and re-layouts: 5.7 us -> 4.35 us
    pallas_call x1, Pallas kernels: 113 us -> 108 us  [body(): pl.pallas_call(functools.partial(kernel, seq, heads_x, tuple(scratch)), o...]
    unnamed x10 -> x7, local copies, waits for them, and re-layouts: 5.7 us -> 4.35 us
where the time goes in v7:
time: 113 us
  Pallas kernels  108 us (96%)
  local copies, waits for them, and re-layouts  4.35 us (4%)
    pallas_call x1, Pallas kernels, body(): pl.pallas_call(functools.partial(kernel, seq, heads_x, tuple(scratch)), o...  108 us
    unnamed x7, local copies, waits for them, and re-layouts  4.35 us

profile of v7, /device:TPU:1, one launch (start us, length us, event | category | flops | bytes accessed | tf_op | source)
XLA Modules:
  0.0 113.2 jit_solution(9117426417093237772)
XLA Ops:
  0.6 108.2 %attention_grad.1 = (bf16[2048,256]{1,0:T(8,128)(2,1)}, bf16[16,128,128]{2,1,0:T(8,128)(2,1)}, bf16[16,128,128]{2,1,0:T(8,128)(2,1)}) custom-call(s32[2]{0:T(128)} %gb_ref.1, s32[3,16]{1,0:T(4,128)} %bitcast.9, bf16[2048,256]{1,0:T(8,128)(2,1)} %q_hbm.1, bf16[2048,256]{1,0:T(8,128)(2,1)} %do_hbm.1, bf16[16,128,128]{2,1,0:T(8,128)(2,1)} %bitcast.7, ...), custom_call_target="tpu_custom_call" | custom-call | tf_op jit(solution)/shard_map/attention_grad/pallas_call | solution.py:742
  108.9 0.0 copy-start.1
  108.9 2.3 %copy.12 = bf16[2048,256]{1,0:T(8,128)(2,1)} copy(bf16[2048,256]{1,0:T(8,128)(2,1)} %get-tuple-element.12) | data formatting | bytes 2097152
  111.2 0.0 copy-done.1
  111.2 0.0 copy-start
  111.2 0.8 copy.13
  112.0 0.4 copy-done
  112.4 0.8 copy.14
Async XLA Ops:
  108.9 2.3 %copy-start.1 = (bf16[16,128,128]{2,1,0:T(8,128)(2,1)S(1)}, bf16[16,128,128]{2,1,0:T(8,128)(2,1)}, u32[]{:S(2)}) copy-start(bf16[16,128,128]{2,1,0:T(8,128)(2,1)} %get-tuple-element.7) | copy-start | bytes 1572868
  111.2 1.2 %copy-start = (bf16[16,128,128]{2,1,0:T(8,128)(2,1)S(1)}, bf16[16,128,128]{2,1,0:T(8,128)(2,1)}, u32[]{:S(2)}) copy-start(bf16[16,128,128]{2,1,0:T(8,128)(2,1)} %get-tuple-element.8) | copy-start | bytes 1572868

commit v8 on v7

--- a/solution.py
+++ b/solution.py
@@ -730,6 +730,26 @@
         arrived(ref.at[:, rest, :], m.sem_o.at[n, 1])
 
 
+def hand_over_kernel(*refs):
+    half = len(refs) // 2
+    for source, target in zip(refs[:half], refs[half:]):
+        target[...] = source[...]
+
+
+def hand_over(arrays, steps=4):
+    specs = [
+        pl.BlockSpec((a.shape[0] // steps, a.shape[1]), lambda i: (i, 0)) for a in arrays
+    ]
+    return pl.pallas_call(
+        hand_over_kernel,
+        grid=(steps,),
+        out_shape=tuple(jax.ShapeDtypeStruct(a.shape, a.dtype) for a in arrays),
+        in_specs=specs,
+        out_specs=tuple(specs),
+        name="hand_over",
+    )(*arrays)
+
+
 def body(query_vectors, key_vectors, value_vectors, output_grad, random_blocks, global_blocks):
     seq = lax.axis_size("seq")
     heads_x = lax.axis_size("head")
@@ -757,7 +777,7 @@
         key_vectors.reshape(blocks, BLOCK, DH),
         value_vectors.reshape(blocks, BLOCK, DH),
     )
-    return query_grad, key_grad.reshape(rows, DH), value_grad.reshape(rows, DH)
+    return hand_over((query_grad, key_grad.reshape(rows, DH), value_grad.reshape(rows, DH)))
 
 
 def solution(mesh):

time: 113 us -> 113 us (level)
  local copies, waits for them, and re-layouts: 4.35 us -> 0 us
  Pallas kernels: 108 us -> 112 us
    unnamed x7 -> x0, local copies, waits for them, and re-layouts: 4.35 us -> none
    pallas_call x0 -> x1, Pallas kernels: none -> 3.76 us  [hand_over(): pl.pallas_call(hand_over_kernel, grid=(steps,), out_shape=tuple((jax.Shap...]
where the time goes in v8:
time: 113 us
  Pallas kernels  112 us (99%)
    pallas_call x1, Pallas kernels, body(): pl.pallas_call(functools.partial(kernel, seq, heads_x, tuple(scratch)), o...  108 us
    pallas_call x1, Pallas kernels, hand_over(): pl.pallas_call(hand_over_kernel, grid=(steps,), out_shape=tuple((jax.Shap...  3.76 us

profile of v8, /device:TPU:1, one launch (start us, length us, event | category | flops | bytes accessed | tf_op | source)
XLA Modules:
  0.0 112.7 jit_solution(8816063869986921349)
XLA Ops:
  0.6 108.3 %attention_grad.1 = (bf16[2048,256]{1,0:T(8,128)(2,1)}, bf16[16,128,128]{2,1,0:T(8,128)(2,1)}, bf16[16,128,128]{2,1,0:T(8,128)(2,1)}) custom-call(s32[2]{0:T(128)} %gb_ref.1, s32[3,16]{1,0:T(4,128)} %bitcast.9, bf16[2048,256]{1,0:T(8,128)(2,1)} %q_hbm.1, bf16[2048,256]{1,0:T(8,128)(2,1)} %do_hbm.1, bf16[16,128,128]{2,1,0:T(8,128)(2,1)} %bitcast.5, ...), custom_call_target="tpu_custom_call" | custom-call | tf_op jit(solution)/shard_map/attention_grad/pallas_call | solution.py:762
  108.9 3.8 %hand_over.1 = (bf16[2048,256]{1,0:T(8,128)(2,1)}, bf16[2048,128]{1,0:T(8,128)(2,1)}, bf16[2048,128]{1,0:T(8,128)(2,1)}) custom-call(bf16[2048,256]{1,0:T(8,128)(2,1)} %get-tuple-element.6.refs_0_, bf16[2048,128]{1,0:T(8,128)(2,1)} %bitcast.7, bf16[2048,128]{1,0:T(8,128)(2,1)} %bitcast.8), custom_call_target="tpu_custom_call" | custom-call | tf_op jit(solution)/shard_map/hand_over/pallas_call | solution.py:743
